TPU v7x, 512 devices: a whole 4x8x8 slice. The times are simulated.
512 devices in a mesh: tick: 64 (over y, z_hi, core), wire: 8 (over z_lo, x).
Axes of the slice: x: 4, y: 8, z: 8 (z_hi: 4, z_lo: 2; z = z_hi * 2 + z_lo), core: 2. Of those that a mesh axis runs over, the one named last changes fastest.
Arguments:
- signal: float32 [16, 512, 8192], P(None, 'wire', 'tick'), may hold values from -6 to 6
- kernel_front: float32 [16, 3, 9], replicated, may hold values from -1.25 to 1.25
- mixing_front: float32 [16, 16], replicated, may hold values from -1.5 to 1.5
- offset_front: float32 [16], replicated, may hold values from -2 to 2
- kernel_back: float32 [16, 3, 9], replicated, may hold values from -1.25 to 1.25
- mixing_back: float32 [16, 16], replicated, may hold values from -1.5 to 1.5
- offset_back: float32 [16], replicated, may hold values from -2 to 2
- upstream: float32 [16, 512, 8192], P(None, 'wire', 'tick'), may hold values from -13 to 13
Outputs:
- response: float32 [16, 512, 8192], P(None, 'wire', 'tick')
- signal_grad: float32 [16, 512, 8192], P(None, 'wire', 'tick')
- kernel_front_grad: float32 [16, 3, 9], replicated
- mixing_front_grad: float32 [16, 16], replicated
- offset_front_grad: float32 [16], replicated
- kernel_back_grad: float32 [16, 3, 9], replicated
- mixing_back_grad: float32 [16, 16], replicated
- offset_back_grad: float32 [16], replicated
All inputs are finite; a program needn't handle non-finite values.
Results may differ from a plain program's by a relative error of at most 0.0003.
Values sent between devices are 32-bit elements; how exact they have to be, the bound alone decides.
No kernel may reach another device: no remote copies, remote signals or barrier semaphores. Data moves between devices by JAX's collectives and lax.ppermute only.
A program may use at most 64 MiB of HBM per device.

v0:
```python
import math

import jax
import jax.numpy as jnp
from jax import lax
from jax.sharding import PartitionSpec as P

TICK_DILATION = 8


def with_halo(block, sides, width):
    for axis, dim in sides:
        count = lax.axis_size(axis)
        forward = [(i, i + 1) for i in range(count - 1)]
        backward = [(target, source) for source, target in forward]
        low = lax.ppermute(
            lax.slice_in_dim(block, block.shape[dim] - width, None, axis=dim), axis, forward
        )
        high = lax.ppermute(lax.slice_in_dim(block, 0, width, axis=dim), axis, backward)
        block = jnp.concatenate([low, block, high], axis=dim)
    return block


def spread(field, tick_deep, wire_deep):
    longer = with_halo(field, (("tick", 2),), tick_deep)
    return with_halo(longer, (("wire", 1),), wire_deep)


def depthwise(padded_input, kernel_weight, row_count, column_count):
    total_sum = jnp.zeros((padded_input.shape[0], row_count, column_count), jnp.float32)
    for row_index in range(3):
        for column_index in range(9):
            total_sum = (
                total_sum
                + kernel_weight[:, row_index, column_index][:, None, None]
                * padded_input[
                    :,
                    row_index : row_index + row_count,
                    TICK_DILATION * column_index : TICK_DILATION * column_index + column_count,
                ]
            )
    return total_sum


def tap_grads(upward_gradient, padded_input):
    row_count = upward_gradient.shape[1]
    column_count = upward_gradient.shape[2]
    text_lines = []
    for row_index in range(3):
        text_lines.append(
            jnp.stack(
                [
                    jnp.sum(
                        upward_gradient
                        * padded_input[
                            :,
                            row_index : row_index + row_count,
                            TICK_DILATION * column_index : TICK_DILATION * column_index
                            + column_count,
                        ],
                        axis=(1, 2),
                    )
                    for column_index in range(9)
                ],
                axis=1,
            )
        )
    return jnp.stack(text_lines, axis=1)


def mixing(matrix, field, offset):
    return (
        jnp.einsum("oc,cwt->owt", matrix, field, precision=lax.Precision.HIGHEST)
        + offset[:, None, None]
    )


def slope(preact):
    sig = jax.nn.sigmoid(preact)
    return sig * (1.0 + preact * (1.0 - sig))


def per_device(
    signal,
    kernel_front,
    mixing_front,
    offset_front,
    kernel_back,
    mixing_back,
    offset_back,
    upstream,
):
    row_count = signal.shape[1]
    column_count = signal.shape[2]
    kernel_extent = 4 * TICK_DILATION
    padded_in = spread(signal, kernel_extent, 1)
    taps_front = depthwise(padded_in, kernel_front, row_count, column_count)
    pre_front = mixing(mixing_front, taps_front, offset_front)
    padded_act = spread(jax.nn.silu(pre_front), kernel_extent, 1)
    taps_back = depthwise(padded_act, kernel_back, row_count, column_count)
    pre_back = mixing(mixing_back, taps_back, offset_back)
    response = jax.nn.silu(pre_back)
    grad_back = upstream * slope(pre_back)
    gmix_back = jnp.einsum("owt,cwt->oc", grad_back, taps_back, precision=lax.Precision.HIGHEST)
    gbias_back = jnp.sum(grad_back, axis=(1, 2))
    under_back = jnp.einsum("oc,owt->cwt", mixing_back, grad_back, precision=lax.Precision.HIGHEST)
    gkern_back = tap_grads(under_back, padded_act)
    into_front = depthwise(
        spread(under_back, kernel_extent, 1), kernel_back[:, ::-1, ::-1], row_count, column_count
    )
    grad_front = into_front * slope(pre_front)
    gmix_front = jnp.einsum("owt,cwt->oc", grad_front, taps_front, precision=lax.Precision.HIGHEST)
    gbias_front = jnp.sum(grad_front, axis=(1, 2))
    under_front = jnp.einsum(
        "oc,owt->cwt", mixing_front, grad_front, precision=lax.Precision.HIGHEST
    )
    gkern_front = tap_grads(under_front, padded_in)
    signal_grad = depthwise(
        spread(under_front, kernel_extent, 1), kernel_front[:, ::-1, ::-1], row_count, column_count
    )
    totals = lax.psum(
        (gkern_front, gmix_front, gbias_front, gkern_back, gmix_back, gbias_back), ("tick", "wire")
    )
    factor = 1.0 / math.sqrt(
        row_count * lax.axis_size("wire") * column_count * lax.axis_size("tick")
    )
    return (
        response,
        signal_grad,
        totals[0] * factor,
        totals[1] * factor,
        totals[2] * factor,
        totals[3] * factor,
        totals[4] * factor,
        totals[5] * factor,
    )


def solution(mesh):
    in_specs = (P(None, "wire", "tick"), P(), P(), P(), P(), P(), P(), P(None, "wire", "tick"))
    out_specs = (P(None, "wire", "tick"), P(None, "wire", "tick"), P(), P(), P(), P(), P(), P())
    return jax.shard_map(
        per_device, mesh=mesh, in_specs=in_specs, out_specs=out_specs, check_vma=False
    )
```

profile of v0, /device:TPU:30, one launch (start us, length us, event | category | flops | bytes accessed | tf_op | source)
XLA Modules:
  0.0 259.0 jit_solution(9432671093252713411)
XLA Ops:
  0.6 1.4 constant_dynamic-update-slice_fusion.1
  2.2 1.9 collective-permute-start
  4.1 10.3 %collective-permute-start.1 = (f32[16,64,32]{2,0,1:T(8,128)S(1)}, f32[16,64,32]{2,0,1:T(8,128)S(1)}, u32[]{:S(2)}, u32[]{:S(2)}) collective-permute-start(f32[16,64,32]{2,0,1:T(8,128)S(1)} %get-tuple-element.132), channel_id=1, source_target_pairs={{8,0},{16,8},{24,16},{32,24},{40,32},{48,40},{56,48},{64,56},{72,6... | collective-permute-start | bytes 393224 | tf_op jit(solution)/shard_map/ppermute | solution.py:19
  14.5 9.6 %collective-permute-done = f32[16,64,32]{2,0,1:T(8,128)S(1)} collective-permute-done((f32[16,64,32]{2,0,1:T(8,128)S(1)}, f32[16,64,32]{2,0,1:T(8,128)S(1)}, u32[]{:S(2)}, u32[]{:S(2)}) %collective-permute-start) | collective-permute-done | bytes 131104 | tf_op jit(solution)/shard_map/ppermute | solution.py:16
  24.0 1.3 collective-permute-done.1
  25.4 2.9 %collective-permute-start.2 = (f32[16,1,192]{2,0,1:T(8,128)S(1)}, f32[16,1,192]{2,0,1:T(8,128)S(1)}, u32[]{:S(2)}, u32[]{:S(2)}) collective-permute-start(f32[16,1,192]{2,0,1:T(8,128)S(1)} %get-tuple-element.120), channel_id=1, source_target_pairs={{0,1},{1,2},{2,3},{3,4},{4,5},{5,6},{6,7},{8,9},{9,10},{10,11},{11... | collective-permute-start | bytes 36872 | tf_op jit(solution)/shard_map/ppermute | solution.py:16
  28.3 2.9 %collective-permute-start.3 = (f32[16,1,192]{2,0,1:T(8,128)S(1)}, f32[16,1,192]{2,0,1:T(8,128)S(1)}, u32[]{:S(2)}, u32[]{:S(2)}) collective-permute-start(f32[16,1,192]{2,0,1:T(8,128)S(1)} %get-tuple-element.121), channel_id=1, source_target_pairs={{1,0},{2,1},{3,2},{4,3},{5,4},{6,5},{7,6},{9,8},{10,9},{11,10},{12... | collective-permute-start | bytes 36872 | tf_op jit(solution)/shard_map/ppermute | solution.py:19
  31.3 4.7 %collective-permute-done.3 = f32[16,1,192]{2,0,1:T(8,128)S(1)} collective-permute-done((f32[16,1,192]{2,0,1:T(8,128)S(1)}, f32[16,1,192]{2,0,1:T(8,128)S(1)}, u32[]{:S(2)}, u32[]{:S(2)}) %collective-permute-start.3) | collective-permute-done | bytes 12320 | tf_op jit(solution)/shard_map/ppermute | solution.py:19
  36.1 0.9 maximum_maximum_fusion
  37.0 3.9 %multiply_add_fusion.1 = f32[16,64,128]{2,0,1:T(8,128)S(1)} fusion(f32[16,64,128]{2,0,1:T(8,128)S(1)} %get-tuple-element.130, f32[16,65,192]{2,0,1:T(8,128)S(1)} %get-tuple-element.119, f32[16,64,160]{2,0,1:T(8,128)S(1)} %constant_dynamic-update-slice_fusion, f32[16,65,192]{2,0,1:T(8,128)S(1)} %get-tuple-element.118, f32[16]{0:T(128)S(1)} %get-tuple-element.185, ...), kind=kLoop, calls=%fused_computation.251 | loop fusion | flops 7471104 | bytes 12715712 | tf_op jit(solution)/shard_map/add | solution.py:34
  41.0 1.4 fusion.93
  42.6 2.4 collective-permute-start.4
  45.1 6.1 %collective-permute-start.5 = (f32[16,64,32]{2,0,1:T(8,128)S(1)}, f32[16,64,32]{2,0,1:T(8,128)S(1)}, u32[]{:S(2)}, u32[]{:S(2)}) collective-permute-start(f32[16,64,32]{2,0,1:T(8,128)S(1)} %get-tuple-element.128), channel_id=1, source_target_pairs={{8,0},{16,8},{24,16},{32,24},{40,32},{48,40},{56,48},{64,56},{72,6... | collective-permute-start | bytes 393224 | tf_op jit(solution)/shard_map/ppermute | solution.py:19
  51.2 7.9 %collective-permute-done.4 = f32[16,64,32]{2,0,1:T(8,128)S(1)} collective-permute-done((f32[16,64,32]{2,0,1:T(8,128)S(1)}, f32[16,64,32]{2,0,1:T(8,128)S(1)}, u32[]{:S(2)}, u32[]{:S(2)}) %collective-permute-start.4) | collective-permute-done | bytes 131104 | tf_op jit(solution)/shard_map/ppermute | solution.py:16
  59.1 1.6 collective-permute-done.5
  60.7 2.7 %collective-permute-start.6 = (f32[16,1,192]{2,0,1:T(8,128)S(1)}, f32[16,1,192]{2,0,1:T(8,128)S(1)}, u32[]{:S(2)}, u32[]{:S(2)}) collective-permute-start(f32[16,1,192]{2,0,1:T(8,128)S(1)} %get-tuple-element.116), channel_id=1, source_target_pairs={{0,1},{1,2},{2,3},{3,4},{4,5},{5,6},{6,7},{8,9},{9,10},{10,11},{11... | collective-permute-start | bytes 36872 | tf_op jit(solution)/shard_map/ppermute | solution.py:16
  63.5 3.1 %collective-permute-start.7 = (f32[16,1,192]{2,0,1:T(8,128)S(1)}, f32[16,1,192]{2,0,1:T(8,128)S(1)}, u32[]{:S(2)}, u32[]{:S(2)}) collective-permute-start(f32[16,1,192]{2,0,1:T(8,128)S(1)} %get-tuple-element.117), channel_id=1, source_target_pairs={{1,0},{2,1},{3,2},{4,3},{5,4},{6,5},{7,6},{9,8},{10,9},{11,10},{12... | collective-permute-start | bytes 36872 | tf_op jit(solution)/shard_map/ppermute | solution.py:19
  66.6 4.6 %collective-permute-done.7 = f32[16,1,192]{2,0,1:T(8,128)S(1)} collective-permute-done((f32[16,1,192]{2,0,1:T(8,128)S(1)}, f32[16,1,192]{2,0,1:T(8,128)S(1)}, u32[]{:S(2)}, u32[]{:S(2)}) %collective-permute-start.7) | collective-permute-done | bytes 12320 | tf_op jit(solution)/shard_map/ppermute | solution.py:19
  71.2 0.9 maximum_maximum_fusion.1
  72.1 4.5 %multiply_add_fusion = f32[16,64,128]{2,0,1:T(8,128)S(1)} fusion(f32[16,64,128]{2,0,1:T(8,128)S(1)} %get-tuple-element.187, f32[16,65,192]{2,0,1:T(8,128)S(1)} %get-tuple-element.115, f32[16,65,192]{2,0,1:T(8,128)S(1)} %get-tuple-element.114, f32[16]{0:T(128)S(1)} %get-tuple-element.158, f32[16]{0:T(128)S(1)} %get-tuple-element.159, ...), kind=kLoop, calls=%fused_computation.248 | loop fusion | flops 7995392 | bytes 10749632 | tf_op jit(solution)/shard_map/add | solution.py:34
  76.7 1.8 fusion.98
  78.5 3.0 %multiply_reduce_fusion.18 = (f32[16]{0:T(128)S(1)}, f32[16]{0:T(128)S(1)}, f32[16]{0:T(128)S(1)}, f32[16]{0:T(128)S(1)}, f32[16]{0:T(128)S(1)}, /*index=5*/f32[...) fusion(f32[16,65,192]{2,0,1:T(8,128)S(1)} %get-tuple-element.11, ...), kind=kOutput, calls=%fused_computation.210 | convolution fusion | flops 29884128 | bytes 10487936 | tf_op jit(solution)/shard_map/oc,owt->cwt/dot_general | solution.py:106
  81.5 1.1 fusion.102
  82.7 4.1 %collective-permute-start.8 = (f32[16,64,32]{2,0,1:T(8,128)}, f32[16,64,32]{2,0,1:T(8,128)}, u32[]{:S(2)}, u32[]{:S(2)}) collective-permute-start(f32[16,64,32]{2,0,1:T(8,128)} %get-tuple-element.124), channel_id=1, source_target_pairs={{0,8},{8,16},{16,24},{24,32},{32,40},{40,48},{48,56},{56,64},{64,7... | collective-permute-start | bytes 393224 | tf_op jit(solution)/shard_map/ppermute | solution.py:16
  86.8 4.7 %collective-permute-start.9 = (f32[16,64,32]{2,0,1:T(8,128)}, f32[16,64,32]{2,0,1:T(8,128)}, u32[]{:S(2)}, u32[]{:S(2)}) collective-permute-start(f32[16,64,32]{2,0,1:T(8,128)} %get-tuple-element.125), channel_id=1, source_target_pairs={{8,0},{16,8},{24,16},{32,24},{40,32},{48,40},{56,48},{64,56},{72,6... | collective-permute-start | bytes 393224 | tf_op jit(solution)/shard_map/ppermute | solution.py:19
  91.5 4.9 %multiply_reduce_fusion.9 = (f32[16]{0:T(128)S(1)}, f32[16]{0:T(128)S(1)}, f32[16]{0:T(128)S(1)}, f32[16]{0:T(128)S(1)}, f32[16]{0:T(128)S(1)}, /*index=5*/f32[1...) fusion(f32[16,64,128]{2,0,1:T(8,128)} %copy-done.3, f32[16,64,32]{2,0,1:T(8,128)} %copy-done.8, ...), kind=kLoop, calls=%fused_computation.201 | loop fusion | flops 3932016 | bytes 1835584 | tf_op jit(solution)/shard_map/reduce_sum | solution.py:53
  96.5 2.0 convolution_bitcast_fusion.2
  98.5 1.1 collective-permute-done.9
  99.6 0.8 pad_maximum_fusion.18
  100.4 4.2 %collective-permute-start.10 = (f32[16,1,192]{2,0,1:T(8,128)S(1)}, f32[16,1,192]{2,0,1:T(8,128)S(1)}, u32[]{:S(2)}, u32[]{:S(2)}) collective-permute-start(f32[16,1,192]{2,0,1:T(8,128)S(1)} %get-tuple-element.112), channel_id=1, source_target_pairs={{0,1},{1,2},{2,3},{3,4},{4,5},{5,6},{6,7},{8,9},{9,10},{10,11},{11... | collective-permute-start | bytes 36872 | tf_op jit(solution)/shard_map/ppermute | solution.py:16
  104.6 1.9 collective-permute-start.11
  106.5 1.0 copy.26
  107.5 4.8 %collective-permute-done.11 = f32[16,1,192]{2,0,1:T(8,128)S(1)} collective-permute-done((f32[16,1,192]{2,0,1:T(8,128)S(1)}, f32[16,1,192]{2,0,1:T(8,128)S(1)}, u32[]{:S(2)}, u32[]{:S(2)}) %collective-permute-start.11) | collective-permute-done | bytes 12320 | tf_op jit(solution)/shard_map/ppermute | solution.py:19
  112.3 2.4 maximum_maximum_fusion.2
  114.8 6.4 %fusion.99 = (f32[16]{0:T(128)S(1)}, f32[16,64,128]{2,0,1:T(8,128)S(1)}) fusion(f32[16,64,128]{2,0,1:T(8,128)S(1)} %copy-done.12, f32[16,65,192]{2,0,1:T(8,128)S(1)} %get-tuple-element.111, f32[16]{0:T(128)S(1)} %get-tuple-element.133, f32[16]{0:T(128)S(1)} %get-tuple-element.152, f32[16]{0:T(128)S(1)} %get-tuple-element.157, f32[16]{0:T(128)S(1)} %get-tuple-element.156, ...), kind=kLoop, calls=%fused_computation.333 | loop fusion | flops 9175024 | bytes 11273984 | tf_op jit(solution)/shard_map/reduce_sum | solution.py:113
  122.0 3.0 %multiply_reduce_fusion.45 = (f32[16]{0:T(128)S(1)}, f32[16]{0:T(128)S(1)}, f32[16]{0:T(128)S(1)}, f32[16]{0:T(128)S(1)}, f32[16]{0:T(128)S(1)}, /*index=5*/f32[...) fusion(f32[16,65,192]{2,0,1:T(8,128)S(1)} %get-tuple-element.11, ...), kind=kOutput, calls=%fused_computation.237 | convolution fusion | flops 29884128 | bytes 10487936 | tf_op jit(solution)/shard_map/oc,owt->cwt/dot_general | solution.py:114
  125.1 1.1 fusion.101
  126.2 3.7 %collective-permute-start.12 = (f32[16,64,32]{2,0,1:T(8,128)}, f32[16,64,32]{2,0,1:T(8,128)S(1)}, u32[]{:S(2)}, u32[]{:S(2)}) collective-permute-start(f32[16,64,32]{2,0,1:T(8,128)} %get-tuple-element.122), channel_id=1, source_target_pairs={{0,8},{8,16},{16,24},{24,32},{32,40},{40,48},{48,56},{56,64},{64,7... | collective-permute-start | bytes 393224 | tf_op jit(solution)/shard_map/ppermute | solution.py:16
  129.9 4.8 %collective-permute-start.13 = (f32[16,64,32]{2,0,1:T(8,128)}, f32[16,64,32]{2,0,1:T(8,128)}, u32[]{:S(2)}, u32[]{:S(2)}) collective-permute-start(f32[16,64,32]{2,0,1:T(8,128)} %get-tuple-element.123), channel_id=1, source_target_pairs={{8,0},{16,8},{24,16},{32,24},{40,32},{48,40},{56,48},{64,56},{72,6... | collective-permute-start | bytes 393224 | tf_op jit(solution)/shard_map/ppermute | solution.py:19
  134.8 2.9 %multiply_reduce_fusion.36 = (f32[16]{0:T(128)S(1)}, f32[16]{0:T(128)S(1)}, f32[16]{0:T(128)S(1)}, f32[16]{0:T(128)S(1)}, f32[16]{0:T(128)S(1)}, /*index=5*/f32[...) fusion(f32[16,64,128]{2,0,1:T(8,128)S(1)} %get-tuple-element.189, f32[16,64,160]{2,0,1:T(8,128)S(1)} %copy-done.2, ...), kind=kLoop, calls=%fused_computation.228 | loop fusion | flops 2883440 | bytes 3801664 | tf_op jit(solution)/shard_map/reduce_sum | solution.py:53
  137.8 98.3 %all-reduce = (f32[16,3,9]{0,2,1:T(8,128)S(1)}, f32[16,16]{1,0:T(8,128)S(1)}, f32[16]{0:T(128)S(1)}, f32[16,3,9]{0,2,1:T(8,128)S(1)}, f32[16,16]{1,0:T(8,128)S(1)}, /*index=5*/f32[16]{0:T(128)S(1)}) all-reduce(f32[16,3,9]{0,2,1:T(8,128)S(1)} %pad_maximum_fusion.11, ...), channel_id=1, replica_groups=mesh['tick'=64,'wire'=8] {'tick','wire'}, use_global_device_ids=true, to_apply=%region_27.28 | all-reduce | flops 1408 | bytes 11264 | tf_op jit(solution)/shard_map/psum | solution.py:121
  236.7 0.8 pad_maximum_fusion.15
  237.5 5.0 %collective-permute-start.14 = (f32[16,1,192]{2,0,1:T(8,128)S(1)}, f32[16,1,192]{2,0,1:T(8,128)S(1)}, u32[]{:S(2)}, u32[]{:S(2)}) collective-permute-start(f32[16,1,192]{2,0,1:T(8,128)S(1)} %get-tuple-element.108), channel_id=1, source_target_pairs={{0,1},{1,2},{2,3},{3,4},{4,5},{5,6},{6,7},{8,9},{9,10},{10,11},{11... | collective-permute-start | bytes 36872 | tf_op jit(solution)/shard_map/ppermute | solution.py:16
  242.4 2.1 collective-permute-start.15
  246.3 3.8 %collective-permute-done.15 = f32[16,1,192]{2,0,1:T(8,128)S(1)} collective-permute-done((f32[16,1,192]{2,0,1:T(8,128)S(1)}, f32[16,1,192]{2,0,1:T(8,128)S(1)}, u32[]{:S(2)}, u32[]{:S(2)}) %collective-permute-start.15) | collective-permute-done | bytes 12320 | tf_op jit(solution)/shard_map/ppermute | solution.py:19
  250.2 2.1 maximum_maximum_fusion.3
  252.3 5.7 %fusion.14 = f32[16,64,128]{2,0,1:T(8,128)S(1)} fusion(f32[16,64,128]{2,0,1:T(8,128)S(1)} %get-tuple-element.189, f32[16,64,32]{2,0,1:T(8,128)} %collective-permute-done.13, f32[16,64,32]{2,0,1:T(8,128)S(1)} %collective-permute-done.12, f32[16,65,192]{2,0,1:T(8,128)S(1)} %get-tuple-element.107, f32[16,65,192]{2,0,1:T(8,128)S(1)} %get-tuple-element.106, ...), kind=kLoop, calls=%fused_computation.70 | loop fusion | flops 7995392 | bytes 10749632 | tf_op jit(solution)/shard_map/add | solution.py:34
  258.0 1.0 copy.27
  (72 shorter events, 4.2 us)
Async XLA Ops:
  0.6 76.0 %copy-start = (f32[16,16]{1,0:T(8,128)S(1)}, f32[16,16]{1,0:T(8,128)}, u32[]{:S(2)}) copy-start(f32[16,16]{1,0:T(8,128)} %param.13) | copy-start | bytes 3076
  2.0 12.4 %copy-start.15 = (f32[16,3,9]{0,1,2:T(4,128)S(1)}, f32[16,3,9]{0,1,2:T(4,128)}, u32[]{:S(2)}) copy-start(f32[16,3,9]{0,1,2:T(4,128)} %param.9) | copy-start | bytes 5188
  2.2 21.8 %collective-permute-start = (f32[16,64,32]{2,0,1:T(8,128)S(1)}, f32[16,64,32]{2,0,1:T(8,128)S(1)}, u32[]{:S(2)}, u32[]{:S(2)}) collective-permute-start(f32[16,64,32]{2,0,1:T(8,128)S(1)} %get-tuple-element.131), channel_id=1, source_target_pairs={{0,8},{8,16},{16,24},{24,32},{32,40},{40,48},{48,56},{56,64},{64,7... | collective-permute-start | bytes 393224 | tf_op jit(solution)/shard_map/ppermute | solution.py:16
  4.1 21.2 %collective-permute-start.1 = (f32[16,64,32]{2,0,1:T(8,128)S(1)}, f32[16,64,32]{2,0,1:T(8,128)S(1)}, u32[]{:S(2)}, u32[]{:S(2)}) collective-permute-start(f32[16,64,32]{2,0,1:T(8,128)S(1)} %get-tuple-element.132), channel_id=1, source_target_pairs={{8,0},{16,8},{24,16},{32,24},{40,32},{48,40},{56,48},{64,56},{72,6... | collective-permute-start | bytes 393224 | tf_op jit(solution)/shard_map/ppermute | solution.py:19
  24.0 12.9 %copy-start.5 = (f32[16,64,32]{2,0,1:T(8,128)}, f32[16,64,32]{2,0,1:T(8,128)S(1)}, u32[]{:S(2)}) copy-start(f32[16,64,32]{2,0,1:T(8,128)S(1)} %collective-permute-done) | copy-start | bytes 393220
  25.4 5.9 %collective-permute-start.2 = (f32[16,1,192]{2,0,1:T(8,128)S(1)}, f32[16,1,192]{2,0,1:T(8,128)S(1)}, u32[]{:S(2)}, u32[]{:S(2)}) collective-permute-start(f32[16,1,192]{2,0,1:T(8,128)S(1)} %get-tuple-element.120), channel_id=1, source_target_pairs={{0,1},{1,2},{2,3},{3,4},{4,5},{5,6},{6,7},{8,9},{9,10},{10,11},{11... | collective-permute-start | bytes 36872 | tf_op jit(solution)/shard_map/ppermute | solution.py:16
  28.3 7.7 %collective-permute-start.3 = (f32[16,1,192]{2,0,1:T(8,128)S(1)}, f32[16,1,192]{2,0,1:T(8,128)S(1)}, u32[]{:S(2)}, u32[]{:S(2)}) collective-permute-start(f32[16,1,192]{2,0,1:T(8,128)S(1)} %get-tuple-element.121), channel_id=1, source_target_pairs={{1,0},{2,1},{3,2},{4,3},{5,4},{6,5},{7,6},{9,8},{10,9},{11,10},{12... | collective-permute-start | bytes 36872 | tf_op jit(solution)/shard_map/ppermute | solution.py:19
  31.3 5.7 %copy-start.1 = (f32[16,64,160]{2,0,1:T(8,128)}, f32[16,64,160]{2,0,1:T(8,128)S(1)}, u32[]{:S(2)}) copy-start(f32[16,64,160]{2,0,1:T(8,128)S(1)} %constant_dynamic-update-slice_fusion) | copy-start | bytes 1966084
  37.0 4.0 %copy-start.18 = (f32[16,16]{1,0:T(8,128)S(1)}, f32[16,16]{1,0:T(8,128)}, u32[]{:S(2)}) copy-start(f32[16,16]{1,0:T(8,128)} %param.10) | copy-start | bytes 3076
  37.0 4.0 %copy-start.19 = (f32[16]{0:T(128)S(1)}, f32[16]{0:T(128)}, u32[]{:S(2)}) copy-start(f32[16]{0:T(128)} %param.11) | copy-start | bytes 196
  41.0 1.4 copy-start.9
  42.4 8.8 %copy-start.16 = (f32[16,3,9]{0,1,2:T(4,128)S(1)}, f32[16,3,9]{0,1,2:T(4,128)}, u32[]{:S(2)}) copy-start(f32[16,3,9]{0,1,2:T(4,128)} %param.12) | copy-start | bytes 5188
  42.6 16.5 %collective-permute-start.4 = (f32[16,64,32]{2,0,1:T(8,128)S(1)}, f32[16,64,32]{2,0,1:T(8,128)S(1)}, u32[]{:S(2)}, u32[]{:S(2)}) collective-permute-start(f32[16,64,32]{2,0,1:T(8,128)S(1)} %get-tuple-element.127), channel_id=1, source_target_pairs={{0,8},{8,16},{16,24},{24,32},{32,40},{40,48},{48,56},{56,64},{64,7... | collective-permute-start | bytes 393224 | tf_op jit(solution)/shard_map/ppermute | solution.py:16
  45.1 15.6 %collective-permute-start.5 = (f32[16,64,32]{2,0,1:T(8,128)S(1)}, f32[16,64,32]{2,0,1:T(8,128)S(1)}, u32[]{:S(2)}, u32[]{:S(2)}) collective-permute-start(f32[16,64,32]{2,0,1:T(8,128)S(1)} %get-tuple-element.128), channel_id=1, source_target_pairs={{8,0},{16,8},{24,16},{32,24},{40,32},{48,40},{56,48},{64,56},{72,6... | collective-permute-start | bytes 393224 | tf_op jit(solution)/shard_map/ppermute | solution.py:19
  59.1 13.0 %copy-start.7 = (f32[16,64,32]{2,0,1:T(8,128)}, f32[16,64,32]{2,0,1:T(8,128)S(1)}, u32[]{:S(2)}) copy-start(f32[16,64,32]{2,0,1:T(8,128)S(1)} %collective-permute-done.4) | copy-start | bytes 393220
  60.7 11.4 %copy-start.8 = (f32[16,64,32]{2,0,1:T(8,128)}, f32[16,64,32]{2,0,1:T(8,128)S(1)}, u32[]{:S(2)}) copy-start(f32[16,64,32]{2,0,1:T(8,128)S(1)} %collective-permute-done.5) | copy-start | bytes 393220
  60.7 5.9 %collective-permute-start.6 = (f32[16,1,192]{2,0,1:T(8,128)S(1)}, f32[16,1,192]{2,0,1:T(8,128)S(1)}, u32[]{:S(2)}, u32[]{:S(2)}) collective-permute-start(f32[16,1,192]{2,0,1:T(8,128)S(1)} %get-tuple-element.116), channel_id=1, source_target_pairs={{0,1},{1,2},{2,3},{3,4},{4,5},{5,6},{6,7},{8,9},{9,10},{10,11},{11... | collective-permute-start | bytes 36872 | tf_op jit(solution)/shard_map/ppermute | solution.py:16
  63.5 7.7 %collective-permute-start.7 = (f32[16,1,192]{2,0,1:T(8,128)S(1)}, f32[16,1,192]{2,0,1:T(8,128)S(1)}, u32[]{:S(2)}, u32[]{:S(2)}) collective-permute-start(f32[16,1,192]{2,0,1:T(8,128)S(1)} %get-tuple-element.117), channel_id=1, source_target_pairs={{1,0},{2,1},{3,2},{4,3},{5,4},{6,5},{7,6},{9,8},{10,9},{11,10},{12... | collective-permute-start | bytes 36872 | tf_op jit(solution)/shard_map/ppermute | solution.py:19
  72.1 4.5 %copy-start.17 = (f32[16,64,128]{2,1,0:T(8,128)S(1)}, f32[16,64,128]{2,1,0:T(8,128)}, u32[]{:S(2)}) copy-start(f32[16,64,128]{2,1,0:T(8,128)} %param.15) | copy-start | bytes 1572868
  72.1 4.5 %copy-start.20 = (f32[16]{0:T(128)S(1)}, f32[16]{0:T(128)}, u32[]{:S(2)}) copy-start(f32[16]{0:T(128)} %param.14) | copy-start | bytes 196
  76.7 1.8 copy-start.11
  78.5 3.0 %copy-start.14 = (f32[16,64,128]{2,0,1:T(8,128)}, f32[16,64,128]{2,0,1:T(8,128)S(1)}, u32[]{:S(2)}) copy-start(f32[16,64,128]{2,0,1:T(8,128)S(1)} %get-tuple-element.103) | copy-start | bytes 1572868
  81.5 9.9 %copy-start.3 = (f32[16,64,128]{2,0,1:T(8,128)}, f32[16,64,128]{2,0,1:T(8,128)S(1)}, u32[]{:S(2)}) copy-start(f32[16,64,128]{2,0,1:T(8,128)S(1)} %get-tuple-element.190) | copy-start | bytes 1572868
  82.7 15.8 %collective-permute-start.8 = (f32[16,64,32]{2,0,1:T(8,128)}, f32[16,64,32]{2,0,1:T(8,128)}, u32[]{:S(2)}, u32[]{:S(2)}) collective-permute-start(f32[16,64,32]{2,0,1:T(8,128)} %get-tuple-element.124), channel_id=1, source_target_pairs={{0,8},{8,16},{16,24},{24,32},{32,40},{40,48},{48,56},{56,64},{64,7... | collective-permute-start | bytes 393224 | tf_op jit(solution)/shard_map/ppermute | solution.py:16
  86.8 12.8 %collective-permute-start.9 = (f32[16,64,32]{2,0,1:T(8,128)}, f32[16,64,32]{2,0,1:T(8,128)}, u32[]{:S(2)}, u32[]{:S(2)}) collective-permute-start(f32[16,64,32]{2,0,1:T(8,128)} %get-tuple-element.125), channel_id=1, source_target_pairs={{8,0},{16,8},{24,16},{32,24},{40,32},{48,40},{56,48},{64,56},{72,6... | collective-permute-start | bytes 393224 | tf_op jit(solution)/shard_map/ppermute | solution.py:19
  96.4 3.2 %copy-start.4 = (f32[16,64,128]{2,0,1:T(8,128)S(1)}, f32[16,64,128]{2,0,1:T(8,128)}, u32[]{:S(2)}) copy-start(f32[16,64,128]{2,0,1:T(8,128)} %copy-done.3) | copy-start | bytes 1572868
  98.5 8.0 %copy-start.13 = (f32[16,64,128]{2,0,1:T(8,128)S(1)}, f32[16,64,128]{2,0,1:T(8,128)}, u32[]{:S(2)}) copy-start(f32[16,64,128]{2,0,1:T(8,128)} %get-tuple-element.126) | copy-start | bytes 1572868
  100.4 7.1 %collective-permute-start.10 = (f32[16,1,192]{2,0,1:T(8,128)S(1)}, f32[16,1,192]{2,0,1:T(8,128)S(1)}, u32[]{:S(2)}, u32[]{:S(2)}) collective-permute-start(f32[16,1,192]{2,0,1:T(8,128)S(1)} %get-tuple-element.112), channel_id=1, source_target_pairs={{0,1},{1,2},{2,3},{3,4},{4,5},{5,6},{6,7},{8,9},{9,10},{10,11},{11... | collective-permute-start | bytes 36872 | tf_op jit(solution)/shard_map/ppermute | solution.py:16
  104.6 7.7 %collective-permute-start.11 = (f32[16,1,192]{2,0,1:T(8,128)S(1)}, f32[16,1,192]{2,0,1:T(8,128)S(1)}, u32[]{:S(2)}, u32[]{:S(2)}) collective-permute-start(f32[16,1,192]{2,0,1:T(8,128)S(1)} %get-tuple-element.113), channel_id=1, source_target_pairs={{1,0},{2,1},{3,2},{4,3},{5,4},{6,5},{7,6},{9,8},{10,9},{11,10},{12... | collective-permute-start | bytes 36872 | tf_op jit(solution)/shard_map/ppermute | solution.py:19
  107.5 7.3 %copy-start.12 = (f32[16,64,128]{2,0,1:T(8,128)S(1)}, f32[16,64,128]{2,0,1:T(8,128)}, u32[]{:S(2)}) copy-start(f32[16,64,128]{2,0,1:T(8,128)} %get-tuple-element.188) | copy-start | bytes 1572868
  114.8 6.4 %copy-start.10 = (f32[16,64,128]{2,0,1:T(8,128)S(1)}, f32[16,64,128]{2,0,1:T(8,128)}, u32[]{:S(2)}) copy-start(f32[16,64,128]{2,0,1:T(8,128)} %copy-done.9) | copy-start | bytes 1572868
  125.0 9.7 %copy-start.2 = (f32[16,64,160]{2,0,1:T(8,128)S(1)}, f32[16,64,160]{2,0,1:T(8,128)}, u32[]{:S(2)}) copy-start(f32[16,64,160]{2,0,1:T(8,128)} %copy-done.1) | copy-start | bytes 1966084
  125.0 9.7 %copy-start.6 = (f32[16,64,32]{2,0,1:T(8,128)S(1)}, f32[16,64,32]{2,0,1:T(8,128)}, u32[]{:S(2)}) copy-start(f32[16,64,32]{2,0,1:T(8,128)} %copy-done.5) | copy-start | bytes 393220
  126.2 110.5 %collective-permute-start.12 = (f32[16,64,32]{2,0,1:T(8,128)}, f32[16,64,32]{2,0,1:T(8,128)S(1)}, u32[]{:S(2)}, u32[]{:S(2)}) collective-permute-start(f32[16,64,32]{2,0,1:T(8,128)} %get-tuple-element.122), channel_id=1, source_target_pairs={{0,8},{8,16},{16,24},{24,32},{32,40},{40,48},{48,56},{56,64},{64,7... | collective-permute-start | bytes 393224 | tf_op jit(solution)/shard_map/ppermute | solution.py:16
  129.9 106.8 %collective-permute-start.13 = (f32[16,64,32]{2,0,1:T(8,128)}, f32[16,64,32]{2,0,1:T(8,128)}, u32[]{:S(2)}, u32[]{:S(2)}) collective-permute-start(f32[16,64,32]{2,0,1:T(8,128)} %get-tuple-element.123), channel_id=1, source_target_pairs={{8,0},{16,8},{24,16},{32,24},{40,32},{48,40},{56,48},{64,56},{72,6... | collective-permute-start | bytes 393224 | tf_op jit(solution)/shard_map/ppermute | solution.py:19
  237.5 8.9 %collective-permute-start.14 = (f32[16,1,192]{2,0,1:T(8,128)S(1)}, f32[16,1,192]{2,0,1:T(8,128)S(1)}, u32[]{:S(2)}, u32[]{:S(2)}) collective-permute-start(f32[16,1,192]{2,0,1:T(8,128)S(1)} %get-tuple-element.108), channel_id=1, source_target_pairs={{0,1},{1,2},{2,3},{3,4},{4,5},{5,6},{6,7},{8,9},{9,10},{10,11},{11... | collective-permute-start | bytes 36872 | tf_op jit(solution)/shard_map/ppermute | solution.py:16
  242.4 7.7 %collective-permute-start.15 = (f32[16,1,192]{2,0,1:T(8,128)S(1)}, f32[16,1,192]{2,0,1:T(8,128)S(1)}, u32[]{:S(2)}, u32[]{:S(2)}) collective-permute-start(f32[16,1,192]{2,0,1:T(8,128)S(1)} %get-tuple-element.109), channel_id=1, source_target_pairs={{1,0},{2,1},{3,2},{4,3},{5,4},{6,5},{7,6},{9,8},{10,9},{11,10},{12... | collective-permute-start | bytes 36872 | tf_op jit(solution)/shard_map/ppermute | solution.py:19
where the time goes:
time: 260 us; the launch traced here: 259 us
  blocking collectives  98.3 us (38%)
  starting transfers between devices  62.9 us (24%)
  waiting for transfers between devices  39.3 us (15%)
  other arithmetic  37.6 us (14%)
  matrix products  12.1 us (5%)
  local copies, waits for them, and re-layouts  7.58 us (3%)
    psum x1, blocking collectives, per_device(): lax.psum((gkern_front, gmix_front, gbias_front, gkern_back, gmix_back, gb...  98.3 us
    ppermute x8, starting transfers between devices, with_halo(): lax.ppermute(lax.slice_in_dim(block, 0, width, axis=dim), axis, backward)  36 us
    ppermute x8, starting transfers between devices, with_halo(): lax.ppermute(lax.slice_in_dim(block, block.shape[dim] - width, None, axis...  26.9 us
    ppermute x8, waiting for transfers between devices, with_halo(): lax.ppermute(lax.slice_in_dim(block, 0, width, axis=dim), axis, backward)  21.9 us
    ppermute x8, waiting for transfers between devices, with_halo(): lax.ppermute(lax.slice_in_dim(block, block.shape[dim] - width, None, axis...  17.5 us
    add x3, other arithmetic, depthwise(): total_sum + kernel_weight[:, row_index, column_index][:, None, None] * pa...  14.2 us
    reduce_sum x2, other arithmetic, tap_grads(): jnp.sum(upward_gradient * padded_input[:, row_index:row_index + row_count...  7.79 us
    reduce_sum x1, other arithmetic, per_device(): gbias_front = jnp.sum(grad_front, axis=(1, 2))  6.43 us
  transfers between devices with their start and end apart: 16, of which 9 were waited for; matrix products, arithmetic and copies ran while one was open for 5% of the time, Pallas kernels for 0%

commit v1 on v0

--- a/solution.py
+++ b/solution.py
@@ -3,9 +3,12 @@
 import jax
 import jax.numpy as jnp
 from jax import lax
-from jax.sharding import PartitionSpec as P
+from jax.sharding import Mesh, PartitionSpec as P
 
 TICK_DILATION = 8
+TICK = ("y", "z_hi", "core")
+WIRE = ("z_lo", "x")
+REDUCTION_ORDER = ("core", "x", ("z_hi", "z_lo"), "y")
 
 
 def with_halo(block, sides, width):
@@ -22,8 +25,8 @@
 
 
 def spread(field, tick_deep, wire_deep):
-    longer = with_halo(field, (("tick", 2),), tick_deep)
-    return with_halo(longer, (("wire", 1),), wire_deep)
+    longer = with_halo(field, ((TICK, 2),), tick_deep)
+    return with_halo(longer, ((WIRE, 1),), wire_deep)
 
 
 def depthwise(padded_input, kernel_weight, row_count, column_count):
@@ -118,11 +121,15 @@
     signal_grad = depthwise(
         spread(under_front, kernel_extent, 1), kernel_front[:, ::-1, ::-1], row_count, column_count
     )
-    totals = lax.psum(
-        (gkern_front, gmix_front, gbias_front, gkern_back, gmix_back, gbias_back), ("tick", "wire")
-    )
+    totals = (gkern_front, gmix_front, gbias_front, gkern_back, gmix_back, gbias_back)
+    packed = jnp.concatenate([item.reshape(-1) for item in totals])
+    for group in REDUCTION_ORDER:
+        packed = lax.psum(packed, group)
+    sizes = [math.prod(item.shape) for item in totals]
+    pieces = jnp.split(packed, [sum(sizes[: k + 1]) for k in range(len(sizes) - 1)])
+    totals = [piece.reshape(item.shape) for piece, item in zip(pieces, totals)]
     factor = 1.0 / math.sqrt(
-        row_count * lax.axis_size("wire") * column_count * lax.axis_size("tick")
+        row_count * lax.axis_size(WIRE) * column_count * lax.axis_size(TICK)
     )
     return (
         response,
@@ -137,8 +144,10 @@
 
 
 def solution(mesh):
-    in_specs = (P(None, "wire", "tick"), P(), P(), P(), P(), P(), P(), P(None, "wire", "tick"))
-    out_specs = (P(None, "wire", "tick"), P(None, "wire", "tick"), P(), P(), P(), P(), P(), P())
+    fine = Mesh(mesh.devices.reshape(8, 4, 2, 2, 4), TICK + WIRE)
+    block = P(None, WIRE, TICK)
+    in_specs = (block, P(), P(), P(), P(), P(), P(), block)
+    out_specs = (block, block, P(), P(), P(), P(), P(), P())
     return jax.shard_map(
-        per_device, mesh=mesh, in_specs=in_specs, out_specs=out_specs, check_vma=False
+        per_device, mesh=fine, in_specs=in_specs, out_specs=out_specs, check_vma=False
     )

time: 260 us -> 216 us (0.83)
  the two profiles are of different devices: /device:TPU:30 before, /device:TPU:27 now
where the time goes in v1:
time: 216 us; the launch traced here: 215 us
  waiting for transfers between devices  68.6 us (32%)
  starting transfers between devices  53.2 us (25%)
  blocking collectives  34.9 us (16%)
  other arithmetic  33.2 us (15%)
  matrix products  12.1 us (6%)
  local copies, waits for them, and re-layouts  11.9 us (6%)
    ppermute x8, waiting for transfers between devices, with_halo(): lax.ppermute(lax.slice_in_dim(block, 0, width, axis=dim), axis, backward)  43.7 us
    psum x4, blocking collectives, per_device(): packed = lax.psum(packed, group)  34.9 us
    ppermute x8, starting transfers between devices, with_halo(): lax.ppermute(lax.slice_in_dim(block, block.shape[dim] - width, None, axis...  34.1 us
    ppermute x8, waiting for transfers between devices, with_halo(): lax.ppermute(lax.slice_in_dim(block, block.shape[dim] - width, None, axis...  24.8 us
    ppermute x8, starting transfers between devices, with_halo(): lax.ppermute(lax.slice_in_dim(block, 0, width, axis=dim), axis, backward)  19.2 us
    add x3, other arithmetic, depthwise(): total_sum + kernel_weight[:, row_index, column_index][:, None, None] * pa...  12.9 us
    reduce_sum x2, other arithmetic, tap_grads(): jnp.sum(upward_gradient * padded_input[:, row_index:row_index + row_count...  6.91 us
    unnamed x47, local copies, waits for them, and re-layouts  6.58 us
  transfers between devices with their start and end apart: 16, of which 10 were waited for; matrix products, arithmetic and copies ran while one was open for 6% of the time, Pallas kernels for 0%

profile of v1, /device:TPU:27, one launch (start us, length us, event | category | flops | bytes accessed | tf_op | source)
XLA Modules:
  0.0 215.1 jit_solution(8928391900136740163)
XLA Ops:
  0.6 1.4 constant_dynamic-update-slice_fusion.1
  2.2 6.4 %collective-permute-start = (f32[16,64,32]{2,0,1:T(8,128)S(1)}, f32[16,64,32]{2,0,1:T(8,128)S(1)}, u32[]{:S(2)}, u32[]{:S(2)}) collective-permute-start(f32[16,64,32]{2,0,1:T(8,128)S(1)} %get-tuple-element.133), channel_id=1, source_target_pairs={{0,8},{8,16},{16,24},{24,32},{32,40},{40,48},{48,56},{56,64},{64,7... | collective-permute-start | bytes 393224 | tf_op jit(solution)/shard_map/ppermute | solution.py:19
  8.6 1.9 collective-permute-start.1
  10.6 5.6 %collective-permute-done = f32[16,64,32]{2,0,1:T(8,128)S(1)} collective-permute-done((f32[16,64,32]{2,0,1:T(8,128)S(1)}, f32[16,64,32]{2,0,1:T(8,128)S(1)}, u32[]{:S(2)}, u32[]{:S(2)}) %collective-permute-start) | collective-permute-done | bytes 131104 | tf_op jit(solution)/shard_map/ppermute | solution.py:19
  16.2 12.0 %collective-permute-done.1 = f32[16,64,32]{2,0,1:T(8,128)S(1)} collective-permute-done((f32[16,64,32]{2,0,1:T(8,128)S(1)}, f32[16,64,32]{2,0,1:T(8,128)S(1)}, u32[]{:S(2)}, u32[]{:S(2)}) %collective-permute-start.1) | collective-permute-done | bytes 131104 | tf_op jit(solution)/shard_map/ppermute | solution.py:22
  28.3 3.1 %collective-permute-start.2 = (f32[16,1,192]{2,0,1:T(8,128)S(1)}, f32[16,1,192]{2,0,1:T(8,128)S(1)}, u32[]{:S(2)}, u32[]{:S(2)}) collective-permute-start(f32[16,1,192]{2,0,1:T(8,128)S(1)} %get-tuple-element.122), channel_id=1, source_target_pairs={{0,1},{1,2},{2,3},{3,4},{4,5},{5,6},{6,7},{8,9},{9,10},{10,11},{11... | collective-permute-start | bytes 36872 | tf_op jit(solution)/shard_map/ppermute | solution.py:19
  31.4 2.2 %collective-permute-start.3 = (f32[16,1,192]{2,0,1:T(8,128)S(1)}, f32[16,1,192]{2,0,1:T(8,128)S(1)}, u32[]{:S(2)}, u32[]{:S(2)}) collective-permute-start(f32[16,1,192]{2,0,1:T(8,128)S(1)} %get-tuple-element.123), channel_id=1, source_target_pairs={{1,0},{2,1},{3,2},{4,3},{5,4},{6,5},{7,6},{9,8},{10,9},{11,10},{12... | collective-permute-start | bytes 36872 | tf_op jit(solution)/shard_map/ppermute | solution.py:22
  33.6 2.2 %collective-permute-done.3 = f32[16,1,192]{2,0,1:T(8,128)S(1)} collective-permute-done((f32[16,1,192]{2,0,1:T(8,128)S(1)}, f32[16,1,192]{2,0,1:T(8,128)S(1)}, u32[]{:S(2)}, u32[]{:S(2)}) %collective-permute-start.3) | collective-permute-done | bytes 12320 | tf_op jit(solution)/shard_map/ppermute | solution.py:22
  35.9 0.9 maximum_maximum_fusion
  36.8 3.9 %multiply_add_fusion.1 = f32[16,64,128]{2,0,1:T(8,128)S(1)} fusion(f32[16,64,128]{2,0,1:T(8,128)S(1)} %get-tuple-element.132, f32[16,65,192]{2,0,1:T(8,128)S(1)} %get-tuple-element.121, f32[16,64,160]{2,0,1:T(8,128)S(1)} %constant_dynamic-update-slice_fusion, f32[16,65,192]{2,0,1:T(8,128)S(1)} %get-tuple-element.120, f32[16]{0:T(128)S(1)} %get-tuple-element.187, ...), kind=kLoop, calls=%fused_computation.251 | loop fusion | flops 7471104 | bytes 12715712 | tf_op jit(solution)/shard_map/add | solution.py:37
  40.8 1.4 fusion.93
  42.4 2.2 %collective-permute-start.4 = (f32[16,64,32]{2,0,1:T(8,128)S(1)}, f32[16,64,32]{2,0,1:T(8,128)S(1)}, u32[]{:S(2)}, u32[]{:S(2)}) collective-permute-start(f32[16,64,32]{2,0,1:T(8,128)S(1)} %get-tuple-element.129), channel_id=1, source_target_pairs={{0,8},{8,16},{16,24},{24,32},{32,40},{40,48},{48,56},{56,64},{64,7... | collective-permute-start | bytes 393224 | tf_op jit(solution)/shard_map/ppermute | solution.py:19
  44.6 2.2 %collective-permute-start.5 = (f32[16,64,32]{2,0,1:T(8,128)S(1)}, f32[16,64,32]{2,0,1:T(8,128)S(1)}, u32[]{:S(2)}, u32[]{:S(2)}) collective-permute-start(f32[16,64,32]{2,0,1:T(8,128)S(1)} %get-tuple-element.130), channel_id=1, source_target_pairs={{8,0},{16,8},{24,16},{32,24},{40,32},{48,40},{56,48},{64,56},{72,6... | collective-permute-start | bytes 393224 | tf_op jit(solution)/shard_map/ppermute | solution.py:22
  46.8 6.7 %collective-permute-done.4 = f32[16,64,32]{2,0,1:T(8,128)S(1)} collective-permute-done((f32[16,64,32]{2,0,1:T(8,128)S(1)}, f32[16,64,32]{2,0,1:T(8,128)S(1)}, u32[]{:S(2)}, u32[]{:S(2)}) %collective-permute-start.4) | collective-permute-done | bytes 131104 | tf_op jit(solution)/shard_map/ppermute | solution.py:19
  53.5 9.8 %collective-permute-done.5 = f32[16,64,32]{2,0,1:T(8,128)S(1)} collective-permute-done((f32[16,64,32]{2,0,1:T(8,128)S(1)}, f32[16,64,32]{2,0,1:T(8,128)S(1)}, u32[]{:S(2)}, u32[]{:S(2)}) %collective-permute-start.5) | collective-permute-done | bytes 131104 | tf_op jit(solution)/shard_map/ppermute | solution.py:22
  63.3 4.9 %collective-permute-start.6 = (f32[16,1,192]{2,0,1:T(8,128)S(1)}, f32[16,1,192]{2,0,1:T(8,128)S(1)}, u32[]{:S(2)}, u32[]{:S(2)}) collective-permute-start(f32[16,1,192]{2,0,1:T(8,128)S(1)} %get-tuple-element.118), channel_id=1, source_target_pairs={{0,1},{1,2},{2,3},{3,4},{4,5},{5,6},{6,7},{8,9},{9,10},{10,11},{11... | collective-permute-start | bytes 36872 | tf_op jit(solution)/shard_map/ppermute | solution.py:19
  68.3 1.9 collective-permute-start.7
  70.2 2.5 %collective-permute-done.7 = f32[16,1,192]{2,0,1:T(8,128)S(1)} collective-permute-done((f32[16,1,192]{2,0,1:T(8,128)S(1)}, f32[16,1,192]{2,0,1:T(8,128)S(1)}, u32[]{:S(2)}, u32[]{:S(2)}) %collective-permute-start.7) | collective-permute-done | bytes 12320 | tf_op jit(solution)/shard_map/ppermute | solution.py:22
  73.7 4.5 %multiply_add_fusion = f32[16,64,128]{2,0,1:T(8,128)S(1)} fusion(f32[16,64,128]{2,0,1:T(8,128)S(1)} %get-tuple-element.195, f32[16,65,192]{2,0,1:T(8,128)S(1)} %get-tuple-element.117, f32[16,65,192]{2,0,1:T(8,128)S(1)} %get-tuple-element.116, f32[16]{0:T(128)S(1)} %get-tuple-element.160, f32[16]{0:T(128)S(1)} %get-tuple-element.161, ...), kind=kLoop, calls=%fused_computation.248 | loop fusion | flops 7995392 | bytes 10749632 | tf_op jit(solution)/shard_map/add | solution.py:37
  78.2 1.8 fusion.98
  80.0 3.0 %multiply_reduce_fusion.18 = (f32[16]{0:T(128)S(1)}, f32[16]{0:T(128)S(1)}, f32[16]{0:T(128)S(1)}, f32[16]{0:T(128)S(1)}, f32[16]{0:T(128)S(1)}, /*index=5*/f32[...) fusion(f32[16,65,192]{2,0,1:T(8,128)S(1)} %get-tuple-element.11, ...), kind=kOutput, calls=%fused_computation.210 | convolution fusion | flops 29884128 | bytes 10487936 | tf_op jit(solution)/shard_map/oc,owt->cwt/dot_general | solution.py:109
  83.1 1.1 fusion.102
  84.2 2.1 collective-permute-start.8
  86.4 2.4 %collective-permute-start.9 = (f32[16,64,32]{2,0,1:T(8,128)}, f32[16,64,32]{2,0,1:T(8,128)}, u32[]{:S(2)}, u32[]{:S(2)}) collective-permute-start(f32[16,64,32]{2,0,1:T(8,128)} %get-tuple-element.127), channel_id=1, source_target_pairs={{8,0},{16,8},{24,16},{32,24},{40,32},{48,40},{56,48},{64,56},{72,6... | collective-permute-start | bytes 393224 | tf_op jit(solution)/shard_map/ppermute | solution.py:22
  88.8 5.1 %multiply_reduce_fusion.9 = (f32[16]{0:T(128)S(1)}, f32[16]{0:T(128)S(1)}, f32[16]{0:T(128)S(1)}, f32[16]{0:T(128)S(1)}, f32[16]{0:T(128)S(1)}, /*index=5*/f32[1...) fusion(f32[16,64,128]{2,0,1:T(8,128)} %copy-done.3, f32[16,64,32]{2,0,1:T(8,128)} %copy-done.8, ...), kind=kLoop, calls=%fused_computation.201 | loop fusion | flops 3932016 | bytes 1835584 | tf_op jit(solution)/shard_map/reduce_sum | solution.py:56
  94.0 2.0 convolution_bitcast_fusion.2
  96.0 2.5 %collective-permute-done.8 = f32[16,64,32]{2,0,1:T(8,128)} collective-permute-done((f32[16,64,32]{2,0,1:T(8,128)}, f32[16,64,32]{2,0,1:T(8,128)}, u32[]{:S(2)}, u32[]{:S(2)}) %collective-permute-start.8) | collective-permute-done | bytes 131104 | tf_op jit(solution)/shard_map/ppermute | solution.py:19
  98.5 8.5 %collective-permute-done.9 = f32[16,64,32]{2,0,1:T(8,128)} collective-permute-done((f32[16,64,32]{2,0,1:T(8,128)}, f32[16,64,32]{2,0,1:T(8,128)}, u32[]{:S(2)}, u32[]{:S(2)}) %collective-permute-start.9) | collective-permute-done | bytes 131104 | tf_op jit(solution)/shard_map/ppermute | solution.py:22
  107.8 2.3 %collective-permute-start.10 = (f32[16,1,192]{2,0,1:T(8,128)S(1)}, f32[16,1,192]{2,0,1:T(8,128)S(1)}, u32[]{:S(2)}, u32[]{:S(2)}) collective-permute-start(f32[16,1,192]{2,0,1:T(8,128)S(1)} %get-tuple-element.114), channel_id=1, source_target_pairs={{0,1},{1,2},{2,3},{3,4},{4,5},{5,6},{6,7},{8,9},{9,10},{10,11},{11... | collective-permute-start | bytes 36872 | tf_op jit(solution)/shard_map/ppermute | solution.py:19
  110.0 3.0 %collective-permute-start.11 = (f32[16,1,192]{2,0,1:T(8,128)S(1)}, f32[16,1,192]{2,0,1:T(8,128)S(1)}, u32[]{:S(2)}, u32[]{:S(2)}) collective-permute-start(f32[16,1,192]{2,0,1:T(8,128)S(1)} %get-tuple-element.115), channel_id=1, source_target_pairs={{1,0},{2,1},{3,2},{4,3},{5,4},{6,5},{7,6},{9,8},{10,9},{11,10},{12... | collective-permute-start | bytes 36872 | tf_op jit(solution)/shard_map/ppermute | solution.py:22
  113.4 2.0 copy.40
  115.4 2.5 %maximum_maximum_fusion.2 = (f32[16,65,192]{2,0,1:T(8,128)S(1)}, f32[16,65,192]{2,0,1:T(8,128)S(1)}) fusion(f32[16,64,32]{2,0,1:T(8,128)} %collective-permute-done.9, f32[16,64,128]{2,0,1:T(8,128)S(1)} %copy-done.4, f32[16,64,32]{2,0,1:T(8,128)} %collective-permute-done.8, f32[16,1,192]{2,0,1:T(8,128)S(1)} %collective-permute-done.10, ...), kind=kLoop, calls=%fused_computation.54 | loop fusion | flops 1198080 | bytes 2408448 | tf_op jit(solution)/shard_map/concatenate | solution.py:23
  117.9 6.5 %fusion.99 = (f32[16]{0:T(128)S(1)}, f32[16,64,128]{2,0,1:T(8,128)S(1)}) fusion(f32[16,64,128]{2,0,1:T(8,128)S(1)} %copy-done.13, f32[16,65,192]{2,0,1:T(8,128)S(1)} %get-tuple-element.113, f32[16]{0:T(128)S(1)} %get-tuple-element.135, f32[16]{0:T(128)S(1)} %get-tuple-element.154, f32[16]{0:T(128)S(1)} %get-tuple-element.159, f32[16]{0:T(128)S(1)} %get-tuple-element.158, ...), kind=kLoop, calls=%fused_computation.333 | loop fusion | flops 9175024 | bytes 11273984 | tf_op jit(solution)/shard_map/reduce_sum | solution.py:116
  125.2 3.0 %multiply_reduce_fusion.45 = (f32[16]{0:T(128)S(1)}, f32[16]{0:T(128)S(1)}, f32[16]{0:T(128)S(1)}, f32[16]{0:T(128)S(1)}, f32[16]{0:T(128)S(1)}, /*index=5*/f32[...) fusion(f32[16,65,192]{2,0,1:T(8,128)S(1)} %get-tuple-element.12, ...), kind=kOutput, calls=%fused_computation.237 | convolution fusion | flops 29884128 | bytes 10487936 | tf_op jit(solution)/shard_map/oc,owt->cwt/dot_general | solution.py:117
  128.3 1.1 fusion.101
  130.2 1.9 multiply_reduce_fusion.36
  132.5 2.5 %psum.28 = f32[1408]{0:T(1024)S(1)} all-reduce(f32[1408]{0:T(1024)S(1)} %concatenate.175), channel_id=1, replica_groups=mesh['y'=8,'z_hi'=4,'core'=2,'z_lo'=2,'x'=4] {'core'}, use_global_device_ids=true, to_apply=%region_56.57 | all-reduce | flops 1408 | bytes 11264 | tf_op jit(solution)/shard_map/psum | solution.py:127
  135.0 6.2 %psum.29 = f32[1408]{0:T(1024)S(1)} all-reduce(f32[1408]{0:T(1024)S(1)} %psum.28), channel_id=1, replica_groups=mesh['y'=8,'z_hi'=4,'core'=2,'z_lo'=2,'x'=4] {'x'}, use_global_device_ids=true, to_apply=%region_57.58 | all-reduce | flops 1408 | bytes 11264 | tf_op jit(solution)/shard_map/psum | solution.py:127
  141.2 15.5 %psum.30 = f32[1408]{0:T(1024)S(1)} all-reduce(f32[1408]{0:T(1024)S(1)} %psum.29), channel_id=1, replica_groups=mesh['y'=8,'z_hi'=4,'core'=2,'z_lo'=2,'x'=4] {'z_hi','z_lo'}, use_global_device_ids=true, to_apply=%region_58.59 | all-reduce | flops 1408 | bytes 11264 | tf_op jit(solution)/shard_map/psum | solution.py:127
  156.7 10.7 %psum.31 = f32[1408]{0:T(1024)S(1)} all-reduce(f32[1408]{0:T(1024)S(1)} %psum.30), channel_id=1, replica_groups=mesh['y'=8,'z_hi'=4,'core'=2,'z_lo'=2,'x'=4] {'y'}, use_global_device_ids=true, to_apply=%region_59.60 | all-reduce | flops 1408 | bytes 11264 | tf_op jit(solution)/shard_map/psum | solution.py:127
  167.5 11.2 %collective-permute-start.12 = (f32[16,64,32]{2,0,1:T(8,128)}, f32[16,64,32]{2,0,1:T(8,128)S(1)}, u32[]{:S(2)}, u32[]{:S(2)}) collective-permute-start(f32[16,64,32]{2,0,1:T(8,128)} %get-tuple-element.124), channel_id=1, source_target_pairs={{0,8},{8,16},{16,24},{24,32},{32,40},{40,48},{48,56},{56,64},{64,7... | collective-permute-start | bytes 393224 | tf_op jit(solution)/shard_map/ppermute | solution.py:19
  178.6 2.1 collective-permute-start.13
  180.8 9.9 %collective-permute-done.12 = f32[16,64,32]{2,0,1:T(8,128)S(1)} collective-permute-done((f32[16,64,32]{2,0,1:T(8,128)}, f32[16,64,32]{2,0,1:T(8,128)S(1)}, u32[]{:S(2)}, u32[]{:S(2)}) %collective-permute-start.12) | collective-permute-done | bytes 131104 | tf_op jit(solution)/shard_map/ppermute | solution.py:19
  190.7 8.8 %collective-permute-done.13 = f32[16,64,32]{2,0,1:T(8,128)S(1)} collective-permute-done((f32[16,64,32]{2,0,1:T(8,128)}, f32[16,64,32]{2,0,1:T(8,128)S(1)}, u32[]{:S(2)}, u32[]{:S(2)}) %collective-permute-start.13) | collective-permute-done | bytes 131104 | tf_op jit(solution)/shard_map/ppermute | solution.py:22
  199.6 1.9 collective-permute-start.14
  201.5 3.6 %collective-permute-start.15 = (f32[16,1,192]{2,0,1:T(8,128)S(1)}, f32[16,1,192]{2,0,1:T(8,128)S(1)}, u32[]{:S(2)}, u32[]{:S(2)}) collective-permute-start(f32[16,1,192]{2,0,1:T(8,128)S(1)} %get-tuple-element.111), channel_id=1, source_target_pairs={{1,0},{2,1},{3,2},{4,3},{5,4},{6,5},{7,6},{9,8},{10,9},{11,10},{12... | collective-permute-start | bytes 36872 | tf_op jit(solution)/shard_map/ppermute | solution.py:22
  209.6 4.5 %fusion.14 = f32[16,64,128]{2,0,1:T(8,128)S(1)} fusion(f32[16,64,128]{2,0,1:T(8,128)S(1)} %get-tuple-element.197, f32[16,64,32]{2,0,1:T(8,128)S(1)} %collective-permute-done.13, f32[16,64,32]{2,0,1:T(8,128)S(1)} %collective-permute-done.12, f32[16,65,192]{2,0,1:T(8,128)S(1)} %get-tuple-element.109, f32[16,65,192]{2,0,1:T(8,128)S(1)} %get-tuple-element.108, ...), kind=kLoop, calls=%fused_computation.70 | loop fusion | flops 7995392 | bytes 10749632 | tf_op jit(solution)/shard_map/add | solution.py:37
  214.1 1.0 copy.41
  (86 shorter events, 9.7 us)
Async XLA Ops:
  0.6 77.5 %copy-start = (f32[16,16]{1,0:T(8,128)S(1)}, f32[16,16]{1,0:T(8,128)}, u32[]{:S(2)}) copy-start(f32[16,16]{1,0:T(8,128)} %param.13) | copy-start | bytes 3076
  2.0 8.5 %copy-start.15 = (f32[16,3,9]{0,1,2:T(4,128)S(1)}, f32[16,3,9]{0,1,2:T(4,128)}, u32[]{:S(2)}) copy-start(f32[16,3,9]{0,1,2:T(4,128)} %param.9) | copy-start | bytes 5188
  2.2 14.0 %collective-permute-start = (f32[16,64,32]{2,0,1:T(8,128)S(1)}, f32[16,64,32]{2,0,1:T(8,128)S(1)}, u32[]{:S(2)}, u32[]{:S(2)}) collective-permute-start(f32[16,64,32]{2,0,1:T(8,128)S(1)} %get-tuple-element.133), channel_id=1, source_target_pairs={{0,8},{8,16},{16,24},{24,32},{32,40},{40,48},{48,56},{56,64},{64,7... | collective-permute-start | bytes 393224 | tf_op jit(solution)/shard_map/ppermute | solution.py:19
  8.6 19.6 %collective-permute-start.1 = (f32[16,64,32]{2,0,1:T(8,128)S(1)}, f32[16,64,32]{2,0,1:T(8,128)S(1)}, u32[]{:S(2)}, u32[]{:S(2)}) collective-permute-start(f32[16,64,32]{2,0,1:T(8,128)S(1)} %get-tuple-element.134), channel_id=1, source_target_pairs={{8,0},{16,8},{24,16},{32,24},{40,32},{48,40},{56,48},{64,56},{72,6... | collective-permute-start | bytes 393224 | tf_op jit(solution)/shard_map/ppermute | solution.py:22
  16.2 20.5 %copy-start.5 = (f32[16,64,32]{2,0,1:T(8,128)}, f32[16,64,32]{2,0,1:T(8,128)S(1)}, u32[]{:S(2)}) copy-start(f32[16,64,32]{2,0,1:T(8,128)S(1)} %collective-permute-done) | copy-start | bytes 393220
  28.3 5.4 %collective-permute-start.2 = (f32[16,1,192]{2,0,1:T(8,128)S(1)}, f32[16,1,192]{2,0,1:T(8,128)S(1)}, u32[]{:S(2)}, u32[]{:S(2)}) collective-permute-start(f32[16,1,192]{2,0,1:T(8,128)S(1)} %get-tuple-element.122), channel_id=1, source_target_pairs={{0,1},{1,2},{2,3},{3,4},{4,5},{5,6},{6,7},{8,9},{9,10},{10,11},{11... | collective-permute-start | bytes 36872 | tf_op jit(solution)/shard_map/ppermute | solution.py:19
  31.4 4.5 %collective-permute-start.3 = (f32[16,1,192]{2,0,1:T(8,128)S(1)}, f32[16,1,192]{2,0,1:T(8,128)S(1)}, u32[]{:S(2)}, u32[]{:S(2)}) collective-permute-start(f32[16,1,192]{2,0,1:T(8,128)S(1)} %get-tuple-element.123), channel_id=1, source_target_pairs={{1,0},{2,1},{3,2},{4,3},{5,4},{6,5},{7,6},{9,8},{10,9},{11,10},{12... | collective-permute-start | bytes 36872 | tf_op jit(solution)/shard_map/ppermute | solution.py:22
  33.6 3.1 %copy-start.1 = (f32[16,64,160]{2,0,1:T(8,128)}, f32[16,64,160]{2,0,1:T(8,128)S(1)}, u32[]{:S(2)}) copy-start(f32[16,64,160]{2,0,1:T(8,128)S(1)} %constant_dynamic-update-slice_fusion) | copy-start | bytes 1966084
  36.8 4.0 %copy-start.18 = (f32[16,16]{1,0:T(8,128)S(1)}, f32[16,16]{1,0:T(8,128)}, u32[]{:S(2)}) copy-start(f32[16,16]{1,0:T(8,128)} %param.10) | copy-start | bytes 3076
  36.8 4.0 %copy-start.19 = (f32[16]{0:T(128)S(1)}, f32[16]{0:T(128)}, u32[]{:S(2)}) copy-start(f32[16]{0:T(128)} %param.11) | copy-start | bytes 196
  40.8 1.4 copy-start.10
  42.2 4.5 %copy-start.16 = (f32[16,3,9]{0,1,2:T(4,128)S(1)}, f32[16,3,9]{0,1,2:T(4,128)}, u32[]{:S(2)}) copy-start(f32[16,3,9]{0,1,2:T(4,128)} %param.12) | copy-start | bytes 5188
  42.4 11.1 %collective-permute-start.4 = (f32[16,64,32]{2,0,1:T(8,128)S(1)}, f32[16,64,32]{2,0,1:T(8,128)S(1)}, u32[]{:S(2)}, u32[]{:S(2)}) collective-permute-start(f32[16,64,32]{2,0,1:T(8,128)S(1)} %get-tuple-element.129), channel_id=1, source_target_pairs={{0,8},{8,16},{16,24},{24,32},{32,40},{40,48},{48,56},{56,64},{64,7... | collective-permute-start | bytes 393224 | tf_op jit(solution)/shard_map/ppermute | solution.py:19
  44.6 18.7 %collective-permute-start.5 = (f32[16,64,32]{2,0,1:T(8,128)S(1)}, f32[16,64,32]{2,0,1:T(8,128)S(1)}, u32[]{:S(2)}, u32[]{:S(2)}) collective-permute-start(f32[16,64,32]{2,0,1:T(8,128)S(1)} %get-tuple-element.130), channel_id=1, source_target_pairs={{8,0},{16,8},{24,16},{32,24},{40,32},{48,40},{56,48},{64,56},{72,6... | collective-permute-start | bytes 393224 | tf_op jit(solution)/shard_map/ppermute | solution.py:22
  53.5 20.1 %copy-start.7 = (f32[16,64,32]{2,0,1:T(8,128)}, f32[16,64,32]{2,0,1:T(8,128)S(1)}, u32[]{:S(2)}) copy-start(f32[16,64,32]{2,0,1:T(8,128)S(1)} %collective-permute-done.4) | copy-start | bytes 393220
  63.3 10.4 %copy-start.8 = (f32[16,64,32]{2,0,1:T(8,128)}, f32[16,64,32]{2,0,1:T(8,128)S(1)}, u32[]{:S(2)}) copy-start(f32[16,64,32]{2,0,1:T(8,128)S(1)} %collective-permute-done.5) | copy-start | bytes 393220
  63.3 6.9 %collective-permute-start.6 = (f32[16,1,192]{2,0,1:T(8,128)S(1)}, f32[16,1,192]{2,0,1:T(8,128)S(1)}, u32[]{:S(2)}, u32[]{:S(2)}) collective-permute-start(f32[16,1,192]{2,0,1:T(8,128)S(1)} %get-tuple-element.118), channel_id=1, source_target_pairs={{0,1},{1,2},{2,3},{3,4},{4,5},{5,6},{6,7},{8,9},{9,10},{10,11},{11... | collective-permute-start | bytes 36872 | tf_op jit(solution)/shard_map/ppermute | solution.py:19
  68.3 4.5 %collective-permute-start.7 = (f32[16,1,192]{2,0,1:T(8,128)S(1)}, f32[16,1,192]{2,0,1:T(8,128)S(1)}, u32[]{:S(2)}, u32[]{:S(2)}) collective-permute-start(f32[16,1,192]{2,0,1:T(8,128)S(1)} %get-tuple-element.119), channel_id=1, source_target_pairs={{1,0},{2,1},{3,2},{4,3},{5,4},{6,5},{7,6},{9,8},{10,9},{11,10},{12... | collective-permute-start | bytes 36872 | tf_op jit(solution)/shard_map/ppermute | solution.py:22
  73.7 4.5 %copy-start.17 = (f32[16,64,128]{2,1,0:T(8,128)S(1)}, f32[16,64,128]{2,1,0:T(8,128)}, u32[]{:S(2)}) copy-start(f32[16,64,128]{2,1,0:T(8,128)} %param.15) | copy-start | bytes 1572868
  73.7 4.5 %copy-start.20 = (f32[16]{0:T(128)S(1)}, f32[16]{0:T(128)}, u32[]{:S(2)}) copy-start(f32[16]{0:T(128)} %param.14) | copy-start | bytes 196
  78.2 1.8 copy-start.12
  80.0 3.0 %copy-start.14 = (f32[16,64,128]{2,0,1:T(8,128)}, f32[16,64,128]{2,0,1:T(8,128)S(1)}, u32[]{:S(2)}) copy-start(f32[16,64,128]{2,0,1:T(8,128)S(1)} %get-tuple-element.105) | copy-start | bytes 1572868
  83.1 5.7 %copy-start.3 = (f32[16,64,128]{2,0,1:T(8,128)}, f32[16,64,128]{2,0,1:T(8,128)S(1)}, u32[]{:S(2)}) copy-start(f32[16,64,128]{2,0,1:T(8,128)S(1)} %get-tuple-element.198) | copy-start | bytes 1572868
  84.2 14.2 %collective-permute-start.8 = (f32[16,64,32]{2,0,1:T(8,128)}, f32[16,64,32]{2,0,1:T(8,128)}, u32[]{:S(2)}, u32[]{:S(2)}) collective-permute-start(f32[16,64,32]{2,0,1:T(8,128)} %get-tuple-element.126), channel_id=1, source_target_pairs={{0,8},{8,16},{16,24},{24,32},{32,40},{40,48},{48,56},{56,64},{64,7... | collective-permute-start | bytes 393224 | tf_op jit(solution)/shard_map/ppermute | solution.py:19
  86.4 20.5 %collective-permute-start.9 = (f32[16,64,32]{2,0,1:T(8,128)}, f32[16,64,32]{2,0,1:T(8,128)}, u32[]{:S(2)}, u32[]{:S(2)}) collective-permute-start(f32[16,64,32]{2,0,1:T(8,128)} %get-tuple-element.127), channel_id=1, source_target_pairs={{8,0},{16,8},{24,16},{32,24},{40,32},{48,40},{56,48},{64,56},{72,6... | collective-permute-start | bytes 393224 | tf_op jit(solution)/shard_map/ppermute | solution.py:22
  93.9 13.1 %copy-start.4 = (f32[16,64,128]{2,0,1:T(8,128)S(1)}, f32[16,64,128]{2,0,1:T(8,128)}, u32[]{:S(2)}) copy-start(f32[16,64,128]{2,0,1:T(8,128)} %copy-done.3) | copy-start | bytes 1572868
  107.8 7.6 %collective-permute-start.10 = (f32[16,1,192]{2,0,1:T(8,128)S(1)}, f32[16,1,192]{2,0,1:T(8,128)S(1)}, u32[]{:S(2)}, u32[]{:S(2)}) collective-permute-start(f32[16,1,192]{2,0,1:T(8,128)S(1)} %get-tuple-element.114), channel_id=1, source_target_pairs={{0,1},{1,2},{2,3},{3,4},{4,5},{5,6},{6,7},{8,9},{9,10},{10,11},{11... | collective-permute-start | bytes 36872 | tf_op jit(solution)/shard_map/ppermute | solution.py:19
  110.0 5.4 %collective-permute-start.11 = (f32[16,1,192]{2,0,1:T(8,128)S(1)}, f32[16,1,192]{2,0,1:T(8,128)S(1)}, u32[]{:S(2)}, u32[]{:S(2)}) collective-permute-start(f32[16,1,192]{2,0,1:T(8,128)S(1)} %get-tuple-element.115), channel_id=1, source_target_pairs={{1,0},{2,1},{3,2},{4,3},{5,4},{6,5},{7,6},{9,8},{10,9},{11,10},{12... | collective-permute-start | bytes 36872 | tf_op jit(solution)/shard_map/ppermute | solution.py:22
  115.4 2.5 %copy-start.13 = (f32[16,64,128]{2,0,1:T(8,128)S(1)}, f32[16,64,128]{2,0,1:T(8,128)}, u32[]{:S(2)}) copy-start(f32[16,64,128]{2,0,1:T(8,128)} %get-tuple-element.196) | copy-start | bytes 1572868
  117.9 6.5 %copy-start.11 = (f32[16,64,128]{2,0,1:T(8,128)S(1)}, f32[16,64,128]{2,0,1:T(8,128)}, u32[]{:S(2)}) copy-start(f32[16,64,128]{2,0,1:T(8,128)} %copy-done.10) | copy-start | bytes 1572868
  128.3 1.6 copy-start.2
  128.3 1.7 copy-start.6
  128.3 1.9 copy-start.9
  167.5 23.2 %collective-permute-start.12 = (f32[16,64,32]{2,0,1:T(8,128)}, f32[16,64,32]{2,0,1:T(8,128)S(1)}, u32[]{:S(2)}, u32[]{:S(2)}) collective-permute-start(f32[16,64,32]{2,0,1:T(8,128)} %get-tuple-element.124), channel_id=1, source_target_pairs={{0,8},{8,16},{16,24},{24,32},{32,40},{40,48},{48,56},{56,64},{64,7... | collective-permute-start | bytes 393224 | tf_op jit(solution)/shard_map/ppermute | solution.py:19
  178.6 20.9 %collective-permute-start.13 = (f32[16,64,32]{2,0,1:T(8,128)}, f32[16,64,32]{2,0,1:T(8,128)S(1)}, u32[]{:S(2)}, u32[]{:S(2)}) collective-permute-start(f32[16,64,32]{2,0,1:T(8,128)} %get-tuple-element.125), channel_id=1, source_target_pairs={{8,0},{16,8},{24,16},{32,24},{40,32},{48,40},{56,48},{64,56},{72,6... | collective-permute-start | bytes 393224 | tf_op jit(solution)/shard_map/ppermute | solution.py:22
  199.6 9.2 %collective-permute-start.14 = (f32[16,1,192]{2,0,1:T(8,128)S(1)}, f32[16,1,192]{2,0,1:T(8,128)S(1)}, u32[]{:S(2)}, u32[]{:S(2)}) collective-permute-start(f32[16,1,192]{2,0,1:T(8,128)S(1)} %get-tuple-element.110), channel_id=1, source_target_pairs={{0,1},{1,2},{2,3},{3,4},{4,5},{5,6},{6,7},{8,9},{9,10},{10,11},{11... | collective-permute-start | bytes 36872 | tf_op jit(solution)/shard_map/ppermute | solution.py:19
  201.5 7.2 %collective-permute-start.15 = (f32[16,1,192]{2,0,1:T(8,128)S(1)}, f32[16,1,192]{2,0,1:T(8,128)S(1)}, u32[]{:S(2)}, u32[]{:S(2)}) collective-permute-start(f32[16,1,192]{2,0,1:T(8,128)S(1)} %get-tuple-element.111), channel_id=1, source_target_pairs={{1,0},{2,1},{3,2},{4,3},{5,4},{6,5},{7,6},{9,8},{10,9},{11,10},{12... | collective-permute-start | bytes 36872 | tf_op jit(solution)/shard_map/ppermute | solution.py:22

commit v2 on v1

v2 whole, which is shorter than its diff:
```python
import math

import jax
import jax.numpy as jnp
from jax import lax
from jax.experimental import pallas as pl
from jax.experimental.pallas import tpu as pltpu
from jax.sharding import Mesh, PartitionSpec as P

TICK = ("y", "z_hi", "core")
WIRE = ("z_lo", "x")
REDUCTION_ORDER = ("core", "x", ("z_hi", "z_lo"), "y")

CHANNELS, WIRES, TICKS = 16, 64, 128
STEP = 8
BLOCKS = TICKS // STEP
MARGIN = 4
ROWS = WIRES + 2 * MARGIN
FIRST = 8
OWN = FIRST + MARGIN
DEEP = FIRST + ROWS + 8
TILE = 128
F32, BF16 = jnp.float32, jnp.bfloat16


def lanes(shape):
    return lax.broadcasted_iota(jnp.int32, shape, len(shape) - 1)


def exchange(tiles):
    tiles = list(tiles)
    lane = lanes(tiles[0].shape)
    for bit in range(4):
        shift = STEP << bit
        upper = (lane & shift) != 0
        for low in range(16):
            if low >> bit & 1:
                continue
            high = low | 1 << bit
            a, b = tiles[low], tiles[high]
            tiles[low] = jnp.where(upper, pltpu.roll(b, shift, 1), a)
            tiles[high] = jnp.where(upper, b, pltpu.roll(a, TILE - shift, 1))
    return tiles


def tap(row, column, flip):
    return (2 - row) * 9 + 8 - column if flip else row * 9 + column


def convolve(source, target, kernel, flip, planes, first, groups):
    def group(index, _):
        base = first + 8 * index
        weights = [[kernel[tap(i, j, flip)] for j in range(9)] for i in range(3)]
        sums = {}
        for at in range(planes + 8):
            rows = [source[at, pl.ds(base + i - 1, 8), :] for i in range(3)]
            for j in range(9):
                plane = at - j
                if not 0 <= plane < planes:
                    continue
                value = weights[0][j] * rows[0] + weights[1][j] * rows[1] + weights[2][j] * rows[2]
                sums[plane] = sums[plane] + value if j else value
                if j == 8:
                    target[plane, pl.ds(base, 8), :] = sums.pop(plane)
        return 0

    lax.fori_loop(0, groups, group, 0)


def correlate(upward, ahead, source, start, lines, place):
    def group(index, carry):
        base = OWN + 8 * index
        sums = list(carry)
        ups = {}
        for at in range(BLOCKS + 8):
            if at < BLOCKS:
                ups[at] = upward[ahead + at, pl.ds(base, 8), :]
            rows = [source[start + at, pl.ds(base + i - 1, 8), :] for i in range(3)]
            for j in range(9):
                if 0 <= at - j < BLOCKS:
                    for i in range(3):
                        sums[9 * i + j] = sums[9 * i + j] + ups[at - j] * rows[i]
        return tuple(sums)

    zero = tuple(jnp.zeros((8, TILE), F32) for _ in range(27))
    sums = lax.fori_loop(0, WIRES // 8, group, zero)
    for k in range(27):
        lines[place + k : place + k + 1, :] = jnp.sum(sums[k], axis=0, keepdims=True)


def split(value):
    high = value.astype(BF16)
    return high, (value - high.astype(F32)).astype(BF16)


def mix(value, matrix):
    both = jnp.dot(jnp.concatenate(split(value), axis=1), matrix, preferred_element_type=F32)
    return both[:, :TILE] + both[:, TILE:]


def outer(left, right):
    lh, ll = split(left)
    rh, rl = split(right)
    return lax.dot_general(
        jnp.concatenate([lh, lh, ll], axis=0),
        jnp.concatenate([rh, rl, rh], axis=0),
        (((0,), (0,)), ((), ())),
        preferred_element_type=F32,
    )


def exact(left, right, contract):
    return lax.dot_general(
        left,
        right,
        (contract, ((), ())),
        precision=lax.Precision.HIGHEST,
        preferred_element_type=F32,
    )


def body(
    place, s_own, s_low, s_high, u_own, u_low, u_high, h_up, h_down, c_low, c_high,
    taps_front, taps_back, mixings, offsets,
    response, signal_grad, sums,
    sig, ups, fields_f, act, slope, fields_b, grads, u_back, u_front, result,
    kernel_front, kernel_back, halves, lines,
):
    tick_at, wire_at = place[0], place[1]

    spread = (lanes((CHANNELS, TILE)) // STEP) == lax.broadcasted_iota(
        jnp.int32, (CHANNELS, TILE), 0
    )
    spread = jnp.where(spread, 1.0, 0.0)
    for kernel, raw in ((kernel_front, taps_front), (kernel_back, taps_back)):
        wide = exact(raw[...], spread, ((0,), (0,)))
        for k in range(27):
            kernel[k] = jnp.broadcast_to(wide[k : k + 1, :], (8, TILE))
    biases = exact(offsets[...], spread, ((1,), (0,)))
    same = (lanes((TILE, TILE)) % STEP) == (
        lax.broadcasted_iota(jnp.int32, (TILE, TILE), 0) % STEP
    )
    for k in range(4):
        wide = exact(exact(spread, mixings[k], ((0,), (0,))), spread, ((1,), (0,)))
        high, low = split(jnp.where(same, wide, 0.0))
        halves[k, 0:TILE, 0:TILE] = high
        halves[k, 0:TILE, TILE:] = low
        halves[k, TILE:, 0:TILE] = high
        halves[k, TILE:, TILE:] = jnp.zeros((TILE, TILE), BF16)

    pad = jnp.zeros((8, TILE), F32)
    for planes in (sig, act, u_back, u_front):

        def clear(at, _, planes=planes):
            planes[at, 0:FIRST, :] = pad
            planes[at, FIRST + ROWS : DEEP, :] = pad
            return 0

        lax.fori_loop(0, planes.shape[0], clear, 0)
    lines[...] = jnp.zeros_like(lines)

    def load(source, row):
        return exchange([source[c, pl.ds(row, 8), :] for c in range(CHANNELS)])

    def fill(group, _):
        row = pl.multiple_of(8 * group, 8)
        for source, target, start in (
            (s_low, sig, 0),
            (s_own, sig, BLOCKS),
            (s_high, sig, 2 * BLOCKS),
            (u_own, ups, BLOCKS // 2),
        ):
            for a, tile in enumerate(load(source, row)):
                target[start + a, pl.ds(OWN + row, 8), :] = tile
        return 0

    lax.fori_loop(0, WIRES // 8, fill, 0)

    def fill_packed(group, _):
        row = pl.multiple_of(8 * group, 8)
        for source, start in ((u_low, 0), (u_high, BLOCKS // 2 + BLOCKS)):
            for a, tile in enumerate(load(source, row)):
                second, plane = divmod(a, BLOCKS // 2)
                at = OWN + row + second * (WIRES // 2)
                ups[start + plane, pl.ds(at, 8), :] = tile
        return 0

    lax.fori_loop(0, WIRES // 16, fill_packed, 0)
    for base, strips in (
        (FIRST, (c_low.at[0], h_up, c_high.at[0])),
        (OWN + WIRES, (c_low.at[1], h_down, c_high.at[1])),
    ):
        for k, strip in enumerate(strips):
            for a, tile in enumerate(load(strip, 0)):
                sig[BLOCKS * k + a, base : base + MARGIN, :] = tile[0:MARGIN]
                plane = BLOCKS * k + a - BLOCKS // 2
                if 0 <= plane < 2 * BLOCKS:
                    ups[plane, base : base + MARGIN, :] = tile[MARGIN:]

    whole = pl.ds(FIRST, ROWS)

    def rows_of(planes, at):
        return planes[pl.ds(at, 2), whole, :].reshape(2 * ROWS, TILE)

    def put(planes, at, value):
        planes[pl.ds(at, 2), whole, :] = value.reshape(2, ROWS, TILE)

    convolve(sig, fields_f, kernel_front, False, 40, FIRST, ROWS // 8)
    order = lax.broadcasted_iota(jnp.int32, (2 * ROWS, TILE), 0)
    wire = jnp.where(order < ROWS, order, order - ROWS) - MARGIN
    wire_in = jnp.logical_and(
        jnp.logical_or(wire >= 0, wire_at > 0), jnp.logical_or(wire < WIRES, wire_at < 7)
    )

    def front(pair, _):
        at = 2 * pair
        value = mix(rows_of(fields_f, at), halves[0]) + biases[0:1, :]
        tick_in = jnp.logical_and(
            jnp.logical_or(at >= 12, tick_at > 0), jnp.logical_or(at < 28, tick_at < 63)
        )
        inside = jnp.logical_and(wire_in, tick_in)
        sigmoid = 1.0 / (1.0 + jnp.exp(-value))
        put(act, at, jnp.where(inside, value * sigmoid, 0.0))
        put(slope, at, jnp.where(inside, sigmoid * (1.0 + value * (1.0 - sigmoid)), 0.0))
        return 0

    lax.fori_loop(0, 20, front, 0)

    convolve(act, fields_b, kernel_back, False, 32, FIRST, ROWS // 8)

    def back(pair, _):
        at = 2 * pair
        value = mix(rows_of(fields_b, at), halves[1]) + biases[1:2, :]
        sigmoid = 1.0 / (1.0 + jnp.exp(-value))
        put(result, at, value * sigmoid)
        grad = rows_of(ups, at) * (sigmoid * (1.0 + value * (1.0 - sigmoid)))
        put(grads, at, grad)
        put(u_back, at, mix(grad, halves[2]))
        return 0

    lax.fori_loop(0, 16, back, 0)

    def give(target, start):
        def some(group, _):
            row = pl.multiple_of(8 * group, 8)
            tiles = [result[start + a, pl.ds(OWN + row, 8), :] for a in range(BLOCKS)]
            for c, tile in enumerate(exchange(tiles)):
                target[c, pl.ds(row, 8), :] = tile
            return 0

        lax.fori_loop(0, WIRES // 8, some, 0)

    def tally(ahead, fields, start, square_at, line_at):
        own = pl.ds(OWN, WIRES)

        def some(pair, carry):
            square, line = carry
            grad = grads[pl.ds(ahead + 2 * pair, 2), own, :].reshape(2 * WIRES, TILE)
            field = fields[pl.ds(start + 2 * pair, 2), own, :].reshape(2 * WIRES, TILE)
            line = line + jnp.sum(grad.reshape(2 * WIRES // 8, 8, TILE), axis=0)
            return square + outer(grad, field), line

        square, line = lax.fori_loop(
            0, BLOCKS // 2, some, (jnp.zeros((TILE, TILE), F32), jnp.zeros((8, TILE), F32))
        )
        square = jnp.where(same, square, 0.0).reshape(CHANNELS, STEP, TILE)
        lines[square_at : square_at + CHANNELS, :] = jnp.sum(square, axis=1)
        lines[line_at : line_at + 1, :] = jnp.sum(line, axis=0, keepdims=True)

    give(response, 8)
    tally(8, fields_b, 8, 64, 27)
    correlate(u_back, 8, act, 8, lines, 0)

    convolve(u_back, fields_b, kernel_back, True, 24, FIRST, ROWS // 8)

    def under_front(pair, _):
        at = 2 * pair
        grad = rows_of(fields_b, at) * rows_of(slope, at + 8)
        put(grads, at, grad)
        put(u_front, at, mix(grad, halves[3]))
        return 0

    lax.fori_loop(0, 12, under_front, 0)
    tally(4, fields_f, 12, 80, 59)
    correlate(u_front, 4, sig, 12, lines, 32)
    convolve(u_front, result, kernel_front, True, 16, OWN, WIRES // 8)
    give(signal_grad, 0)

    found = lines[...]
    for shift in (1, 2, 4):
        found = found + pltpu.roll(found, TILE - shift, 1)
    row = lax.broadcasted_iota(jnp.int32, (8, TILE), 0)
    for k in range(12):
        turned = pltpu.roll(found[8 * k : 8 * k + 8], 0, 1, stride=1, stride_axis=0)
        sums[k : k + 1, :] = jnp.sum(
            jnp.where(lanes((8, TILE)) % STEP == row, turned, 0.0), axis=0, keepdims=True
        )


def local(*arrays, interpret=False):
    vmem = pl.BlockSpec(memory_space=pltpu.VMEM)
    field = jax.ShapeDtypeStruct((CHANNELS, WIRES, TICKS), F32)
    planes = lambda count: pltpu.VMEM((count, DEEP, TILE), F32)
    return pl.pallas_call(
        body,
        out_shape=(field, field, jax.ShapeDtypeStruct((12, TILE), F32)),
        in_specs=[pl.BlockSpec(memory_space=pltpu.SMEM)] + [vmem] * (len(arrays) - 1),
        out_specs=(vmem, vmem, vmem),
        scratch_shapes=[
            planes(48),
            planes(32),
            planes(40),
            planes(40),
            planes(40),
            planes(32),
            planes(32),
            planes(32),
            planes(24),
            planes(32),
            pltpu.VMEM((27, 8, TILE), F32),
            pltpu.VMEM((27, 8, TILE), F32),
            pltpu.VMEM((4, 2 * TILE, 2 * TILE), BF16),
            pltpu.VMEM((96, TILE), F32),
        ],
        compiler_params=pltpu.CompilerParams(vmem_limit_bytes=48 * 1024 * 1024),
        interpret=interpret,
        name="blocks",
    )(*arrays)


def shift(value, axes, step):
    count = lax.axis_size(axes)
    pairs = [(i, i + step) for i in range(count) if 0 <= i + step < count]
    return lax.ppermute(value, axes, pairs)


def per_device(
    signal,
    kernel_front,
    mixing_front,
    offset_front,
    kernel_back,
    mixing_back,
    offset_back,
    upstream,
):
    s_low, s_high = shift(signal, TICK, 1), shift(signal, TICK, -1)
    strip_down = jnp.concatenate([signal[:, WIRES - 4 :], upstream[:, WIRES - 4 :]], axis=1)
    strip_up = jnp.concatenate([signal[:, :4], upstream[:, :4]], axis=1)
    h_up, h_down = shift(strip_down, WIRE, 1), shift(strip_up, WIRE, -1)
    pack = lambda part: jnp.concatenate([part[:, : WIRES // 2], part[:, WIRES // 2 :]], axis=2)
    u_low = shift(pack(upstream[:, :, 64:]), TICK, 1)
    u_high = shift(pack(upstream[:, :, :64]), TICK, -1)
    corner = jnp.stack([h_up, h_down])
    c_low, c_high = shift(corner, TICK, 1), shift(corner, TICK, -1)
    place = jnp.stack([lax.axis_index(TICK), lax.axis_index(WIRE)]).astype(jnp.int32)
    response, signal_grad, sums = local(
        place,
        *(signal, s_low, s_high, upstream, u_low, u_high, h_up, h_down, c_low, c_high),
        kernel_front.reshape(CHANNELS, 27),
        kernel_back.reshape(CHANNELS, 27),
        jnp.stack([mixing_front.T, mixing_back.T, mixing_back, mixing_front]),
        jnp.stack([offset_front, offset_back]),
    )
    for group in REDUCTION_ORDER:
        sums = lax.psum(sums, group)
    factor = 1.0 / math.sqrt(WIRES * lax.axis_size(WIRE) * TICKS * lax.axis_size(TICK))
    rows = (sums * factor).reshape(12, CHANNELS, STEP).transpose(0, 2, 1).reshape(96, CHANNELS)
    taps_of = lambda first: rows[first : first + 27].T.reshape(CHANNELS, 3, 9)
    return (
        response,
        signal_grad,
        taps_of(32),
        rows[80:96],
        rows[59],
        taps_of(0),
        rows[64:80],
        rows[27],
    )


def solution(mesh):
    fine = Mesh(mesh.devices.reshape(8, 4, 2, 2, 4), TICK + WIRE)
    block = P(None, WIRE, TICK)
    in_specs = (block, P(), P(), P(), P(), P(), P(), block)
    out_specs = (block, block, P(), P(), P(), P(), P(), P())
    return jax.shard_map(
        per_device, mesh=fine, in_specs=in_specs, out_specs=out_specs, check_vma=False
    )
```

time: 216 us -> 144 us (0.67)
  the two profiles are of different devices: /device:TPU:27 before, /device:TPU:2 now
where the time goes in v2:
time: 144 us; the launch traced here: 143 us
  blocking collectives  67.4 us (47%)
  Pallas kernels  38.6 us (27%)
  starting transfers between devices  27.2 us (19%)
  local copies, waits for them, and re-layouts  7.73 us (5%)
    psum x4, blocking collectives, per_device(): sums = lax.psum(sums, group)  67.4 us
    pallas_call x1, Pallas kernels, local(): pl.pallas_call(body, out_shape=(field, field, jax.ShapeDtypeStruct((12, T...  38.6 us
    ppermute x8, starting transfers between devices, shift(): return lax.ppermute(value, axes, pairs)  27.2 us
    unnamed x20, local copies, waits for them, and re-layouts  3.32 us
  transfers between devices with their start and end apart: 8, of which 0 were waited for; matrix products, arithmetic and copies ran while one was open for 3% of the time, Pallas kernels for 0%

profile of v2, /device:TPU:2, one launch (start us, length us, event | category | flops | bytes accessed | tf_op | source)
XLA Modules:
  0.0 143.0 jit_solution(2550448699696289475)
XLA Ops:
  0.6 0.0 copy-start
  0.6 1.4 collective-permute-start.1
  2.1 3.1 %collective-permute-start = (f32[16,64,128]{2,1,0:T(8,128)}, f32[16,64,128]{2,1,0:T(8,128)S(1)}, u32[]{:S(2)}, u32[]{:S(2)}) collective-permute-start(f32[16,64,128]{2,1,0:T(8,128)} %s_own.1), channel_id=1, source_target_pairs={{0,8},{8,16},{16,24},{24,32},{32,40},{40,48},{48,56},{56,64},{64,7... | collective-permute-start | bytes 1572872 | tf_op jit(solution)/shard_map/ppermute | solution.py:334
  5.2 0.9 fusion
  6.0 0.9 fusion.1
  7.0 3.4 %collective-permute-start.4 = (f32[16,8,128]{2,1,0:T(8,128)S(1)}, f32[16,8,128]{2,1,0:T(8,128)S(1)}, u32[]{:S(2)}, u32[]{:S(2)}) collective-permute-start(f32[16,8,128]{2,1,0:T(8,128)S(1)} %pad_maximum_fusion.3), channel_id=1, source_target_pairs={{0,1},{1,2},{2,3},{3,4},{4,5},{5,6},{6,7},{8,9},{9,10},{10,11},{11... | collective-permute-start | bytes 196616 | tf_op jit(solution)/shard_map/ppermute | solution.py:334
  10.4 5.7 %collective-permute-start.5 = (f32[16,8,128]{2,1,0:T(8,128)S(1)}, f32[16,8,128]{2,1,0:T(8,128)S(1)}, u32[]{:S(2)}, u32[]{:S(2)}) collective-permute-start(f32[16,8,128]{2,1,0:T(8,128)S(1)} %pad_maximum_fusion.4), channel_id=1, source_target_pairs={{1,0},{2,1},{3,2},{4,3},{5,4},{6,5},{7,6},{9,8},{10,9},{11,10},{12... | collective-permute-start | bytes 196616 | tf_op jit(solution)/shard_map/ppermute | solution.py:334
  16.1 0.2 fusion.2
  16.3 0.1 pad_maximum_fusion
  16.5 1.9 %collective-permute-start.2 = (f32[16,32,128]{2,1,0:T(8,128)S(1)}, f32[16,32,128]{2,1,0:T(8,128)S(1)}, u32[]{:S(2)}, u32[]{:S(2)}) collective-permute-start(f32[16,32,128]{2,1,0:T(8,128)S(1)} %pad_maximum_fusion), channel_id=1, source_target_pairs={{0,8},{8,16},{16,24},{24,32},{32,40},{40,48},{48,56},{56,64},{64,7... | collective-permute-start | bytes 786440 | tf_op jit(solution)/shard_map/ppermute | solution.py:334
  18.4 0.0 collective-permute-done.4.h_up
  18.4 0.0 collective-permute-done.5.h_down
  18.4 1.3 collective-permute-start.7
  19.7 0.0 copy-start.1
  19.7 0.8 pad_maximum_fusion.1
  20.6 1.3 collective-permute-start.3
  21.8 0.0 copy-start.6
  21.9 0.0 copy-start.7
  21.9 0.6 copy-done.6
  22.5 0.0 copy-done.7
  22.5 0.0 copy-start.2
  22.5 0.0 collective-permute-done.7.c_high
  22.6 9.2 %collective-permute-start.6 = (f32[2,16,8,128]{3,2,1,0:T(8,128)S(1)}, f32[2,16,8,128]{3,2,1,0:T(8,128)S(1)}, u32[]{:S(2)}, u32[]{:S(2)}) collective-permute-start(f32[2,16,8,128]{3,2,1,0:T(8,128)S(1)} %pad_maximum_fusion.2), channel_id=1, source_target_pairs={{0,8},{8,16},{16,24},{24,32},{32,40},{40,48},{48,56},{56,64},{64,7... | collective-permute-start | bytes 393224 | tf_op jit(solution)/shard_map/ppermute | solution.py:334
  31.8 0.1 pad_add_fusion.place
  31.8 0.1 copy.33
  31.9 0.6 copy-done.3
  32.5 0.1 copy.34
  32.6 0.1 copy.42
  32.7 0.1 reshape.42.taps_front
  32.8 0.6 copy-done.5
  33.4 0.1 copy.43
  33.5 0.1 reshape.43.taps_back
  33.6 0.0 collective-permute-done.6.c_low
  33.6 0.0 collective-permute-done.2.u_low
  33.6 0.0 collective-permute-done.3.u_high
  33.7 0.0 collective-permute-done.1.s_high
  33.7 38.6 %blocks.1 = (f32[16,64,128]{2,1,0:T(8,128)}, f32[16,64,128]{2,1,0:T(8,128)}, f32[12,128]{1,0:T(8,128)S(1)}) custom-call(s32[2]{0:T(128)S(1)} %pad_add_fusion.place, f32[16,64,128]{2,1,0:T(8,128)S(1)} %copy-done.1, f32[16,64,128]{2,1,0:T(8,128)S(1)} %collective-permute-done.s_low, f32[16,64,128]{2,1,0:T(8,128)S(1)} %collective-permute-done.1.s_high, ...), custom_call_target="tpu_custom_call" | custom-call | tf_op jit(solution)/shard_map/blocks/pallas_call | solution.py:304
  72.3 4.1 %psum.28 = f32[12,128]{1,0:T(8,128)S(1)} all-reduce(f32[12,128]{1,0:T(8,128)S(1)} %get-tuple-element.13), channel_id=1, replica_groups=mesh['y'=8,'z_hi'=4,'core'=2,'z_lo'=2,'x'=4] {'core'}, use_global_device_ids=true, to_apply=%region_0.0 | all-reduce | flops 1536 | bytes 12288 | tf_op jit(solution)/shard_map/psum | solution.py:366
  76.4 12.9 %psum.29 = f32[12,128]{1,0:T(8,128)S(1)} all-reduce(f32[12,128]{1,0:T(8,128)S(1)} %psum.28), channel_id=1, replica_groups=mesh['y'=8,'z_hi'=4,'core'=2,'z_lo'=2,'x'=4] {'x'}, use_global_device_ids=true, to_apply=%region_1.0 | all-reduce | flops 1536 | bytes 12288 | tf_op jit(solution)/shard_map/psum | solution.py:366
  89.4 23.8 %psum.30 = f32[12,128]{1,0:T(8,128)S(1)} all-reduce(f32[12,128]{1,0:T(8,128)S(1)} %psum.29), channel_id=1, replica_groups=mesh['y'=8,'z_hi'=4,'core'=2,'z_lo'=2,'x'=4] {'z_hi','z_lo'}, use_global_device_ids=true, to_apply=%region_2.0 | all-reduce | flops 1536 | bytes 12288 | tf_op jit(solution)/shard_map/psum | solution.py:366
  113.1 26.6 %psum.31 = f32[12,128]{1,0:T(8,128)S(1)} all-reduce(f32[12,128]{1,0:T(8,128)S(1)} %psum.30), channel_id=1, replica_groups=mesh['y'=8,'z_hi'=4,'core'=2,'z_lo'=2,'x'=4] {'y'}, use_global_device_ids=true, to_apply=%region_3.0 | all-reduce | flops 1536 | bytes 12288 | tf_op jit(solution)/shard_map/psum | solution.py:366
  139.7 0.1 reshape.38
  139.8 0.1 copy.37
  139.9 0.5 slice_bitcast_fusion.2
  140.4 0.7 copy.39
  141.1 0.6 copy.41
  141.7 0.7 copy.38
  142.4 0.6 copy.40
  (18 shorter events, 0.1 us)
Async XLA Ops:
  0.6 15.5 %copy-start = (f32[16,64,128]{2,1,0:T(8,128)S(1)}, f32[16,64,128]{2,1,0:T(8,128)}, u32[]{:S(2)}) copy-start(f32[16,64,128]{2,1,0:T(8,128)} %u_own.1) | copy-start | bytes 1572868
  0.6 33.0 %collective-permute-start.1 = (f32[16,64,128]{2,1,0:T(8,128)}, f32[16,64,128]{2,1,0:T(8,128)S(1)}, u32[]{:S(2)}, u32[]{:S(2)}) collective-permute-start(f32[16,64,128]{2,1,0:T(8,128)} %s_own.1), channel_id=1, source_target_pairs={{8,0},{16,8},{24,16},{32,24},{40,32},{48,40},{56,48},{64,56},{72,6... | collective-permute-start | bytes 1572872 | tf_op jit(solution)/shard_map/ppermute | solution.py:334
  2.1 31.6 %collective-permute-start = (f32[16,64,128]{2,1,0:T(8,128)}, f32[16,64,128]{2,1,0:T(8,128)S(1)}, u32[]{:S(2)}, u32[]{:S(2)}) collective-permute-start(f32[16,64,128]{2,1,0:T(8,128)} %s_own.1), channel_id=1, source_target_pairs={{0,8},{8,16},{16,24},{24,32},{32,40},{40,48},{48,56},{56,64},{64,7... | collective-permute-start | bytes 1572872 | tf_op jit(solution)/shard_map/ppermute | solution.py:334
  7.0 11.4 %collective-permute-start.4 = (f32[16,8,128]{2,1,0:T(8,128)S(1)}, f32[16,8,128]{2,1,0:T(8,128)S(1)}, u32[]{:S(2)}, u32[]{:S(2)}) collective-permute-start(f32[16,8,128]{2,1,0:T(8,128)S(1)} %pad_maximum_fusion.3), channel_id=1, source_target_pairs={{0,1},{1,2},{2,3},{3,4},{4,5},{5,6},{6,7},{8,9},{9,10},{10,11},{11... | collective-permute-start | bytes 196616 | tf_op jit(solution)/shard_map/ppermute | solution.py:334
  10.4 8.0 %collective-permute-start.5 = (f32[16,8,128]{2,1,0:T(8,128)S(1)}, f32[16,8,128]{2,1,0:T(8,128)S(1)}, u32[]{:S(2)}, u32[]{:S(2)}) collective-permute-start(f32[16,8,128]{2,1,0:T(8,128)S(1)} %pad_maximum_fusion.4), channel_id=1, source_target_pairs={{1,0},{2,1},{3,2},{4,3},{5,4},{6,5},{7,6},{9,8},{10,9},{11,10},{12... | collective-permute-start | bytes 196616 | tf_op jit(solution)/shard_map/ppermute | solution.py:334
  16.5 17.2 %collective-permute-start.2 = (f32[16,32,128]{2,1,0:T(8,128)S(1)}, f32[16,32,128]{2,1,0:T(8,128)S(1)}, u32[]{:S(2)}, u32[]{:S(2)}) collective-permute-start(f32[16,32,128]{2,1,0:T(8,128)S(1)} %pad_maximum_fusion), channel_id=1, source_target_pairs={{0,8},{8,16},{16,24},{24,32},{32,40},{40,48},{48,56},{56,64},{64,7... | collective-permute-start | bytes 786440 | tf_op jit(solution)/shard_map/ppermute | solution.py:334
  18.4 4.1 %collective-permute-start.7 = (f32[2,16,8,128]{3,2,1,0:T(8,128)S(1)}, f32[2,16,8,128]{3,2,1,0:T(8,128)S(1)}, u32[]{:S(2)}, u32[]{:S(2)}) collective-permute-start(f32[2,16,8,128]{3,2,1,0:T(8,128)S(1)} %pad_maximum_fusion.2), channel_id=1, source_target_pairs={{8,0},{16,8},{24,16},{32,24},{40,32},{48,40},{56,48},{64,56},{72,6... | collective-permute-start | bytes 393224 | tf_op jit(solution)/shard_map/ppermute | solution.py:334
  19.7 14.0 %copy-start.1 = (f32[16,64,128]{2,1,0:T(8,128)S(1)}, f32[16,64,128]{2,1,0:T(8,128)}, u32[]{:S(2)}) copy-start(f32[16,64,128]{2,1,0:T(8,128)} %s_own.1) | copy-start | bytes 1572868
  20.6 13.1 %collective-permute-start.3 = (f32[16,32,128]{2,1,0:T(8,128)}, f32[16,32,128]{2,1,0:T(8,128)S(1)}, u32[]{:S(2)}, u32[]{:S(2)}) collective-permute-start(f32[16,32,128]{2,1,0:T(8,128)} %pad_maximum_fusion.1), channel_id=1, source_target_pairs={{8,0},{16,8},{24,16},{32,24},{40,32},{48,40},{56,48},{64,56},{72,6... | collective-permute-start | bytes 786440 | tf_op jit(solution)/shard_map/ppermute | solution.py:334
  21.8 0.7 copy-start.6
  21.9 0.7 copy-start.7
  22.5 9.3 %copy-start.2 = (f32[16,16]{1,0:T(8,128)S(1)}, f32[16,16]{1,0:T(8,128)}, u32[]{:S(2)}) copy-start(f32[16,16]{1,0:T(8,128)} %param.10) | copy-start | bytes 3076
  22.6 11.1 %collective-permute-start.6 = (f32[2,16,8,128]{3,2,1,0:T(8,128)S(1)}, f32[2,16,8,128]{3,2,1,0:T(8,128)S(1)}, u32[]{:S(2)}, u32[]{:S(2)}) collective-permute-start(f32[2,16,8,128]{3,2,1,0:T(8,128)S(1)} %pad_maximum_fusion.2), channel_id=1, source_target_pairs={{0,8},{8,16},{16,24},{24,32},{32,40},{40,48},{48,56},{56,64},{64,7... | collective-permute-start | bytes 393224 | tf_op jit(solution)/shard_map/ppermute | solution.py:334
  31.8 0.7 copy-start.3
  31.8 0.8 copy-start.4
  32.7 0.7 copy-start.5

commit v3 on v2

v3 whole, which is shorter than its diff:
```python
import math

import jax
import jax.numpy as jnp
from jax import lax
from jax.experimental import pallas as pl
from jax.experimental.pallas import tpu as pltpu
from jax.sharding import Mesh, PartitionSpec as P

TICK = ("y", "z_hi", "core")
WIRE = ("z_lo", "x")
REDUCTION_ORDER = ("core", "x", ("z_hi", "z_lo"), "y")

CHANNELS, WIRES, TICKS = 16, 64, 128
STEP = 8
BLOCKS = TICKS // STEP
MARGIN = 4
OWN = 12
DEEP = 88
PACK = WIRES // 2
TILE = 128
F32, BF16 = jnp.float32, jnp.bfloat16


def lanes(shape):
    return lax.broadcasted_iota(jnp.int32, shape, len(shape) - 1)


def exchange(tiles):
    tiles = list(tiles)
    lane = lanes(tiles[0].shape)
    for bit in range(4):
        shift = STEP << bit
        upper = (lane & shift) != 0
        for low in range(16):
            if low >> bit & 1:
                continue
            high = low | 1 << bit
            a, b = tiles[low], tiles[high]
            tiles[low] = jnp.where(upper, pltpu.roll(b, shift, 1), a)
            tiles[high] = jnp.where(upper, b, pltpu.roll(a, TILE - shift, 1))
    return tiles


def tap(row, column, flip):
    return (2 - row) * 9 + 8 - column if flip else row * 9 + column


def convolve(source, target, kernel, flip, planes, first, last):
    def group(index, _):
        base = OWN + jnp.minimum(first + 8 * index, last - 8)
        weights = [[kernel[tap(i, j, flip)] for j in range(9)] for i in range(3)]
        sums = {}
        for at in range(planes + 8):
            rows = [source[at, pl.ds(base + i - 1, 8), :] for i in range(3)]
            for j in range(9):
                plane = at - j
                if not 0 <= plane < planes:
                    continue
                value = weights[0][j] * rows[0] + weights[1][j] * rows[1] + weights[2][j] * rows[2]
                sums[plane] = sums[plane] + value if j else value
                if j == 8:
                    target[plane, pl.ds(base, 8), :] = sums.pop(plane)
        return 0

    lax.fori_loop(0, (last - first + 7) // 8, group, 0)


def correlate(upward, ahead, source, start, lines, place):
    def group(index, carry):
        base = OWN + 8 * index
        sums = list(carry)
        ups = {}
        for at in range(BLOCKS + 8):
            if at < BLOCKS:
                ups[at] = upward[ahead + at, pl.ds(base, 8), :]
            rows = [source[start + at, pl.ds(base + i - 1, 8), :] for i in range(3)]
            for j in range(9):
                if 0 <= at - j < BLOCKS:
                    for i in range(3):
                        sums[9 * i + j] = sums[9 * i + j] + ups[at - j] * rows[i]
        return tuple(sums)

    zero = tuple(jnp.zeros((8, TILE), F32) for _ in range(27))
    sums = lax.fori_loop(0, WIRES // 8, group, zero)
    for k in range(27):
        lines[place + k : place + k + 1, :] = jnp.sum(sums[k], axis=0, keepdims=True)


def split(value):
    high = value.astype(BF16)
    return high, (value - high.astype(F32)).astype(BF16)


def mix(value, matrix):
    both = jnp.dot(jnp.concatenate(split(value), axis=1), matrix, preferred_element_type=F32)
    return both[:, :TILE] + both[:, TILE:]


def outer(left, right):
    lh, ll = split(left)
    rh, rl = split(right)
    return lax.dot_general(
        jnp.concatenate([lh, lh, ll], axis=0),
        jnp.concatenate([rh, rl, rh], axis=0),
        (((0,), (0,)), ((), ())),
        preferred_element_type=F32,
    )


def exact(left, right, contract):
    return lax.dot_general(
        left,
        right,
        (contract, ((), ())),
        precision=lax.Precision.HIGHEST,
        preferred_element_type=F32,
    )


PLANES = dict(
    sig=48, ups=32, fields_f=40, act=40, slope=40, fields_b=32, grads_b=32, u_back=32, result=32,
    grads_f=24, u_front=24, back_out=16,
)


def load(source, row):
    return exchange([source[c, pl.ds(row, 8), :] for c in range(CHANNELS)])


class Stages:
    def __init__(self, held, halves, biases, place):
        self.__dict__.update(held)
        self.halves, self.biases, self.place = halves, biases, place

    def front(self, at, count, wire, wires, margin):
        rows = pl.ds(OWN + wire, wires)
        value = self.fields_f[pl.ds(at, count), rows, :].reshape(count * wires, TILE)
        value = mix(value, self.halves[0]) + self.biases[0:1, :]
        order = lax.broadcasted_iota(jnp.int32, (count, wires, TILE), 0)
        tick_at, wire_at = self.place[0], self.place[1]
        plane = at + order
        inside = jnp.logical_and(
            jnp.logical_or(plane >= 12, tick_at > 0), jnp.logical_or(plane < 28, tick_at < 63)
        )
        if margin:
            line = wire + lax.broadcasted_iota(jnp.int32, (count, wires, TILE), 1)
            inside = jnp.logical_and(
                inside,
                jnp.logical_and(
                    jnp.logical_or(line >= 0, wire_at > 0),
                    jnp.logical_or(line < WIRES, wire_at < 7),
                ),
            )
        sigmoid = 1.0 / (1.0 + jnp.exp(-value))
        act = (value * sigmoid).reshape(count, wires, TILE)
        slope = (sigmoid * (1.0 + value * (1.0 - sigmoid))).reshape(count, wires, TILE)
        self.act[pl.ds(at, count), rows, :] = jnp.where(inside, act, 0.0)
        self.slope[pl.ds(at, count), rows, :] = jnp.where(inside, slope, 0.0)

    def back(self, at, count, wire, wires):
        rows = pl.ds(OWN + wire, wires)
        here = lambda planes: planes[pl.ds(at, count), rows, :].reshape(count * wires, TILE)
        value = mix(here(self.fields_b), self.halves[1]) + self.biases[1:2, :]
        sigmoid = 1.0 / (1.0 + jnp.exp(-value))
        grad = here(self.ups) * (sigmoid * (1.0 + value * (1.0 - sigmoid)))
        under = mix(grad, self.halves[2])
        for planes, field in (
            (self.result, value * sigmoid), (self.grads_b, grad), (self.u_back, under)
        ):
            planes[pl.ds(at, count), rows, :] = field.reshape(count, wires, TILE)

    def under_front(self, fields, at, count, wire, wires):
        rows = pl.ds(OWN + wire, wires)
        grad = fields[pl.ds(at, count), rows, :] * self.slope[pl.ds(at + 8, count), rows, :]
        under = mix(grad.reshape(count * wires, TILE), self.halves[3])
        self.grads_f[pl.ds(at, count), rows, :] = grad
        self.u_front[pl.ds(at, count), rows, :] = under.reshape(count, wires, TILE)


def loop(count, step, unroll):
    def one(index, _):
        step(index)
        return 0

    lax.fori_loop(0, count, one, 0, unroll=unroll)


def inner(place, s_own, u_own, low, high, taps_front, taps_back, mixings, offsets, *rest):
    held = dict(zip(PLANES, rest))
    kernel_front, kernel_back, halves, biases, fields_d = rest[len(PLANES) :]

    spread = (lanes((CHANNELS, TILE)) // STEP) == lax.broadcasted_iota(
        jnp.int32, (CHANNELS, TILE), 0
    )
    spread = jnp.where(spread, 1.0, 0.0)
    for kernel, raw in ((kernel_front, taps_front), (kernel_back, taps_back)):
        wide = exact(raw[...], spread, ((0,), (0,)))
        for k in range(27):
            kernel[k] = jnp.broadcast_to(wide[k : k + 1, :], (8, TILE))
    biases[...] = exact(offsets[...], spread, ((1,), (0,)))
    same = (lanes((TILE, TILE)) % STEP) == (
        lax.broadcasted_iota(jnp.int32, (TILE, TILE), 0) % STEP
    )
    for k in range(4):
        wide = exact(exact(spread, mixings[k], ((0,), (0,))), spread, ((1,), (0,)))
        upper, lower = split(jnp.where(same, wide, 0.0))
        halves[k, 0:TILE, 0:TILE] = upper
        halves[k, 0:TILE, TILE:] = lower
        halves[k, TILE:, 0:TILE] = upper
        halves[k, TILE:, TILE:] = jnp.zeros((TILE, TILE), BF16)

    sig, ups = held["sig"], held["ups"]

    def fill(group):
        row = pl.multiple_of(8 * group, 8)
        for source, target, start in (
            (low, sig, 0),
            (s_own, sig, BLOCKS),
            (high, sig, 2 * BLOCKS),
            (u_own, ups, BLOCKS // 2),
        ):
            for a, tile in enumerate(load(source, row)):
                target[start + a, pl.ds(OWN + row, 8), :] = tile

    loop(WIRES // 8, fill, 1)

    def fill_packed(group):
        row = pl.multiple_of(8 * group, 8)
        for source, start in ((low, 0), (high, BLOCKS // 2 + BLOCKS)):
            for a, tile in enumerate(load(source, WIRES + row)):
                second, plane = divmod(a, BLOCKS // 2)
                ups[start + plane, pl.ds(OWN + row + second * PACK, 8), :] = tile

    loop(PACK // 8, fill_packed, 1)

    do = Stages(held, halves, biases, place)
    convolve(sig, do.fields_f, kernel_front, False, 40, 1, 63)
    loop(20, lambda k: do.front(2 * k, 2, 0, WIRES, False), 10)
    convolve(do.act, do.fields_b, kernel_back, False, 32, 2, 62)
    loop(16, lambda k: do.back(2 * k, 2, 0, WIRES), 8)
    convolve(do.u_back, fields_d, kernel_back, True, 24, 3, 61)
    loop(12, lambda k: do.under_front(fields_d, 2 * k, 2, 0, WIRES), 6)
    convolve(do.u_front, do.back_out, kernel_front, True, 16, 4, 60)


def border(place, h_up, h_down, *rest):
    many = len(PLANES) + 4
    response, signal_grad, sums = rest[many : many + 3]
    held = dict(zip(PLANES, rest[many + 3 :]))
    kernel_front, kernel_back, halves, biases = rest[len(PLANES) : many]
    fields_d, lines = rest[many + 3 + len(PLANES) :]
    do = Stages(held, halves, biases, place)
    sig, ups = do.sig, do.ups

    for second, base, strip in ((1, OWN - MARGIN, h_up), (0, OWN + WIRES, h_down)):
        pairs = [load(strip, 8 * k) for k in range(3)]
        for a in range(BLOCKS):
            sig[a, base : base + MARGIN, :] = pairs[0][a][:MARGIN]
            sig[BLOCKS + a, base : base + MARGIN, :] = pairs[0][a][MARGIN:]
            sig[2 * BLOCKS + a, base : base + MARGIN, :] = pairs[1][a][:MARGIN]
            ups[BLOCKS // 2 + a, base : base + MARGIN, :] = pairs[1][a][MARGIN:]
            plane = a - second * (BLOCKS // 2)
            if 0 <= plane < BLOCKS // 2:
                ups[plane, base : base + MARGIN, :] = pairs[2][a][:MARGIN]
                ups[BLOCKS // 2 + BLOCKS + plane, base : base + MARGIN, :] = pairs[2][a][MARGIN:]

    for start in (-3, 59):
        convolve(sig, do.fields_f, kernel_front, False, 40, start, start + 8)
    for start in (-3, 59):
        do.front(0, 40, start, 8, True)
    for start in (-2, 58):
        convolve(do.act, do.fields_b, kernel_back, False, 32, start, start + 8)
    for start in (-2, 58):
        do.back(0, 32, start, 8)
    for start in (-1, 57):
        convolve(do.u_back, fields_d, kernel_back, True, 24, start, start + 8)
    for start in (-1, 57):
        do.under_front(fields_d, 0, 24, start, 8)
    for start in (0, 56):
        convolve(do.u_front, do.back_out, kernel_front, True, 16, start, start + 8)

    lines[...] = jnp.zeros_like(lines)
    same = (lanes((TILE, TILE)) % STEP) == (
        lax.broadcasted_iota(jnp.int32, (TILE, TILE), 0) % STEP
    )

    def give(group):
        row = pl.multiple_of(8 * group, 8)
        for source, start, target in ((do.result, 8, response), (do.back_out, 0, signal_grad)):
            tiles = [source[start + a, pl.ds(OWN + row, 8), :] for a in range(BLOCKS)]
            for c, tile in enumerate(exchange(tiles)):
                target[c, pl.ds(row, 8), :] = tile

    loop(WIRES // 8, give, 1)

    def tally(grads, ahead, fields, start, square_at, line_at):
        own = pl.ds(OWN, WIRES)

        def some(pair, carry):
            square, line = carry
            grad = grads[pl.ds(ahead + 2 * pair, 2), own, :].reshape(2 * WIRES, TILE)
            field = fields[pl.ds(start + 2 * pair, 2), own, :].reshape(2 * WIRES, TILE)
            line = line + jnp.sum(grad.reshape(2 * WIRES // 8, 8, TILE), axis=0)
            return square + outer(grad, field), line

        square, line = lax.fori_loop(
            0,
            BLOCKS // 2,
            some,
            (jnp.zeros((TILE, TILE), F32), jnp.zeros((8, TILE), F32)),
            unroll=8,
        )
        square = jnp.where(same, square, 0.0).reshape(CHANNELS, STEP, TILE)
        lines[square_at : square_at + CHANNELS, :] = jnp.sum(square, axis=1)
        lines[line_at : line_at + 1, :] = jnp.sum(line, axis=0, keepdims=True)

    tally(do.grads_b, 8, do.fields_b, 8, 64, 27)
    tally(do.grads_f, 4, do.fields_f, 12, 80, 59)
    correlate(do.u_back, 8, do.act, 8, lines, 0)
    correlate(do.u_front, 4, sig, 12, lines, 32)

    found = lines[...]
    for step in (1, 2, 4):
        found = found + pltpu.roll(found, TILE - step, 1)
    row = lax.broadcasted_iota(jnp.int32, (8, TILE), 0)
    for k in range(12):
        turned = pltpu.roll(found[8 * k : 8 * k + 8], 0, 1, stride=1, stride_axis=0)
        sums[k : k + 1, :] = jnp.sum(
            jnp.where(lanes((8, TILE)) % STEP == row, turned, 0.0), axis=0, keepdims=True
        )


VMEM = pl.BlockSpec(memory_space=pltpu.VMEM)
SMEM = pl.BlockSpec(memory_space=pltpu.SMEM)
SIZES = dict(compiler_params=pltpu.CompilerParams(vmem_limit_bytes=24 * 1024 * 1024))
HELD = [jax.ShapeDtypeStruct((count, DEEP, TILE), F32) for count in PLANES.values()]


def call_inner(*arrays):
    tables = [
        jax.ShapeDtypeStruct((27, 8, TILE), F32),
        jax.ShapeDtypeStruct((27, 8, TILE), F32),
        jax.ShapeDtypeStruct((4, 2 * TILE, 2 * TILE), BF16),
        jax.ShapeDtypeStruct((2, TILE), F32),
    ]
    return pl.pallas_call(
        inner,
        out_shape=HELD + tables,
        in_specs=[SMEM] + [VMEM] * (len(arrays) - 1),
        out_specs=[VMEM] * (len(HELD) + 4),
        scratch_shapes=[pltpu.VMEM((24, DEEP, TILE), F32)],
        name="inner",
        **SIZES,
    )(*arrays)


def call_border(*arrays):
    field = jax.ShapeDtypeStruct((CHANNELS, WIRES, TICKS), F32)
    return pl.pallas_call(
        border,
        out_shape=[field, field, jax.ShapeDtypeStruct((12, TILE), F32)] + HELD,
        in_specs=[SMEM] + [VMEM] * (len(arrays) - 1),
        out_specs=[VMEM] * (3 + len(HELD)),
        scratch_shapes=[
            pltpu.VMEM((24, DEEP, TILE), F32),
            pltpu.VMEM((96, TILE), F32),
        ],
        input_output_aliases={3 + k: 3 + k for k in range(len(HELD))},
        name="border",
        **SIZES,
    )(*arrays)[:3]


def shift(value, axes, step):
    count = lax.axis_size(axes)
    pairs = [(i, i + step) for i in range(count) if 0 <= i + step < count]
    return lax.ppermute(value, axes, pairs)


def per_device(
    signal,
    kernel_front,
    mixing_front,
    offset_front,
    kernel_back,
    mixing_back,
    offset_back,
    upstream,
):
    pack = lambda part: jnp.concatenate([part[:, :PACK], part[:, PACK:]], axis=2)
    join = lambda *parts: jnp.concatenate(parts, axis=1)
    low = shift(join(signal, pack(upstream[:, :, 64:])), TICK, 1)
    high = shift(join(signal, pack(upstream[:, :, :64])), TICK, -1)

    def strip(first, packed):
        rows = slice(first, first + MARGIN)
        halves = slice(packed, packed + MARGIN)
        return join(
            low[:, rows], signal[:, rows], high[:, rows], upstream[:, rows],
            low[:, halves], high[:, halves],
        )

    h_up = shift(strip(WIRES - MARGIN, WIRES + PACK - MARGIN), WIRE, 1)
    h_down = shift(strip(0, WIRES), WIRE, -1)
    place = jnp.stack([lax.axis_index(TICK), lax.axis_index(WIRE)]).astype(jnp.int32)
    held = call_inner(
        place,
        *(signal, upstream, low, high),
        kernel_front.reshape(CHANNELS, 27),
        kernel_back.reshape(CHANNELS, 27),
        jnp.stack([mixing_front.T, mixing_back.T, mixing_back, mixing_front]),
        jnp.stack([offset_front, offset_back]),
    )
    response, signal_grad, sums = call_border(place, h_up, h_down, *held)
    for group in REDUCTION_ORDER:
        sums = lax.psum(sums, group)
    factor = 1.0 / math.sqrt(WIRES * lax.axis_size(WIRE) * TICKS * lax.axis_size(TICK))
    rows = (sums * factor).reshape(12, CHANNELS, STEP).transpose(0, 2, 1).reshape(96, CHANNELS)
    taps_of = lambda first: rows[first : first + 27].T.reshape(CHANNELS, 3, 9)
    return (
        response,
        signal_grad,
        taps_of(32),
        rows[80:96],
        rows[59],
        taps_of(0),
        rows[64:80],
        rows[27],
    )


def solution(mesh):
    fine = Mesh(mesh.devices.reshape(8, 4, 2, 2, 4), TICK + WIRE)
    block = P(None, WIRE, TICK)
    in_specs = (block, P(), P(), P(), P(), P(), P(), block)
    out_specs = (block, block, P(), P(), P(), P(), P(), P())
    return jax.shard_map(
        per_device, mesh=fine, in_specs=in_specs, out_specs=out_specs, check_vma=False
    )
```

time: 144 us -> 122 us (0.85)
  starting transfers between devices: 27.2 us -> 13.5 us
  Pallas kernels: 38.6 us -> 25.6 us
  blocking collectives: 67.4 us -> 73.5 us
  local copies, waits for them, and re-layouts: 7.73 us -> 5.6 us
    ppermute x8 -> x4, starting transfers between devices: 27.2 us -> 13.5 us  [shift(): return lax.ppermute(value, axes, pairs)]
    pallas_call x1 -> x2, Pallas kernels: 38.6 us -> 25.6 us  [the longest x1 16.1 us: call_inner(): pl.pallas_call(inner, out_shape=HELD + tables, in_specs=[SMEM] + [VMEM] *...]
    psum x4, blocking collectives: 67.4 us -> 73.5 us  [per_device(): sums = lax.psum(sums, group)]
    unnamed x20, local copies, waits for them, and re-layouts: 3.32 us -> 1.42 us
  transfers between devices with their start and end apart: 8 -> 4, of which waited for: 0 -> 1; matrix products, arithmetic and copies ran while one was open for 3% -> 1% of each run, Pallas kernels for 0% -> 13%
where the time goes in v3:
time: 122 us
  blocking collectives  73.5 us (60%)
  Pallas kernels  25.6 us (21%)
  starting transfers between devices  13.5 us (11%)
  local copies, waits for them, and re-layouts  5.6 us (5%)
  other arithmetic  1.52 us (1%)
  waiting for transfers between devices  1.41 us (1%)
    psum x4, blocking collectives, per_device(): sums = lax.psum(sums, group)  73.5 us
    pallas_call x1, Pallas kernels, call_inner(): pl.pallas_call(inner, out_shape=HELD + tables, in_specs=[SMEM] + [VMEM] *...  16.1 us
    ppermute x4, starting transfers between devices, shift(): return lax.ppermute(value, axes, pairs)  13.5 us
    pallas_call x1, Pallas kernels, call_border(): pl.pallas_call(border, out_shape=[field, field, jax.ShapeDtypeStruct((12,...  9.46 us
  transfers between devices with their start and end apart: 4, of which 1 were waited for; matrix products, arithmetic and copies ran while one was open for 1% of the time, Pallas kernels for 13%

profile of v3, /device:TPU:2, one launch (start us, length us, event | category | flops | bytes accessed | tf_op | source)
XLA Modules:
  0.0 122.0 jit_solution(15255156355501156249)
XLA Ops:
  0.6 0.0 copy-start.1
  0.6 1.5 %fusion.4 = (f32[16,32,64]{2,1,0:T(8,128)S(1)}, f32[16,32,64]{2,1,0:T(8,128)S(1)}, f32[16,32,64]{2,1,0:T(8,128)S(1)}, f32[16,32,64]{2,1,0:T(8,128)S(1)}) fusion(f32[16,64,128]{2,1,0:T(8,128)} %u_own.1), kind=kLoop, calls=%fused_computation.14 | loop fusion | bytes 1048576 | tf_op jit(solution)/shard_map/slice | solution.py:391
  2.1 0.0 copy-done.1
  2.1 0.0 copy-start.2
  2.1 0.0 copy-start.3
  2.1 0.0 copy-start.4
  2.1 0.0 copy-start.5
  2.2 0.0 copy-start.6
  2.2 0.0 copy-start.7
  2.2 0.0 copy-start
  2.2 1.4 %pad_maximum_fusion = (f32[16,96,128]{2,1,0:T(8,128)}, f32[16,96,128]{2,1,0:T(8,128)}) fusion(f32[16,64,128]{2,1,0:T(8,128)S(1)} %copy-done.1, f32[16,32,64]{2,1,0:T(8,128)S(1)} %get-tuple-element.77, f32[16,32,64]{2,1,0:T(8,128)S(1)} %get-tuple-element.76, f32[16,32,64]{2,1,0:T(8,128)S(1)} %get-tuple-element.78, f32[16,32,64]{2,1,0:T(8,128)S(1)} %get-tuple-element.79), kind=kLoop, calls=%fused_computation | loop fusion | flops 786432 | bytes 2621440 | tf_op jit(solution)/shard_map/concatenate | solution.py:392
  3.6 1.3 %collective-permute-start.1 = (f32[16,96,128]{2,1,0:T(8,128)}, f32[16,96,128]{2,1,0:T(8,128)S(1)}, u32[]{:S(2)}, u32[]{:S(2)}) collective-permute-start(f32[16,96,128]{2,1,0:T(8,128)} %get-tuple-element.74), channel_id=1, source_target_pairs={{8,0},{16,8},{24,16},{32,24},{40,32},{48,40},{56,48},{64,56},{72,6... | collective-permute-start | bytes 2359304 | tf_op jit(solution)/shard_map/ppermute | solution.py:378
  4.9 3.1 %collective-permute-start = (f32[16,96,128]{2,1,0:T(8,128)}, f32[16,96,128]{2,1,0:T(8,128)S(1)}, u32[]{:S(2)}, u32[]{:S(2)}) collective-permute-start(f32[16,96,128]{2,1,0:T(8,128)} %get-tuple-element.75), channel_id=1, source_target_pairs={{0,8},{8,16},{16,24},{24,32},{32,40},{40,48},{48,56},{56,64},{64,7... | collective-permute-start | bytes 2359304 | tf_op jit(solution)/shard_map/ppermute | solution.py:378
  8.0 0.0 copy-done.2
  8.0 0.1 copy.45
  8.1 0.0 copy-done.3
  8.1 0.1 copy.46
  8.2 0.0 copy-done.4
  8.2 0.1 copy.54
  8.3 0.1 reshape.42.taps_front
  8.4 0.0 copy-done.5
  8.4 0.1 copy.55
  8.5 0.1 reshape.43.taps_back
  8.5 0.0 copy-done.6
  8.5 0.0 copy-done.7
  8.6 0.0 copy-done
  8.6 0.0 collective-permute-done.1.high
  8.7 1.4 %collective-permute-done.low = f32[16,96,128]{2,1,0:T(8,128)S(1)} collective-permute-done((f32[16,96,128]{2,1,0:T(8,128)}, f32[16,96,128]{2,1,0:T(8,128)S(1)}, u32[]{:S(2)}, u32[]{:S(2)}) %collective-permute-start) | collective-permute-done | bytes 786464 | tf_op jit(solution)/shard_map/ppermute | solution.py:378
  10.1 0.1 concatenate.22
  10.2 3.4 %collective-permute-start.2 = (f32[16,24,128]{2,1,0:T(8,128)S(1)}, f32[16,24,128]{2,1,0:T(8,128)S(1)}, u32[]{:S(2)}, u32[]{:S(2)}) collective-permute-start(f32[16,24,128]{2,1,0:T(8,128)S(1)} %concatenate.22), channel_id=1, source_target_pairs={{0,1},{1,2},{2,3},{3,4},{4,5},{5,6},{6,7},{8,9},{9,10},{10,11},{11... | collective-permute-start | bytes 589832 | tf_op jit(solution)/shard_map/ppermute | solution.py:378
  13.6 0.1 concatenate.23
  13.7 5.7 %collective-permute-start.3 = (f32[16,24,128]{2,1,0:T(8,128)S(1)}, f32[16,24,128]{2,1,0:T(8,128)S(1)}, u32[]{:S(2)}, u32[]{:S(2)}) collective-permute-start(f32[16,24,128]{2,1,0:T(8,128)S(1)} %concatenate.23), channel_id=1, source_target_pairs={{1,0},{2,1},{3,2},{4,3},{5,4},{6,5},{7,6},{9,8},{10,9},{11,10},{12... | collective-permute-start | bytes 589832 | tf_op jit(solution)/shard_map/ppermute | solution.py:378
  19.4 0.1 pad_add_fusion.place
  19.5 16.1 %inner.1 = (f32[48,88,128]{2,1,0:T(8,128)S(1)}, f32[32,88,128]{2,1,0:T(8,128)S(1)}, f32[40,88,128]{2,1,0:T(8,128)S(1)}, f32[40,88,128]{2,1,0:T(8,128)S(1)}, f32[...) custom-call(s32[2]{0:T(128)S(1)} %pad_add_fusion.place, ...), custom_call_target="tpu_custom_call" | custom-call | tf_op jit(solution)/shard_map/inner/pallas_call | solution.py:347
  35.6 0.0 collective-permute-done.2.h_up
  35.7 0.0 collective-permute-done.3.h_down
  35.7 9.5 %border.1 = (f32[16,64,128]{2,1,0:T(8,128)}, f32[16,64,128]{2,1,0:T(8,128)}, f32[12,128]{1,0:T(8,128)S(1)}, f32[48,88,128]{2,1,0:T(8,128)S(1)}, f32[32,88,128]{2...) custom-call(s32[2]{0:T(128)S(1)} %pad_add_fusion.place, ...), custom_call_target="tpu_custom_call", output_to_operand_aliasing={{3}: (3, {}), {4}: (4, {}), {5}: (5, {}), {6}: (6, {}), {7}... | custom-call | tf_op jit(solution)/shard_map/border/pallas_call | solution.py:360
  45.1 19.7 %psum.28 = f32[12,128]{1,0:T(8,128)S(1)} all-reduce(f32[12,128]{1,0:T(8,128)S(1)} %get-tuple-element.45), channel_id=1, replica_groups=mesh['y'=8,'z_hi'=4,'core'=2,'z_lo'=2,'x'=4] {'core'}, use_global_device_ids=true, to_apply=%region_0.0 | all-reduce | flops 1536 | bytes 12288 | tf_op jit(solution)/shard_map/psum | solution.py:417
  64.8 8.7 %psum.29 = f32[12,128]{1,0:T(8,128)S(1)} all-reduce(f32[12,128]{1,0:T(8,128)S(1)} %psum.28), channel_id=1, replica_groups=mesh['y'=8,'z_hi'=4,'core'=2,'z_lo'=2,'x'=4] {'x'}, use_global_device_ids=true, to_apply=%region_1.0 | all-reduce | flops 1536 | bytes 12288 | tf_op jit(solution)/shard_map/psum | solution.py:417
  73.5 23.4 %psum.30 = f32[12,128]{1,0:T(8,128)S(1)} all-reduce(f32[12,128]{1,0:T(8,128)S(1)} %psum.29), channel_id=1, replica_groups=mesh['y'=8,'z_hi'=4,'core'=2,'z_lo'=2,'x'=4] {'z_hi','z_lo'}, use_global_device_ids=true, to_apply=%region_2.0 | all-reduce | flops 1536 | bytes 12288 | tf_op jit(solution)/shard_map/psum | solution.py:417
  96.9 21.7 %psum.31 = f32[12,128]{1,0:T(8,128)S(1)} all-reduce(f32[12,128]{1,0:T(8,128)S(1)} %psum.30), channel_id=1, replica_groups=mesh['y'=8,'z_hi'=4,'core'=2,'z_lo'=2,'x'=4] {'y'}, use_global_device_ids=true, to_apply=%region_3.0 | all-reduce | flops 1536 | bytes 12288 | tf_op jit(solution)/shard_map/psum | solution.py:417
  118.7 0.1 reshape.38
  118.8 0.1 copy.49
  118.8 0.5 slice_bitcast_fusion.2
  119.4 0.7 copy.51
  120.1 0.6 copy.53
  120.7 0.7 copy.50
  121.3 0.6 copy.52
  (10 shorter events, 0.1 us)
Async XLA Ops:
  0.6 1.5 %copy-start.1 = (f32[16,64,128]{2,1,0:T(8,128)S(1)}, f32[16,64,128]{2,1,0:T(8,128)}, u32[]{:S(2)}) copy-start(f32[16,64,128]{2,1,0:T(8,128)} %s_own.1) | copy-start | bytes 1572868
  2.1 5.9 %copy-start.2 = (f32[16,16]{1,0:T(8,128)S(1)}, f32[16,16]{1,0:T(8,128)}, u32[]{:S(2)}) copy-start(f32[16,16]{1,0:T(8,128)} %param.10) | copy-start | bytes 3076
  2.1 6.0 %copy-start.3 = (f32[16,16]{1,0:T(8,128)S(1)}, f32[16,16]{1,0:T(8,128)}, u32[]{:S(2)}) copy-start(f32[16,16]{1,0:T(8,128)} %param.13) | copy-start | bytes 3076
  2.1 6.0 %copy-start.4 = (f32[16,3,9]{0,1,2:T(4,128)S(1)}, f32[16,3,9]{0,1,2:T(4,128)}, u32[]{:S(2)}) copy-start(f32[16,3,9]{0,1,2:T(4,128)} %param.9) | copy-start | bytes 5188
  2.1 6.2 %copy-start.5 = (f32[16,3,9]{0,1,2:T(4,128)S(1)}, f32[16,3,9]{0,1,2:T(4,128)}, u32[]{:S(2)}) copy-start(f32[16,3,9]{0,1,2:T(4,128)} %param.12) | copy-start | bytes 5188
  2.2 6.4 %copy-start.6 = (f32[16]{0:T(128)S(1)}, f32[16]{0:T(128)}, u32[]{:S(2)}) copy-start(f32[16]{0:T(128)} %param.14) | copy-start | bytes 196
  2.2 6.4 %copy-start.7 = (f32[16]{0:T(128)S(1)}, f32[16]{0:T(128)}, u32[]{:S(2)}) copy-start(f32[16]{0:T(128)} %param.11) | copy-start | bytes 196
  2.2 6.4 %copy-start = (f32[16,64,128]{2,1,0:T(8,128)S(1)}, f32[16,64,128]{2,1,0:T(8,128)}, u32[]{:S(2)}) copy-start(f32[16,64,128]{2,1,0:T(8,128)} %u_own.1) | copy-start | bytes 1572868
  3.6 5.0 %collective-permute-start.1 = (f32[16,96,128]{2,1,0:T(8,128)}, f32[16,96,128]{2,1,0:T(8,128)S(1)}, u32[]{:S(2)}, u32[]{:S(2)}) collective-permute-start(f32[16,96,128]{2,1,0:T(8,128)} %get-tuple-element.74), channel_id=1, source_target_pairs={{8,0},{16,8},{24,16},{32,24},{40,32},{48,40},{56,48},{64,56},{72,6... | collective-permute-start | bytes 2359304 | tf_op jit(solution)/shard_map/ppermute | solution.py:378
  4.9 5.1 %collective-permute-start = (f32[16,96,128]{2,1,0:T(8,128)}, f32[16,96,128]{2,1,0:T(8,128)S(1)}, u32[]{:S(2)}, u32[]{:S(2)}) collective-permute-start(f32[16,96,128]{2,1,0:T(8,128)} %get-tuple-element.75), channel_id=1, source_target_pairs={{0,8},{8,16},{16,24},{24,32},{32,40},{40,48},{48,56},{56,64},{64,7... | collective-permute-start | bytes 2359304 | tf_op jit(solution)/shard_map/ppermute | solution.py:378
  10.2 25.5 %collective-permute-start.2 = (f32[16,24,128]{2,1,0:T(8,128)S(1)}, f32[16,24,128]{2,1,0:T(8,128)S(1)}, u32[]{:S(2)}, u32[]{:S(2)}) collective-permute-start(f32[16,24,128]{2,1,0:T(8,128)S(1)} %concatenate.22), channel_id=1, source_target_pairs={{0,1},{1,2},{2,3},{3,4},{4,5},{5,6},{6,7},{8,9},{9,10},{10,11},{11... | collective-permute-start | bytes 589832 | tf_op jit(solution)/shard_map/ppermute | solution.py:378
  13.7 21.9 %collective-permute-start.3 = (f32[16,24,128]{2,1,0:T(8,128)S(1)}, f32[16,24,128]{2,1,0:T(8,128)S(1)}, u32[]{:S(2)}, u32[]{:S(2)}) collective-permute-start(f32[16,24,128]{2,1,0:T(8,128)S(1)} %concatenate.23), channel_id=1, source_target_pairs={{1,0},{2,1},{3,2},{4,3},{5,4},{6,5},{7,6},{9,8},{10,9},{11,10},{12... | collective-permute-start | bytes 589832 | tf_op jit(solution)/shard_map/ppermute | solution.py:378

commit v4 on v3

--- a/solution.py
+++ b/solution.py
@@ -1,3 +1,4 @@
+import functools
 import math
 
 import jax
@@ -26,20 +27,18 @@
     return lax.broadcasted_iota(jnp.int32, shape, len(shape) - 1)
 
 
+def turn(tile, shift):
+    return pltpu.roll(tile, shift, 1) if shift else tile
+
+
 def exchange(tiles):
-    tiles = list(tiles)
     lane = lanes(tiles[0].shape)
+    tiles = [turn(tile, STEP * c) for c, tile in enumerate(tiles)]
+    tiles = [tiles[-k % 16] for k in range(16)]
     for bit in range(4):
-        shift = STEP << bit
-        upper = (lane & shift) != 0
-        for low in range(16):
-            if low >> bit & 1:
-                continue
-            high = low | 1 << bit
-            a, b = tiles[low], tiles[high]
-            tiles[low] = jnp.where(upper, pltpu.roll(b, shift, 1), a)
-            tiles[high] = jnp.where(upper, b, pltpu.roll(a, TILE - shift, 1))
-    return tiles
+        upper = (lane & (STEP << bit)) != 0
+        tiles = [jnp.where(upper, tiles[k - (1 << bit)], tiles[k]) for k in range(16)]
+    return [turn(tile, (TILE - STEP * a) % TILE) for a, tile in enumerate(tiles)]
 
 
 def tap(row, column, flip):
@@ -186,10 +185,11 @@
     lax.fori_loop(0, count, one, 0, unroll=unroll)
 
 
-def inner(place, s_own, u_own, low, high, taps_front, taps_back, mixings, offsets, *rest):
-    held = dict(zip(PLANES, rest))
-    kernel_front, kernel_back, halves, biases, fields_d = rest[len(PLANES) :]
-
+def prepare(s_own, u_own, taps_front, taps_back, mixings, offsets, *rest):
+    sig, kernel_front, kernel_back, halves, biases, own_up, own_down = rest
+    for strip, rows in ((own_up, pl.ds(0, MARGIN)), (own_down, pl.ds(WIRES - MARGIN, MARGIN))):
+        strip[:, :MARGIN, :] = s_own[:, rows, :]
+        strip[:, MARGIN:, :] = u_own[:, rows, :]
     spread = (lanes((CHANNELS, TILE)) // STEP) == lax.broadcasted_iota(
         jnp.int32, (CHANNELS, TILE), 0
     )
@@ -210,15 +210,49 @@
         halves[k, TILE:, 0:TILE] = upper
         halves[k, TILE:, TILE:] = jnp.zeros((TILE, TILE), BF16)
 
+    def fill(group):
+        row = pl.multiple_of(8 * group, 8)
+        for a, tile in enumerate(load(s_own, row)):
+            sig[BLOCKS + a, pl.ds(OWN + row, 8), :] = tile
+
+    loop(WIRES // 8, fill, 1)
+
+
+def cut(low, high, own_up, own_down, *rest):
+    strip_up, strip_down = rest[5:7]
+    slabs, arrived = rest[-2:]
+    copies = []
+    for k, row in enumerate((0, WIRES, WIRES - 8, WIRES + PACK - 8)):
+        for side, source in enumerate((low, high)):
+            at = 2 * k + side
+            copies.append(
+                pltpu.make_async_copy(
+                    source.at[:, pl.ds(row, 8), :], slabs.at[at], arrived.at[at]
+                )
+            )
+    for copy in copies:
+        copy.start()
+    for copy in copies:
+        copy.wait()
+    for strip, own, first, rows in (
+        (strip_up, own_up, 0, slice(0, MARGIN)),
+        (strip_down, own_down, 4, slice(MARGIN, 8)),
+    ):
+        strip[:, 0:8, :] = own[...]
+        for k in range(4):
+            strip[:, 8 + MARGIN * k : 8 + MARGIN * (k + 1), :] = slabs[first + k, :, rows, :]
+
+
+def inner(place, low, high, u_own, *rest):
+    kernel_front, kernel_back, halves, biases = rest[1:5]
+    held = dict(zip(PLANES, rest[5:]))
+    fields_d = rest[-1]
     sig, ups = held["sig"], held["ups"]
 
     def fill(group):
         row = pl.multiple_of(8 * group, 8)
         for source, target, start in (
-            (low, sig, 0),
-            (s_own, sig, BLOCKS),
-            (high, sig, 2 * BLOCKS),
-            (u_own, ups, BLOCKS // 2),
+            (low, sig, 0), (high, sig, 2 * BLOCKS), (u_own, ups, BLOCKS // 2)
         ):
             for a, tile in enumerate(load(source, row)):
                 target[start + a, pl.ds(OWN + row, 8), :] = tile
@@ -256,10 +290,10 @@
     for second, base, strip in ((1, OWN - MARGIN, h_up), (0, OWN + WIRES, h_down)):
         pairs = [load(strip, 8 * k) for k in range(3)]
         for a in range(BLOCKS):
-            sig[a, base : base + MARGIN, :] = pairs[0][a][:MARGIN]
-            sig[BLOCKS + a, base : base + MARGIN, :] = pairs[0][a][MARGIN:]
-            sig[2 * BLOCKS + a, base : base + MARGIN, :] = pairs[1][a][:MARGIN]
-            ups[BLOCKS // 2 + a, base : base + MARGIN, :] = pairs[1][a][MARGIN:]
+            sig[BLOCKS + a, base : base + MARGIN, :] = pairs[0][a][:MARGIN]
+            ups[BLOCKS // 2 + a, base : base + MARGIN, :] = pairs[0][a][MARGIN:]
+            sig[a, base : base + MARGIN, :] = pairs[1][a][:MARGIN]
+            sig[2 * BLOCKS + a, base : base + MARGIN, :] = pairs[1][a][MARGIN:]
             plane = a - second * (BLOCKS // 2)
             if 0 <= plane < BLOCKS // 2:
                 ups[plane, base : base + MARGIN, :] = pairs[2][a][:MARGIN]
@@ -324,6 +358,7 @@
     for step in (1, 2, 4):
         found = found + pltpu.roll(found, TILE - step, 1)
     row = lax.broadcasted_iota(jnp.int32, (8, TILE), 0)
+    sums[12:16, :] = jnp.zeros((4, TILE), F32)
     for k in range(12):
         turned = pltpu.roll(found[8 * k : 8 * k + 8], 0, 1, stride=1, stride_axis=0)
         sums[k : k + 1, :] = jnp.sum(
@@ -333,25 +368,61 @@
 
 VMEM = pl.BlockSpec(memory_space=pltpu.VMEM)
 SMEM = pl.BlockSpec(memory_space=pltpu.SMEM)
-SIZES = dict(compiler_params=pltpu.CompilerParams(vmem_limit_bytes=24 * 1024 * 1024))
+
+
+def room(mebibytes):
+    return pltpu.CompilerParams(vmem_limit_bytes=mebibytes * 1024 * 1024)
+
+
 HELD = [jax.ShapeDtypeStruct((count, DEEP, TILE), F32) for count in PLANES.values()]
 
 
+TABLES = [
+    jax.ShapeDtypeStruct((27, 8, TILE), F32),
+    jax.ShapeDtypeStruct((27, 8, TILE), F32),
+    jax.ShapeDtypeStruct((4, 2 * TILE, 2 * TILE), BF16),
+    jax.ShapeDtypeStruct((2, TILE), F32),
+]
+
+
+def call_prepare(*arrays):
+    return pl.pallas_call(
+        prepare,
+        out_shape=HELD[:1] + TABLES + [jax.ShapeDtypeStruct((CHANNELS, 8, TICKS), F32)] * 2,
+        in_specs=[VMEM] * len(arrays),
+        out_specs=[VMEM] * 7,
+        name="prepare",
+        compiler_params=room(12),
+    )(*arrays)
+
+
+def call_cut(*arrays):
+    strip = jax.ShapeDtypeStruct((CHANNELS, 24, TICKS), F32)
+    return pl.pallas_call(
+        cut,
+        out_shape=[strip, strip] + HELD[:1] + TABLES,
+        in_specs=[pl.BlockSpec(memory_space=pl.ANY)] * 2 + [VMEM] * (len(arrays) - 2),
+        out_specs=[VMEM] * 7,
+        scratch_shapes=[
+            pltpu.VMEM((8, CHANNELS, 8, TICKS), F32),
+            pltpu.SemaphoreType.DMA((8,)),
+        ],
+        input_output_aliases={4 + k: 2 + k for k in range(5)},
+        name="cut",
+        compiler_params=room(16),
+    )(*arrays)
+
+
 def call_inner(*arrays):
-    tables = [
-        jax.ShapeDtypeStruct((27, 8, TILE), F32),
-        jax.ShapeDtypeStruct((27, 8, TILE), F32),
-        jax.ShapeDtypeStruct((4, 2 * TILE, 2 * TILE), BF16),
-        jax.ShapeDtypeStruct((2, TILE), F32),
-    ]
     return pl.pallas_call(
         inner,
-        out_shape=HELD + tables,
+        out_shape=HELD,
         in_specs=[SMEM] + [VMEM] * (len(arrays) - 1),
-        out_specs=[VMEM] * (len(HELD) + 4),
+        out_specs=[VMEM] * len(HELD),
         scratch_shapes=[pltpu.VMEM((24, DEEP, TILE), F32)],
+        input_output_aliases={4: 0},
         name="inner",
-        **SIZES,
+        compiler_params=room(24),
     )(*arrays)
 
 
@@ -359,7 +430,7 @@
     field = jax.ShapeDtypeStruct((CHANNELS, WIRES, TICKS), F32)
     return pl.pallas_call(
         border,
-        out_shape=[field, field, jax.ShapeDtypeStruct((12, TILE), F32)] + HELD,
+        out_shape=[field, field, jax.ShapeDtypeStruct((16, TILE), F32)] + HELD,
         in_specs=[SMEM] + [VMEM] * (len(arrays) - 1),
         out_specs=[VMEM] * (3 + len(HELD)),
         scratch_shapes=[
@@ -368,8 +439,39 @@
         ],
         input_output_aliases={3 + k: 3 + k for k in range(len(HELD))},
         name="border",
-        **SIZES,
+        compiler_params=room(24),
     )(*arrays)[:3]
+
+
+def unpack(sums, front_taps, front_square, front_line, back_taps, back_square, back_line, factor):
+    row = lax.broadcasted_iota(jnp.int32, (16, STEP, TILE), 1)
+    wide = jnp.broadcast_to(sums[...][:, None, :], (16, STEP, TILE))
+    wide = jnp.where(lanes(wide.shape) % STEP == row, wide, 0.0).reshape(16 * STEP, TILE)
+    channel = lax.broadcasted_iota(jnp.int32, (TILE, CHANNELS), 0) // STEP
+    pick = jnp.where(channel == lanes((TILE, CHANNELS)), 1.0, 0.0)
+    rows = exact(wide, pick, ((1,), (0,))) * factor
+    for taps, square, line, first, square_at, line_at in (
+        (front_taps, front_square, front_line, 32, 80, 59),
+        (back_taps, back_square, back_line, 0, 64, 27),
+    ):
+        for i in range(3):
+            for j in range(9):
+                at = first + 9 * i + j
+                taps[j, i : i + 1, :] = rows[at : at + 1, :]
+        square[...] = rows[square_at : square_at + CHANNELS, :]
+        line[...] = rows[line_at : line_at + 1, :]
+
+
+def call_unpack(sums, factor):
+    shapes = [(9, 3, CHANNELS), (CHANNELS, CHANNELS), (1, CHANNELS)] * 2
+    return pl.pallas_call(
+        functools.partial(unpack, factor=factor),
+        out_shape=[jax.ShapeDtypeStruct(shape, F32) for shape in shapes],
+        in_specs=[VMEM],
+        out_specs=[VMEM] * 6,
+        name="unpack",
+        compiler_params=room(6),
+    )(sums)
 
 
 def shift(value, axes, step):
@@ -393,40 +495,34 @@
     low = shift(join(signal, pack(upstream[:, :, 64:])), TICK, 1)
     high = shift(join(signal, pack(upstream[:, :, :64])), TICK, -1)
 
-    def strip(first, packed):
-        rows = slice(first, first + MARGIN)
-        halves = slice(packed, packed + MARGIN)
-        return join(
-            low[:, rows], signal[:, rows], high[:, rows], upstream[:, rows],
-            low[:, halves], high[:, halves],
-        )
-
-    h_up = shift(strip(WIRES - MARGIN, WIRES + PACK - MARGIN), WIRE, 1)
-    h_down = shift(strip(0, WIRES), WIRE, -1)
-    place = jnp.stack([lax.axis_index(TICK), lax.axis_index(WIRE)]).astype(jnp.int32)
-    held = call_inner(
-        place,
-        *(signal, upstream, low, high),
+    sig, *tables, own_up, own_down = call_prepare(
+        signal,
+        upstream,
         kernel_front.reshape(CHANNELS, 27),
         kernel_back.reshape(CHANNELS, 27),
         jnp.stack([mixing_front.T, mixing_back.T, mixing_back, mixing_front]),
         jnp.stack([offset_front, offset_back]),
     )
-    response, signal_grad, sums = call_border(place, h_up, h_down, *held)
+    strip_up, strip_down, sig, *tables = call_cut(low, high, own_up, own_down, sig, *tables)
+    h_up, h_down = shift(strip_down, WIRE, 1), shift(strip_up, WIRE, -1)
+    place = jnp.stack([lax.axis_index(TICK), lax.axis_index(WIRE)]).astype(jnp.int32)
+    held = call_inner(place, low, high, upstream, sig, *tables)
+    response, signal_grad, sums = call_border(place, h_up, h_down, *held, *tables)
     for group in REDUCTION_ORDER:
         sums = lax.psum(sums, group)
     factor = 1.0 / math.sqrt(WIRES * lax.axis_size(WIRE) * TICKS * lax.axis_size(TICK))
-    rows = (sums * factor).reshape(12, CHANNELS, STEP).transpose(0, 2, 1).reshape(96, CHANNELS)
-    taps_of = lambda first: rows[first : first + 27].T.reshape(CHANNELS, 3, 9)
+    front_taps, front_square, front_line, back_taps, back_square, back_line = call_unpack(
+        sums, factor
+    )
     return (
         response,
         signal_grad,
-        taps_of(32),
-        rows[80:96],
-        rows[59],
-        taps_of(0),
-        rows[64:80],
-        rows[27],
+        front_taps.transpose(2, 1, 0),
+        front_square,
+        front_line.reshape(CHANNELS),
+        back_taps.transpose(2, 1, 0),
+        back_square,
+        back_line.reshape(CHANNELS),
     )
 
 

time: 122 us -> 118 us (0.967)
  blocking collectives: 73.5 us -> 70.2 us
  local copies, waits for them, and re-layouts: 5.6 us -> 3.06 us
  starting transfers between devices: 13.5 us -> 15 us
  waiting for transfers between devices: 1.41 us -> 0.01 us
    psum x4, blocking collectives: 73.5 us -> 70.2 us  [per_device(): sums = lax.psum(sums, group)]
    ppermute x4, starting transfers between devices: 13.5 us -> 15 us  [shift(): return lax.ppermute(value, axes, pairs)]
    slice x6 -> x0, local copies, waits for them, and re-layouts: 1.41 us -> none  [the longest x2 0.67 us: per_device(): rows[64:80]]
    ppermute x4, waiting for transfers between devices: 1.41 us -> 0.01 us  [shift(): return lax.ppermute(value, axes, pairs)]
    pallas_call x2 -> x5, Pallas kernels: 25.6 us -> 26.8 us  [the longest x1 13.3 us: call_inner(): pl.pallas_call(inner, out_shape=HELD, in_specs=[SMEM] + [VMEM] * (len(arr...]
  transfers between devices with their start and end apart: 4 -> 4, of which waited for: 1 -> 0; matrix products, arithmetic and copies ran while one was open for 1% -> 1% of each run, Pallas kernels for 13% -> 13%
where the time goes in v4:
time: 118 us; the launch traced here: 117 us
  blocking collectives  70.2 us (59%)
  Pallas kernels  26.8 us (23%)
  starting transfers between devices  15 us (13%)
  local copies, waits for them, and re-layouts  3.06 us (3%)
  other arithmetic  1.51 us (1%)
    psum x4, blocking collectives, per_device(): sums = lax.psum(sums, group)  70.2 us
    ppermute x4, starting transfers between devices, shift(): return lax.ppermute(value, axes, pairs)  15 us
    pallas_call x1, Pallas kernels, call_inner(): pl.pallas_call(inner, out_shape=HELD, in_specs=[SMEM] + [VMEM] * (len(arr...  13.3 us
    pallas_call x1, Pallas kernels, call_border(): pl.pallas_call(border, out_shape=[field, field, jax.ShapeDtypeStruct((16,...  8.41 us
  transfers between devices with their start and end apart: 4, of which 0 were waited for; matrix products, arithmetic and copies ran while one was open for 1% of the time, Pallas kernels for 13%

profile of v4, /device:TPU:2, one launch (start us, length us, event | category | flops | bytes accessed | tf_op | source)
XLA Modules:
  0.0 117.4 jit_solution(10312033615282047484)
XLA Ops:
  0.6 0.0 copy-start.1
  0.6 1.5 %fusion = (f32[16,32,64]{2,1,0:T(8,128)S(1)}, f32[16,32,64]{2,1,0:T(8,128)S(1)}, f32[16,32,64]{2,1,0:T(8,128)S(1)}, f32[16,32,64]{2,1,0:T(8,128)S(1)}) fusion(f32[16,64,128]{2,1,0:T(8,128)} %u_own.3), kind=kLoop, calls=%fused_computation.5 | loop fusion | bytes 1048576 | tf_op jit(solution)/shard_map/slice | solution.py:493
  2.1 0.0 copy-done.1
  2.1 0.0 copy-start.3
  2.1 0.0 copy-start.4
  2.1 0.0 copy-start.5
  2.2 0.0 copy-start.6
  2.2 0.0 copy-start.7
  2.2 0.0 copy-start.8
  2.2 0.0 copy-start
  2.2 1.4 %pad_maximum_fusion = (f32[16,96,128]{2,1,0:T(8,128)}, f32[16,96,128]{2,1,0:T(8,128)}) fusion(f32[16,64,128]{2,1,0:T(8,128)S(1)} %copy-done.1, f32[16,32,64]{2,1,0:T(8,128)S(1)} %get-tuple-element.81, f32[16,32,64]{2,1,0:T(8,128)S(1)} %get-tuple-element.80, f32[16,32,64]{2,1,0:T(8,128)S(1)} %get-tuple-element.82, f32[16,32,64]{2,1,0:T(8,128)S(1)} %get-tuple-element.83), kind=kLoop, calls=%fused_computation | loop fusion | flops 786432 | bytes 2621440 | tf_op jit(solution)/shard_map/concatenate | solution.py:494
  3.6 1.3 %collective-permute-start.1 = (f32[16,96,128]{2,1,0:T(8,128)}, f32[16,96,128]{2,1,0:T(8,128)}, u32[]{:S(2)}, u32[]{:S(2)}) collective-permute-start(f32[16,96,128]{2,1,0:T(8,128)} %get-tuple-element.78), channel_id=1, source_target_pairs={{8,0},{16,8},{24,16},{32,24},{40,32},{48,40},{56,48},{64,56},{72,6... | collective-permute-start | bytes 2359304 | tf_op jit(solution)/shard_map/ppermute | solution.py:480
  4.9 3.9 %collective-permute-start = (f32[16,96,128]{2,1,0:T(8,128)}, f32[16,96,128]{2,1,0:T(8,128)}, u32[]{:S(2)}, u32[]{:S(2)}) collective-permute-start(f32[16,96,128]{2,1,0:T(8,128)} %get-tuple-element.79), channel_id=1, source_target_pairs={{0,8},{8,16},{16,24},{24,32},{32,40},{40,48},{48,56},{56,64},{64,7... | collective-permute-start | bytes 2359304 | tf_op jit(solution)/shard_map/ppermute | solution.py:480
  8.8 0.0 copy-done.3
  8.8 0.1 copy.40
  8.9 0.0 copy-done.4
  8.9 0.1 copy.41
  9.0 0.0 copy-done.5
  9.0 0.1 copy.44
  9.1 0.1 reshape.32.taps_front
  9.2 0.0 copy-done.6
  9.2 0.1 copy.45
  9.3 0.1 reshape.33.taps_back
  9.4 0.0 copy-done.7
  9.4 0.0 copy-done.8
  9.4 0.0 copy-done
  9.4 0.0 copy-start.2
  9.4 1.0 copy-done.2
  10.5 2.3 %prepare.1 = (f32[48,88,128]{2,1,0:T(8,128)S(1)}, f32[27,8,128]{2,1,0:T(8,128)S(1)}, f32[27,8,128]{2,1,0:T(8,128)S(1)}, bf16[4,256,256]{2,1,0:T(8,128)(2,1)S(1)}...) custom-call(f32[16,64,128]{2,1,0:T(8,128)S(1)} %copy-done.2, ...), custom_call_target="tpu_custom_call" | custom-call | tf_op jit(solution)/shard_map/prepare/pallas_call | solution.py:389
  12.8 0.0 collective-permute-done.1.high
  12.8 0.0 collective-permute-done.low
  12.8 1.9 %cut.1 = (f32[16,24,128]{2,1,0:T(8,128)}, f32[16,24,128]{2,1,0:T(8,128)}, f32[48,88,128]{2,1,0:T(8,128)S(1)}, f32[27,8,128]{2,1,0:T(8,128)S(1)}, f32[27,8,128]{2...) custom-call(f32[16,96,128]{2,1,0:T(8,128)} %collective-permute-done., ...), custom_call_target="tpu_custom_call", output_to_operand_aliasing={{2}: (4, {}), {3}: (5, {}), {4}: (6, {}), {5}: (7, {}), {6}... | custom-call | tf_op jit(solution)/shard_map/cut/pallas_call | solution.py:401
  14.8 3.4 %collective-permute-start.2 = (f32[16,24,128]{2,1,0:T(8,128)}, f32[16,24,128]{2,1,0:T(8,128)}, u32[]{:S(2)}, u32[]{:S(2)}) collective-permute-start(f32[16,24,128]{2,1,0:T(8,128)} %get-tuple-element.50), channel_id=1, source_target_pairs={{0,1},{1,2},{2,3},{3,4},{4,5},{5,6},{6,7},{8,9},{9,10},{10,11},{11... | collective-permute-start | bytes 589832 | tf_op jit(solution)/shard_map/ppermute | solution.py:480
  18.2 6.4 %collective-permute-start.3 = (f32[16,24,128]{2,1,0:T(8,128)}, f32[16,24,128]{2,1,0:T(8,128)}, u32[]{:S(2)}, u32[]{:S(2)}) collective-permute-start(f32[16,24,128]{2,1,0:T(8,128)} %get-tuple-element.51), channel_id=1, source_target_pairs={{1,0},{2,1},{3,2},{4,3},{5,4},{6,5},{7,6},{9,8},{10,9},{11,10},{12... | collective-permute-start | bytes 589832 | tf_op jit(solution)/shard_map/ppermute | solution.py:480
  24.6 0.1 pad_add_fusion.place
  24.7 13.3 %inner.1 = (f32[48,88,128]{2,1,0:T(8,128)S(1)}, f32[32,88,128]{2,1,0:T(8,128)S(1)}, f32[40,88,128]{2,1,0:T(8,128)S(1)}, f32[40,88,128]{2,1,0:T(8,128)S(1)}, f32[...) custom-call(s32[2]{0:T(128)S(1)} %pad_add_fusion.place, ...), custom_call_target="tpu_custom_call", output_to_operand_aliasing={{0}: (4, {})} | custom-call | tf_op jit(solution)/shard_map/inner/pallas_call | solution.py:417
  38.0 0.0 collective-permute-done.2.h_up
  38.0 0.0 collective-permute-done.3.h_down
  38.0 8.4 %border.1 = (f32[16,64,128]{2,1,0:T(8,128)}, f32[16,64,128]{2,1,0:T(8,128)}, f32[16,128]{1,0:T(8,128)S(1)}, f32[48,88,128]{2,1,0:T(8,128)S(1)}, f32[32,88,128]{2...) custom-call(s32[2]{0:T(128)S(1)} %pad_add_fusion.place, ...), custom_call_target="tpu_custom_call", output_to_operand_aliasing={{3}: (3, {}), {4}: (4, {}), {5}: (5, {}), {6}: (6, {}), {7}... | custom-call | tf_op jit(solution)/shard_map/border/pallas_call | solution.py:431
  46.4 17.0 %psum.28 = f32[16,128]{1,0:T(8,128)S(1)} all-reduce(f32[16,128]{1,0:T(8,128)S(1)} %get-tuple-element.71), channel_id=1, replica_groups=mesh['y'=8,'z_hi'=4,'core'=2,'z_lo'=2,'x'=4] {'core'}, use_global_device_ids=true, to_apply=%region_0.0 | all-reduce | flops 2048 | bytes 16384 | tf_op jit(solution)/shard_map/psum | solution.py:512
  63.4 8.0 %psum.29 = f32[16,128]{1,0:T(8,128)S(1)} all-reduce(f32[16,128]{1,0:T(8,128)S(1)} %psum.28), channel_id=1, replica_groups=mesh['y'=8,'z_hi'=4,'core'=2,'z_lo'=2,'x'=4] {'x'}, use_global_device_ids=true, to_apply=%region_1.0 | all-reduce | flops 2048 | bytes 16384 | tf_op jit(solution)/shard_map/psum | solution.py:512
  71.4 23.4 %psum.30 = f32[16,128]{1,0:T(8,128)S(1)} all-reduce(f32[16,128]{1,0:T(8,128)S(1)} %psum.29), channel_id=1, replica_groups=mesh['y'=8,'z_hi'=4,'core'=2,'z_lo'=2,'x'=4] {'z_hi','z_lo'}, use_global_device_ids=true, to_apply=%region_2.0 | all-reduce | flops 2048 | bytes 16384 | tf_op jit(solution)/shard_map/psum | solution.py:512
  94.8 21.8 %psum.31.sums = f32[16,128]{1,0:T(8,128)S(1)} all-reduce(f32[16,128]{1,0:T(8,128)S(1)} %psum.30), channel_id=1, replica_groups=mesh['y'=8,'z_hi'=4,'core'=2,'z_lo'=2,'x'=4] {'y'}, use_global_device_ids=true, to_apply=%region_3.0 | all-reduce | flops 2048 | bytes 16384 | tf_op jit(solution)/shard_map/psum | solution.py:512
  116.6 0.8 unpack.1
  (2 shorter events, 0.0 us)
Async XLA Ops:
  0.6 1.5 %copy-start.1 = (f32[16,64,128]{2,1,0:T(8,128)S(1)}, f32[16,64,128]{2,1,0:T(8,128)}, u32[]{:S(2)}) copy-start(f32[16,64,128]{2,1,0:T(8,128)} %s_own.1) | copy-start | bytes 1572868
  2.1 6.7 %copy-start.3 = (f32[16,16]{1,0:T(8,128)S(1)}, f32[16,16]{1,0:T(8,128)}, u32[]{:S(2)}) copy-start(f32[16,16]{1,0:T(8,128)} %param.10) | copy-start | bytes 3076
  2.1 6.8 %copy-start.4 = (f32[16,16]{1,0:T(8,128)S(1)}, f32[16,16]{1,0:T(8,128)}, u32[]{:S(2)}) copy-start(f32[16,16]{1,0:T(8,128)} %param.13) | copy-start | bytes 3076
  2.1 6.8 %copy-start.5 = (f32[16,3,9]{0,1,2:T(4,128)S(1)}, f32[16,3,9]{0,1,2:T(4,128)}, u32[]{:S(2)}) copy-start(f32[16,3,9]{0,1,2:T(4,128)} %param.9) | copy-start | bytes 5188
  2.2 7.0 %copy-start.6 = (f32[16,3,9]{0,1,2:T(4,128)S(1)}, f32[16,3,9]{0,1,2:T(4,128)}, u32[]{:S(2)}) copy-start(f32[16,3,9]{0,1,2:T(4,128)} %param.12) | copy-start | bytes 5188
  2.2 7.2 %copy-start.7 = (f32[16]{0:T(128)S(1)}, f32[16]{0:T(128)}, u32[]{:S(2)}) copy-start(f32[16]{0:T(128)} %param.14) | copy-start | bytes 196
  2.2 7.2 %copy-start.8 = (f32[16]{0:T(128)S(1)}, f32[16]{0:T(128)}, u32[]{:S(2)}) copy-start(f32[16]{0:T(128)} %param.11) | copy-start | bytes 196
  2.2 7.2 %copy-start = (f32[16,64,128]{2,1,0:T(8,128)S(1)}, f32[16,64,128]{2,1,0:T(8,128)}, u32[]{:S(2)}) copy-start(f32[16,64,128]{2,1,0:T(8,128)} %u_own.3) | copy-start | bytes 1572868
  3.6 9.2 %collective-permute-start.1 = (f32[16,96,128]{2,1,0:T(8,128)}, f32[16,96,128]{2,1,0:T(8,128)}, u32[]{:S(2)}, u32[]{:S(2)}) collective-permute-start(f32[16,96,128]{2,1,0:T(8,128)} %get-tuple-element.78), channel_id=1, source_target_pairs={{8,0},{16,8},{24,16},{32,24},{40,32},{48,40},{56,48},{64,56},{72,6... | collective-permute-start | bytes 2359304 | tf_op jit(solution)/shard_map/ppermute | solution.py:480
  4.9 7.9 %collective-permute-start = (f32[16,96,128]{2,1,0:T(8,128)}, f32[16,96,128]{2,1,0:T(8,128)}, u32[]{:S(2)}, u32[]{:S(2)}) collective-permute-start(f32[16,96,128]{2,1,0:T(8,128)} %get-tuple-element.79), channel_id=1, source_target_pairs={{0,8},{8,16},{16,24},{24,32},{32,40},{40,48},{48,56},{56,64},{64,7... | collective-permute-start | bytes 2359304 | tf_op jit(solution)/shard_map/ppermute | solution.py:480
  9.4 1.0 copy-start.2
  14.8 23.2 %collective-permute-start.2 = (f32[16,24,128]{2,1,0:T(8,128)}, f32[16,24,128]{2,1,0:T(8,128)}, u32[]{:S(2)}, u32[]{:S(2)}) collective-permute-start(f32[16,24,128]{2,1,0:T(8,128)} %get-tuple-element.50), channel_id=1, source_target_pairs={{0,1},{1,2},{2,3},{3,4},{4,5},{5,6},{6,7},{8,9},{9,10},{10,11},{11... | collective-permute-start | bytes 589832 | tf_op jit(solution)/shard_map/ppermute | solution.py:480
  18.2 19.8 %collective-permute-start.3 = (f32[16,24,128]{2,1,0:T(8,128)}, f32[16,24,128]{2,1,0:T(8,128)}, u32[]{:S(2)}, u32[]{:S(2)}) collective-permute-start(f32[16,24,128]{2,1,0:T(8,128)} %get-tuple-element.51), channel_id=1, source_target_pairs={{1,0},{2,1},{3,2},{4,3},{5,4},{6,5},{7,6},{9,8},{10,9},{11,10},{12... | collective-permute-start | bytes 589832 | tf_op jit(solution)/shard_map/ppermute | solution.py:480

commit v5 on v4

--- a/solution.py
+++ b/solution.py
@@ -121,6 +121,9 @@
     sig=48, ups=32, fields_f=40, act=40, slope=40, fields_b=32, grads_b=32, u_back=32, result=32,
     grads_f=24, u_front=24, back_out=16,
 )
+
+AHEAD = ("sig", "fields_f", "act", "slope")
+BEHIND = tuple(name for name in PLANES if name not in AHEAD)
 
 
 def load(source, row):
@@ -218,12 +221,15 @@
     loop(WIRES // 8, fill, 1)
 
 
-def cut(low, high, own_up, own_down, *rest):
-    strip_up, strip_down = rest[5:7]
+def cut(s_low, s_high, u_low, u_high, own_up, own_down, *rest):
+    strip_up, strip_down = rest[8:10]
     slabs, arrived = rest[-2:]
     copies = []
-    for k, row in enumerate((0, WIRES, WIRES - 8, WIRES + PACK - 8)):
-        for side, source in enumerate((low, high)):
+    signals, upstreams = (s_low, s_high), (u_low, u_high)
+    for k, (row, sources) in enumerate(
+        ((0, signals), (0, upstreams), (WIRES - 8, signals), (PACK - 8, upstreams))
+    ):
+        for side, source in enumerate(sources):
             at = 2 * k + side
             copies.append(
                 pltpu.make_async_copy(
@@ -243,34 +249,42 @@
             strip[:, 8 + MARGIN * k : 8 + MARGIN * (k + 1), :] = slabs[first + k, :, rows, :]
 
 
-def inner(place, low, high, u_own, *rest):
+def first(place, low, high, *rest):
     kernel_front, kernel_back, halves, biases = rest[1:5]
-    held = dict(zip(PLANES, rest[5:]))
-    fields_d = rest[-1]
-    sig, ups = held["sig"], held["ups"]
+    do = Stages(dict(zip(AHEAD, rest[5:])), halves, biases, place)
 
     def fill(group):
         row = pl.multiple_of(8 * group, 8)
-        for source, target, start in (
-            (low, sig, 0), (high, sig, 2 * BLOCKS), (u_own, ups, BLOCKS // 2)
-        ):
+        for source, start in ((low, 0), (high, 2 * BLOCKS)):
             for a, tile in enumerate(load(source, row)):
-                target[start + a, pl.ds(OWN + row, 8), :] = tile
+                do.sig[start + a, pl.ds(OWN + row, 8), :] = tile
 
     loop(WIRES // 8, fill, 1)
+    convolve(do.sig, do.fields_f, kernel_front, False, 40, 1, 63)
+    loop(20, lambda k: do.front(2 * k, 2, 0, WIRES, False), 10)
+
+
+def inner(place, low, high, u_own, act, slope, *rest):
+    kernel_front, kernel_back, halves, biases = rest[:4]
+    held = dict(zip(BEHIND, rest[4:]), act=act, slope=slope)
+    fields_d = rest[-1]
+    do = Stages(held, halves, biases, place)
+
+    def fill(group):
+        row = pl.multiple_of(8 * group, 8)
+        for a, tile in enumerate(load(u_own, row)):
+            do.ups[BLOCKS // 2 + a, pl.ds(OWN + row, 8), :] = tile
+
+    loop(WIRES // 8, fill, 2)
 
     def fill_packed(group):
         row = pl.multiple_of(8 * group, 8)
         for source, start in ((low, 0), (high, BLOCKS // 2 + BLOCKS)):
-            for a, tile in enumerate(load(source, WIRES + row)):
+            for a, tile in enumerate(load(source, row)):
                 second, plane = divmod(a, BLOCKS // 2)
-                ups[start + plane, pl.ds(OWN + row + second * PACK, 8), :] = tile
+                do.ups[start + plane, pl.ds(OWN + row + second * PACK, 8), :] = tile
 
     loop(PACK // 8, fill_packed, 1)
-
-    do = Stages(held, halves, biases, place)
-    convolve(sig, do.fields_f, kernel_front, False, 40, 1, 63)
-    loop(20, lambda k: do.front(2 * k, 2, 0, WIRES, False), 10)
     convolve(do.act, do.fields_b, kernel_back, False, 32, 2, 62)
     loop(16, lambda k: do.back(2 * k, 2, 0, WIRES), 8)
     convolve(do.u_back, fields_d, kernel_back, True, 24, 3, 61)
@@ -377,6 +391,8 @@
 HELD = [jax.ShapeDtypeStruct((count, DEEP, TILE), F32) for count in PLANES.values()]
 
 
+FRONT = [jax.ShapeDtypeStruct((PLANES[name], DEEP, TILE), F32) for name in AHEAD]
+BACK = [jax.ShapeDtypeStruct((PLANES[name], DEEP, TILE), F32) for name in BEHIND]
 TABLES = [
     jax.ShapeDtypeStruct((27, 8, TILE), F32),
     jax.ShapeDtypeStruct((27, 8, TILE), F32),
@@ -400,27 +416,38 @@
     strip = jax.ShapeDtypeStruct((CHANNELS, 24, TICKS), F32)
     return pl.pallas_call(
         cut,
-        out_shape=[strip, strip] + HELD[:1] + TABLES,
-        in_specs=[pl.BlockSpec(memory_space=pl.ANY)] * 2 + [VMEM] * (len(arrays) - 2),
-        out_specs=[VMEM] * 7,
+        out_shape=[strip, strip] + FRONT + TABLES,
+        in_specs=[pl.BlockSpec(memory_space=pl.ANY)] * 4 + [VMEM] * (len(arrays) - 4),
+        out_specs=[VMEM] * 10,
         scratch_shapes=[
             pltpu.VMEM((8, CHANNELS, 8, TICKS), F32),
             pltpu.SemaphoreType.DMA((8,)),
         ],
-        input_output_aliases={4 + k: 2 + k for k in range(5)},
+        input_output_aliases={6 + k: 2 + k for k in range(8)},
         name="cut",
-        compiler_params=room(16),
+        compiler_params=room(24),
+    )(*arrays)
+
+
+def call_first(*arrays):
+    return pl.pallas_call(
+        first,
+        out_shape=FRONT,
+        in_specs=[SMEM] + [VMEM] * (len(arrays) - 1),
+        out_specs=[VMEM] * 4,
+        input_output_aliases={3: 0},
+        name="first",
+        compiler_params=room(24),
     )(*arrays)
 
 
 def call_inner(*arrays):
     return pl.pallas_call(
         inner,
-        out_shape=HELD,
+        out_shape=BACK,
         in_specs=[SMEM] + [VMEM] * (len(arrays) - 1),
-        out_specs=[VMEM] * len(HELD),
+        out_specs=[VMEM] * len(BACK),
         scratch_shapes=[pltpu.VMEM((24, DEEP, TILE), F32)],
-        input_output_aliases={4: 0},
         name="inner",
         compiler_params=room(24),
     )(*arrays)
@@ -491,10 +518,10 @@
     upstream,
 ):
     pack = lambda part: jnp.concatenate([part[:, :PACK], part[:, PACK:]], axis=2)
-    join = lambda *parts: jnp.concatenate(parts, axis=1)
-    low = shift(join(signal, pack(upstream[:, :, 64:])), TICK, 1)
-    high = shift(join(signal, pack(upstream[:, :, :64])), TICK, -1)
-
+    place = jnp.stack([lax.axis_index(TICK), lax.axis_index(WIRE)]).astype(jnp.int32)
+    s_low, s_high = shift(signal, TICK, 1), shift(signal, TICK, -1)
+    u_low = shift(pack(upstream[:, :, 64:]), TICK, 1)
+    u_high = shift(pack(upstream[:, :, :64]), TICK, -1)
     sig, *tables, own_up, own_down = call_prepare(
         signal,
         upstream,
@@ -503,11 +530,17 @@
         jnp.stack([mixing_front.T, mixing_back.T, mixing_back, mixing_front]),
         jnp.stack([offset_front, offset_back]),
     )
-    strip_up, strip_down, sig, *tables = call_cut(low, high, own_up, own_down, sig, *tables)
+    ahead = call_first(place, s_low, s_high, sig, *tables)
+    strip_up, strip_down, *rest = call_cut(
+        s_low, s_high, u_low, u_high, own_up, own_down, *ahead, *tables
+    )
+    ahead, tables = rest[:4], rest[4:]
     h_up, h_down = shift(strip_down, WIRE, 1), shift(strip_up, WIRE, -1)
-    place = jnp.stack([lax.axis_index(TICK), lax.axis_index(WIRE)]).astype(jnp.int32)
-    held = call_inner(place, low, high, upstream, sig, *tables)
-    response, signal_grad, sums = call_border(place, h_up, h_down, *held, *tables)
+    behind = call_inner(place, u_low, u_high, upstream, *ahead[2:], *tables)
+    held = {**dict(zip(AHEAD, ahead)), **dict(zip(BEHIND, behind))}
+    response, signal_grad, sums = call_border(
+        place, h_up, h_down, *(held[name] for name in PLANES), *tables
+    )
     for group in REDUCTION_ORDER:
         sums = lax.psum(sums, group)
     factor = 1.0 / math.sqrt(WIRES * lax.axis_size(WIRE) * TICKS * lax.axis_size(TICK))

time: 118 us -> 105 us (0.89)
  blocking collectives: 70.2 us -> 58.5 us
  starting transfers between devices: 15 us -> 17.5 us
  Pallas kernels: 26.8 us -> 25.1 us
    psum x4, blocking collectives: 70.2 us -> 58.5 us  [per_device(): sums = lax.psum(sums, group)]
    ppermute x4 -> x6, starting transfers between devices: 15 us -> 17.5 us  [shift(): return lax.ppermute(value, axes, pairs)]
    pallas_call x2 -> x3, Pallas kernels: 15.3 us -> 13.9 us  [the longest x1 8.16 us: call_inner(): pl.pallas_call(inner, out_shape=BACK, in_specs=[SMEM] + [VMEM] * (len(arr...]
  transfers between devices with their start and end apart: 4 -> 6, of which waited for: 0 -> 0; matrix products, arithmetic and copies ran while one was open for 1% -> 2% of each run, Pallas kernels for 13% -> 15%
where the time goes in v5:
time: 105 us; the launch traced here: 104 us
  blocking collectives  58.5 us (56%)
  Pallas kernels  25.1 us (24%)
  starting transfers between devices  17.5 us (17%)
  local copies, waits for them, and re-layouts  1.96 us (2%)
    psum x4, blocking collectives, per_device(): sums = lax.psum(sums, group)  58.5 us
    ppermute x6, starting transfers between devices, shift(): return lax.ppermute(value, axes, pairs)  17.5 us
    pallas_call x1, Pallas kernels, call_inner(): pl.pallas_call(inner, out_shape=BACK, in_specs=[SMEM] + [VMEM] * (len(arr...  8.16 us
    pallas_call x1, Pallas kernels, call_border(): pl.pallas_call(border, out_shape=[field, field, jax.ShapeDtypeStruct((16,...  8.03 us
    pallas_call x1, Pallas kernels, call_first(): pl.pallas_call(first, out_shape=FRONT, in_specs=[SMEM] + [VMEM] * (len(ar...  5.48 us
    pallas_call x1, Pallas kernels, call_prepare(): pl.pallas_call(prepare, out_shape=HELD[:1] + TABLES + [jax.ShapeDtypeStru...  2.34 us
  transfers between devices with their start and end apart: 6, of which 0 were waited for; matrix products, arithmetic and copies ran while one was open for 2% of the time, Pallas kernels for 15%

profile of v5, /device:TPU:2, one launch (start us, length us, event | category | flops | bytes accessed | tf_op | source)
XLA Modules:
  0.0 104.3 jit_solution(7382765578562813157)
XLA Ops:
  0.6 0.0 copy-start.6
  0.6 0.0 copy-start.7
  0.7 0.0 copy-start.2
  0.7 0.0 copy-start.3
  0.7 0.0 copy-start.4
  0.7 0.0 copy-start.5
  0.7 1.9 %collective-permute-start = (f32[16,64,128]{2,1,0:T(8,128)}, f32[16,64,128]{2,1,0:T(8,128)S(1)}, u32[]{:S(2)}, u32[]{:S(2)}) collective-permute-start(f32[16,64,128]{2,1,0:T(8,128)} %s_own.1), channel_id=1, source_target_pairs={{0,8},{8,16},{16,24},{24,32},{32,40},{40,48},{48,56},{56,64},{64,7... | collective-permute-start | bytes 1572872 | tf_op jit(solution)/shard_map/ppermute | solution.py:507
  2.6 1.3 %collective-permute-start.1 = (f32[16,64,128]{2,1,0:T(8,128)}, f32[16,64,128]{2,1,0:T(8,128)S(1)}, u32[]{:S(2)}, u32[]{:S(2)}) collective-permute-start(f32[16,64,128]{2,1,0:T(8,128)} %s_own.1), channel_id=1, source_target_pairs={{8,0},{16,8},{24,16},{32,24},{40,32},{48,40},{56,48},{64,56},{72,6... | collective-permute-start | bytes 1572872 | tf_op jit(solution)/shard_map/ppermute | solution.py:507
  3.9 1.4 %fusion = (f32[16,32,64]{2,1,0:T(8,128)S(1)}, f32[16,32,64]{2,1,0:T(8,128)S(1)}, f32[16,32,64]{2,1,0:T(8,128)S(1)}, f32[16,32,64]{2,1,0:T(8,128)S(1)}) fusion(f32[16,64,128]{2,1,0:T(8,128)} %u_own.3), kind=kLoop, calls=%fused_computation.5 | loop fusion | bytes 1048576 | tf_op jit(solution)/shard_map/slice | solution.py:520
  5.3 0.0 copy-start
  5.3 0.0 copy-start.1
  5.3 0.1 pad_maximum_fusion
  5.5 7.1 %collective-permute-start.2 = (f32[16,32,128]{2,1,0:T(8,128)S(1)}, f32[16,32,128]{2,1,0:T(8,128)S(1)}, u32[]{:S(2)}, u32[]{:S(2)}) collective-permute-start(f32[16,32,128]{2,1,0:T(8,128)S(1)} %pad_maximum_fusion), channel_id=1, source_target_pairs={{0,8},{8,16},{16,24},{24,32},{32,40},{40,48},{48,56},{56,64},{64,7... | collective-permute-start | bytes 786440 | tf_op jit(solution)/shard_map/ppermute | solution.py:507
  12.6 0.1 pad_maximum_fusion.1
  12.7 1.3 %collective-permute-start.3 = (f32[16,32,128]{2,1,0:T(8,128)S(1)}, f32[16,32,128]{2,1,0:T(8,128)S(1)}, u32[]{:S(2)}, u32[]{:S(2)}) collective-permute-start(f32[16,32,128]{2,1,0:T(8,128)S(1)} %pad_maximum_fusion.1), channel_id=1, source_target_pairs={{8,0},{16,8},{24,16},{32,24},{40,32},{48,40},{56,48},{64,56},{72,6... | collective-permute-start | bytes 786440 | tf_op jit(solution)/shard_map/ppermute | solution.py:507
  14.0 0.0 copy-done.6
  14.1 0.0 copy-done.7
  14.1 0.0 copy-done.2
  14.1 0.1 copy.43
  14.2 0.0 copy-done.3
  14.2 0.1 copy.44
  14.2 0.0 copy-done.4
  14.2 0.1 copy.47
  14.4 0.1 reshape.32.taps_front
  14.4 0.0 copy-done.5
  14.4 0.1 copy.48
  14.5 0.1 reshape.33.taps_back
  14.6 0.0 copy-done
  14.6 0.0 copy-done.1
  14.7 2.3 %prepare.1 = (f32[48,88,128]{2,1,0:T(8,128)S(1)}, f32[27,8,128]{2,1,0:T(8,128)S(1)}, f32[27,8,128]{2,1,0:T(8,128)S(1)}, bf16[4,256,256]{2,1,0:T(8,128)(2,1)S(1)}...) custom-call(f32[16,64,128]{2,1,0:T(8,128)S(1)} %copy-done.1, ...), custom_call_target="tpu_custom_call" | custom-call | tf_op jit(solution)/shard_map/prepare/pallas_call | solution.py:405
  17.0 0.1 pad_add_fusion.place
  17.1 0.0 collective-permute-done.low.s_low
  17.1 0.0 collective-permute-done.1.high.s_high
  17.1 5.5 %first.1 = (f32[48,88,128]{2,1,0:T(8,128)S(1)}, f32[40,88,128]{2,1,0:T(8,128)S(1)}, f32[40,88,128]{2,1,0:T(8,128)S(1)}, f32[40,88,128]{2,1,0:T(8,128)S(1)}) custom-call(s32[2]{0:T(128)S(1)} %pad_add_fusion.place, f32[16,64,128]{2,1,0:T(8,128)S(1)} %collective-permute-done.low.s_low, ...), custom_call_target="tpu_custom_call", output_to_operand_aliasing={{0}: (3, {})} | custom-call | tf_op jit(solution)/shard_map/first/pallas_call | solution.py:433
  22.6 0.0 collective-permute-done.2.u_low.low
  22.6 0.0 collective-permute-done.3.u_high.high
  22.6 0.2 cut.1
  22.8 3.4 %collective-permute-start.4 = (f32[16,24,128]{2,1,0:T(8,128)S(1)}, f32[16,24,128]{2,1,0:T(8,128)S(1)}, u32[]{:S(2)}, u32[]{:S(2)}) collective-permute-start(f32[16,24,128]{2,1,0:T(8,128)S(1)} %get-tuple-element.57), channel_id=1, source_target_pairs={{0,1},{1,2},{2,3},{3,4},{4,5},{5,6},{6,7},{8,9},{9,10},{10,11},{11... | collective-permute-start | bytes 589832 | tf_op jit(solution)/shard_map/ppermute | solution.py:507
  26.3 2.4 %collective-permute-start.5 = (f32[16,24,128]{2,1,0:T(8,128)S(1)}, f32[16,24,128]{2,1,0:T(8,128)S(1)}, u32[]{:S(2)}, u32[]{:S(2)}) collective-permute-start(f32[16,24,128]{2,1,0:T(8,128)S(1)} %get-tuple-element.58), channel_id=1, source_target_pairs={{1,0},{2,1},{3,2},{4,3},{5,4},{6,5},{7,6},{9,8},{10,9},{11,10},{12... | collective-permute-start | bytes 589832 | tf_op jit(solution)/shard_map/ppermute | solution.py:507
  28.7 8.2 %inner.1 = (f32[32,88,128]{2,1,0:T(8,128)S(1)}, f32[32,88,128]{2,1,0:T(8,128)S(1)}, f32[32,88,128]{2,1,0:T(8,128)S(1)}, f32[32,88,128]{2,1,0:T(8,128)S(1)}, f32[...) custom-call(s32[2]{0:T(128)S(1)} %pad_add_fusion.place, ...), custom_call_target="tpu_custom_call" | custom-call | tf_op jit(solution)/shard_map/inner/pallas_call | solution.py:445
  36.9 0.0 collective-permute-done.4.h_up
  36.9 0.0 collective-permute-done.5.h_down
  36.9 8.0 %border.1 = (f32[16,64,128]{2,1,0:T(8,128)}, f32[16,64,128]{2,1,0:T(8,128)}, f32[16,128]{1,0:T(8,128)S(1)}, f32[48,88,128]{2,1,0:T(8,128)S(1)}, f32[32,88,128]{2...) custom-call(s32[2]{0:T(128)S(1)} %pad_add_fusion.place, ...), custom_call_target="tpu_custom_call", output_to_operand_aliasing={{3}: (3, {}), {4}: (4, {}), {5}: (5, {}), {6}: (6, {}), {7}... | custom-call | tf_op jit(solution)/shard_map/border/pallas_call | solution.py:458
  44.9 11.4 %psum.28 = f32[16,128]{1,0:T(8,128)S(1)} all-reduce(f32[16,128]{1,0:T(8,128)S(1)} %get-tuple-element.77), channel_id=1, replica_groups=mesh['y'=8,'z_hi'=4,'core'=2,'z_lo'=2,'x'=4] {'core'}, use_global_device_ids=true, to_apply=%region_0.0 | all-reduce | flops 2048 | bytes 16384 | tf_op jit(solution)/shard_map/psum | solution.py:545
  56.4 8.7 %psum.29 = f32[16,128]{1,0:T(8,128)S(1)} all-reduce(f32[16,128]{1,0:T(8,128)S(1)} %psum.28), channel_id=1, replica_groups=mesh['y'=8,'z_hi'=4,'core'=2,'z_lo'=2,'x'=4] {'x'}, use_global_device_ids=true, to_apply=%region_1.0 | all-reduce | flops 2048 | bytes 16384 | tf_op jit(solution)/shard_map/psum | solution.py:545
  65.1 19.5 %psum.30 = f32[16,128]{1,0:T(8,128)S(1)} all-reduce(f32[16,128]{1,0:T(8,128)S(1)} %psum.29), channel_id=1, replica_groups=mesh['y'=8,'z_hi'=4,'core'=2,'z_lo'=2,'x'=4] {'z_hi','z_lo'}, use_global_device_ids=true, to_apply=%region_2.0 | all-reduce | flops 2048 | bytes 16384 | tf_op jit(solution)/shard_map/psum | solution.py:545
  84.5 18.9 %psum.31.sums = f32[16,128]{1,0:T(8,128)S(1)} all-reduce(f32[16,128]{1,0:T(8,128)S(1)} %psum.30), channel_id=1, replica_groups=mesh['y'=8,'z_hi'=4,'core'=2,'z_lo'=2,'x'=4] {'y'}, use_global_device_ids=true, to_apply=%region_3.0 | all-reduce | flops 2048 | bytes 16384 | tf_op jit(solution)/shard_map/psum | solution.py:545
  103.5 0.8 unpack.1
  (2 shorter events, 0.0 us)
Async XLA Ops:
  0.6 13.4 %copy-start.6 = (f32[16]{0:T(128)S(1)}, f32[16]{0:T(128)}, u32[]{:S(2)}) copy-start(f32[16]{0:T(128)} %param.14) | copy-start | bytes 196
  0.6 13.4 %copy-start.7 = (f32[16]{0:T(128)S(1)}, f32[16]{0:T(128)}, u32[]{:S(2)}) copy-start(f32[16]{0:T(128)} %param.11) | copy-start | bytes 196
  0.7 13.4 %copy-start.2 = (f32[16,16]{1,0:T(8,128)S(1)}, f32[16,16]{1,0:T(8,128)}, u32[]{:S(2)}) copy-start(f32[16,16]{1,0:T(8,128)} %param.10) | copy-start | bytes 3076
  0.7 13.5 %copy-start.3 = (f32[16,16]{1,0:T(8,128)S(1)}, f32[16,16]{1,0:T(8,128)}, u32[]{:S(2)}) copy-start(f32[16,16]{1,0:T(8,128)} %param.13) | copy-start | bytes 3076
  0.7 13.6 %copy-start.4 = (f32[16,3,9]{0,1,2:T(4,128)S(1)}, f32[16,3,9]{0,1,2:T(4,128)}, u32[]{:S(2)}) copy-start(f32[16,3,9]{0,1,2:T(4,128)} %param.9) | copy-start | bytes 5188
  0.7 13.8 %copy-start.5 = (f32[16,3,9]{0,1,2:T(4,128)S(1)}, f32[16,3,9]{0,1,2:T(4,128)}, u32[]{:S(2)}) copy-start(f32[16,3,9]{0,1,2:T(4,128)} %param.12) | copy-start | bytes 5188
  0.7 16.4 %collective-permute-start = (f32[16,64,128]{2,1,0:T(8,128)}, f32[16,64,128]{2,1,0:T(8,128)S(1)}, u32[]{:S(2)}, u32[]{:S(2)}) collective-permute-start(f32[16,64,128]{2,1,0:T(8,128)} %s_own.1), channel_id=1, source_target_pairs={{0,8},{8,16},{16,24},{24,32},{32,40},{40,48},{48,56},{56,64},{64,7... | collective-permute-start | bytes 1572872 | tf_op jit(solution)/shard_map/ppermute | solution.py:507
  2.6 14.5 %collective-permute-start.1 = (f32[16,64,128]{2,1,0:T(8,128)}, f32[16,64,128]{2,1,0:T(8,128)S(1)}, u32[]{:S(2)}, u32[]{:S(2)}) collective-permute-start(f32[16,64,128]{2,1,0:T(8,128)} %s_own.1), channel_id=1, source_target_pairs={{8,0},{16,8},{24,16},{32,24},{40,32},{48,40},{56,48},{64,56},{72,6... | collective-permute-start | bytes 1572872 | tf_op jit(solution)/shard_map/ppermute | solution.py:507
  5.3 9.3 %copy-start = (f32[16,64,128]{2,1,0:T(8,128)S(1)}, f32[16,64,128]{2,1,0:T(8,128)}, u32[]{:S(2)}) copy-start(f32[16,64,128]{2,1,0:T(8,128)} %u_own.3) | copy-start | bytes 1572868
  5.3 9.3 %copy-start.1 = (f32[16,64,128]{2,1,0:T(8,128)S(1)}, f32[16,64,128]{2,1,0:T(8,128)}, u32[]{:S(2)}) copy-start(f32[16,64,128]{2,1,0:T(8,128)} %s_own.1) | copy-start | bytes 1572868
  5.5 17.1 %collective-permute-start.2 = (f32[16,32,128]{2,1,0:T(8,128)S(1)}, f32[16,32,128]{2,1,0:T(8,128)S(1)}, u32[]{:S(2)}, u32[]{:S(2)}) collective-permute-start(f32[16,32,128]{2,1,0:T(8,128)S(1)} %pad_maximum_fusion), channel_id=1, source_target_pairs={{0,8},{8,16},{16,24},{24,32},{32,40},{40,48},{48,56},{56,64},{64,7... | collective-permute-start | bytes 786440 | tf_op jit(solution)/shard_map/ppermute | solution.py:507
  12.7 9.8 %collective-permute-start.3 = (f32[16,32,128]{2,1,0:T(8,128)S(1)}, f32[16,32,128]{2,1,0:T(8,128)S(1)}, u32[]{:S(2)}, u32[]{:S(2)}) collective-permute-start(f32[16,32,128]{2,1,0:T(8,128)S(1)} %pad_maximum_fusion.1), channel_id=1, source_target_pairs={{8,0},{16,8},{24,16},{32,24},{40,32},{48,40},{56,48},{64,56},{72,6... | collective-permute-start | bytes 786440 | tf_op jit(solution)/shard_map/ppermute | solution.py:507
  22.8 14.0 %collective-permute-start.4 = (f32[16,24,128]{2,1,0:T(8,128)S(1)}, f32[16,24,128]{2,1,0:T(8,128)S(1)}, u32[]{:S(2)}, u32[]{:S(2)}) collective-permute-start(f32[16,24,128]{2,1,0:T(8,128)S(1)} %get-tuple-element.57), channel_id=1, source_target_pairs={{0,1},{1,2},{2,3},{3,4},{4,5},{5,6},{6,7},{8,9},{9,10},{10,11},{11... | collective-permute-start | bytes 589832 | tf_op jit(solution)/shard_map/ppermute | solution.py:507
  26.3 10.6 %collective-permute-start.5 = (f32[16,24,128]{2,1,0:T(8,128)S(1)}, f32[16,24,128]{2,1,0:T(8,128)S(1)}, u32[]{:S(2)}, u32[]{:S(2)}) collective-permute-start(f32[16,24,128]{2,1,0:T(8,128)S(1)} %get-tuple-element.58), channel_id=1, source_target_pairs={{1,0},{2,1},{3,2},{4,3},{5,4},{6,5},{7,6},{9,8},{10,9},{11,10},{12... | collective-permute-start | bytes 589832 | tf_op jit(solution)/shard_map/ppermute | solution.py:507

commit v6 on v5

--- a/solution.py
+++ b/solution.py
@@ -254,12 +254,12 @@
     do = Stages(dict(zip(AHEAD, rest[5:])), halves, biases, place)
 
     def fill(group):
-        row = pl.multiple_of(8 * group, 8)
-        for source, start in ((low, 0), (high, 2 * BLOCKS)):
-            for a, tile in enumerate(load(source, row)):
-                do.sig[start + a, pl.ds(OWN + row, 8), :] = tile
-
-    loop(WIRES // 8, fill, 1)
+        for row in (pl.multiple_of(16 * group, 8), pl.multiple_of(16 * group + 8, 8)):
+            for source, start in ((low, 0), (high, 2 * BLOCKS)):
+                for a, tile in enumerate(load(source, row)):
+                    do.sig[start + a, pl.ds(OWN + row, 8), :] = tile
+
+    loop(WIRES // 16, fill, 1)
     convolve(do.sig, do.fields_f, kernel_front, False, 40, 1, 63)
     loop(20, lambda k: do.front(2 * k, 2, 0, WIRES, False), 10)
 
@@ -271,20 +271,16 @@
     do = Stages(held, halves, biases, place)
 
     def fill(group):
-        row = pl.multiple_of(8 * group, 8)
-        for a, tile in enumerate(load(u_own, row)):
-            do.ups[BLOCKS // 2 + a, pl.ds(OWN + row, 8), :] = tile
-
-    loop(WIRES // 8, fill, 2)
-
-    def fill_packed(group):
+        for row in (pl.multiple_of(16 * group, 8), pl.multiple_of(16 * group + 8, 8)):
+            for a, tile in enumerate(load(u_own, row)):
+                do.ups[BLOCKS // 2 + a, pl.ds(OWN + row, 8), :] = tile
         row = pl.multiple_of(8 * group, 8)
         for source, start in ((low, 0), (high, BLOCKS // 2 + BLOCKS)):
             for a, tile in enumerate(load(source, row)):
                 second, plane = divmod(a, BLOCKS // 2)
                 do.ups[start + plane, pl.ds(OWN + row + second * PACK, 8), :] = tile
 
-    loop(PACK // 8, fill_packed, 1)
+    loop(PACK // 8, fill, 1)
     convolve(do.act, do.fields_b, kernel_back, False, 32, 2, 62)
     loop(16, lambda k: do.back(2 * k, 2, 0, WIRES), 8)
     convolve(do.u_back, fields_d, kernel_back, True, 24, 3, 61)

time: 105 us -> 104 us (level)
  no operation moved by 1% of the time
where the time goes in v6:
time: 104 us
  blocking collectives  58.5 us (56%)
  Pallas kernels  24.4 us (23%)
  starting transfers between devices  17.5 us (17%)
  local copies, waits for them, and re-layouts  1.96 us (2%)
    psum x4, blocking collectives, per_device(): sums = lax.psum(sums, group)  58.5 us
    ppermute x6, starting transfers between devices, shift(): return lax.ppermute(value, axes, pairs)  17.5 us
    pallas_call x1, Pallas kernels, call_border(): pl.pallas_call(border, out_shape=[field, field, jax.ShapeDtypeStruct((16,...  8.03 us
    pallas_call x1, Pallas kernels, call_inner(): pl.pallas_call(inner, out_shape=BACK, in_specs=[SMEM] + [VMEM] * (len(arr...  7.81 us
    pallas_call x1, Pallas kernels, call_first(): pl.pallas_call(first, out_shape=FRONT, in_specs=[SMEM] + [VMEM] * (len(ar...  5.12 us
    pallas_call x1, Pallas kernels, call_prepare(): pl.pallas_call(prepare, out_shape=HELD[:1] + TABLES + [jax.ShapeDtypeStru...  2.34 us
  transfers between devices with their start and end apart: 6, of which 0 were waited for; matrix products, arithmetic and copies ran while one was open for 2% of the time, Pallas kernels for 15%

profile of v6, /device:TPU:2, one launch (start us, length us, event | category | flops | bytes accessed | tf_op | source)
XLA Modules:
  0.0 103.6 jit_solution(16139691006580114991)
XLA Ops:
  0.6 0.0 copy-start.6
  0.6 0.0 copy-start.7
  0.7 0.0 copy-start.2
  0.7 0.0 copy-start.3
  0.7 0.0 copy-start.4
  0.7 0.0 copy-start.5
  0.7 1.9 %collective-permute-start = (f32[16,64,128]{2,1,0:T(8,128)}, f32[16,64,128]{2,1,0:T(8,128)S(1)}, u32[]{:S(2)}, u32[]{:S(2)}) collective-permute-start(f32[16,64,128]{2,1,0:T(8,128)} %s_own.1), channel_id=1, source_target_pairs={{0,8},{8,16},{16,24},{24,32},{32,40},{40,48},{48,56},{56,64},{64,7... | collective-permute-start | bytes 1572872 | tf_op jit(solution)/shard_map/ppermute | solution.py:503
  2.6 1.3 %collective-permute-start.1 = (f32[16,64,128]{2,1,0:T(8,128)}, f32[16,64,128]{2,1,0:T(8,128)S(1)}, u32[]{:S(2)}, u32[]{:S(2)}) collective-permute-start(f32[16,64,128]{2,1,0:T(8,128)} %s_own.1), channel_id=1, source_target_pairs={{8,0},{16,8},{24,16},{32,24},{40,32},{48,40},{56,48},{64,56},{72,6... | collective-permute-start | bytes 1572872 | tf_op jit(solution)/shard_map/ppermute | solution.py:503
  3.9 1.4 %fusion = (f32[16,32,64]{2,1,0:T(8,128)S(1)}, f32[16,32,64]{2,1,0:T(8,128)S(1)}, f32[16,32,64]{2,1,0:T(8,128)S(1)}, f32[16,32,64]{2,1,0:T(8,128)S(1)}) fusion(f32[16,64,128]{2,1,0:T(8,128)} %u_own.3), kind=kLoop, calls=%fused_computation.5 | loop fusion | bytes 1048576 | tf_op jit(solution)/shard_map/slice | solution.py:516
  5.3 0.0 copy-start
  5.3 0.0 copy-start.1
  5.3 0.1 pad_maximum_fusion
  5.5 7.1 %collective-permute-start.2 = (f32[16,32,128]{2,1,0:T(8,128)S(1)}, f32[16,32,128]{2,1,0:T(8,128)S(1)}, u32[]{:S(2)}, u32[]{:S(2)}) collective-permute-start(f32[16,32,128]{2,1,0:T(8,128)S(1)} %pad_maximum_fusion), channel_id=1, source_target_pairs={{0,8},{8,16},{16,24},{24,32},{32,40},{40,48},{48,56},{56,64},{64,7... | collective-permute-start | bytes 786440 | tf_op jit(solution)/shard_map/ppermute | solution.py:503
  12.6 0.1 pad_maximum_fusion.1
  12.7 1.3 %collective-permute-start.3 = (f32[16,32,128]{2,1,0:T(8,128)S(1)}, f32[16,32,128]{2,1,0:T(8,128)S(1)}, u32[]{:S(2)}, u32[]{:S(2)}) collective-permute-start(f32[16,32,128]{2,1,0:T(8,128)S(1)} %pad_maximum_fusion.1), channel_id=1, source_target_pairs={{8,0},{16,8},{24,16},{32,24},{40,32},{48,40},{56,48},{64,56},{72,6... | collective-permute-start | bytes 786440 | tf_op jit(solution)/shard_map/ppermute | solution.py:503
  14.0 0.0 copy-done.6
  14.1 0.0 copy-done.7
  14.1 0.0 copy-done.2
  14.1 0.1 copy.43
  14.2 0.0 copy-done.3
  14.2 0.1 copy.44
  14.2 0.0 copy-done.4
  14.2 0.1 copy.47
  14.4 0.1 reshape.32.taps_front
  14.4 0.0 copy-done.5
  14.4 0.1 copy.48
  14.5 0.1 reshape.33.taps_back
  14.6 0.0 copy-done
  14.6 0.0 copy-done.1
  14.7 2.3 %prepare.1 = (f32[48,88,128]{2,1,0:T(8,128)S(1)}, f32[27,8,128]{2,1,0:T(8,128)S(1)}, f32[27,8,128]{2,1,0:T(8,128)S(1)}, bf16[4,256,256]{2,1,0:T(8,128)(2,1)S(1)}...) custom-call(f32[16,64,128]{2,1,0:T(8,128)S(1)} %copy-done.1, ...), custom_call_target="tpu_custom_call" | custom-call | tf_op jit(solution)/shard_map/prepare/pallas_call | solution.py:401
  17.0 0.1 pad_add_fusion.place
  17.1 0.0 collective-permute-done.low.s_low
  17.1 0.0 collective-permute-done.1.high.s_high
  17.1 5.1 %first.1 = (f32[48,88,128]{2,1,0:T(8,128)S(1)}, f32[40,88,128]{2,1,0:T(8,128)S(1)}, f32[40,88,128]{2,1,0:T(8,128)S(1)}, f32[40,88,128]{2,1,0:T(8,128)S(1)}) custom-call(s32[2]{0:T(128)S(1)} %pad_add_fusion.place, f32[16,64,128]{2,1,0:T(8,128)S(1)} %collective-permute-done.low.s_low, ...), custom_call_target="tpu_custom_call", output_to_operand_aliasing={{0}: (3, {})} | custom-call | tf_op jit(solution)/shard_map/first/pallas_call | solution.py:429
  22.2 0.0 collective-permute-done.2.u_low.low
  22.2 0.0 collective-permute-done.3.u_high.high
  22.2 0.2 cut.1
  22.5 3.4 %collective-permute-start.4 = (f32[16,24,128]{2,1,0:T(8,128)S(1)}, f32[16,24,128]{2,1,0:T(8,128)S(1)}, u32[]{:S(2)}, u32[]{:S(2)}) collective-permute-start(f32[16,24,128]{2,1,0:T(8,128)S(1)} %get-tuple-element.57), channel_id=1, source_target_pairs={{0,1},{1,2},{2,3},{3,4},{4,5},{5,6},{6,7},{8,9},{9,10},{10,11},{11... | collective-permute-start | bytes 589832 | tf_op jit(solution)/shard_map/ppermute | solution.py:503
  25.9 2.4 %collective-permute-start.5 = (f32[16,24,128]{2,1,0:T(8,128)S(1)}, f32[16,24,128]{2,1,0:T(8,128)S(1)}, u32[]{:S(2)}, u32[]{:S(2)}) collective-permute-start(f32[16,24,128]{2,1,0:T(8,128)S(1)} %get-tuple-element.58), channel_id=1, source_target_pairs={{1,0},{2,1},{3,2},{4,3},{5,4},{6,5},{7,6},{9,8},{10,9},{11,10},{12... | collective-permute-start | bytes 589832 | tf_op jit(solution)/shard_map/ppermute | solution.py:503
  28.3 7.8 %inner.1 = (f32[32,88,128]{2,1,0:T(8,128)S(1)}, f32[32,88,128]{2,1,0:T(8,128)S(1)}, f32[32,88,128]{2,1,0:T(8,128)S(1)}, f32[32,88,128]{2,1,0:T(8,128)S(1)}, f32[...) custom-call(s32[2]{0:T(128)S(1)} %pad_add_fusion.place, ...), custom_call_target="tpu_custom_call" | custom-call | tf_op jit(solution)/shard_map/inner/pallas_call | solution.py:441
  36.2 0.0 collective-permute-done.4.h_up
  36.2 0.0 collective-permute-done.5.h_down
  36.2 8.0 %border.1 = (f32[16,64,128]{2,1,0:T(8,128)}, f32[16,64,128]{2,1,0:T(8,128)}, f32[16,128]{1,0:T(8,128)S(1)}, f32[48,88,128]{2,1,0:T(8,128)S(1)}, f32[32,88,128]{2...) custom-call(s32[2]{0:T(128)S(1)} %pad_add_fusion.place, ...), custom_call_target="tpu_custom_call", output_to_operand_aliasing={{3}: (3, {}), {4}: (4, {}), {5}: (5, {}), {6}: (6, {}), {7}... | custom-call | tf_op jit(solution)/shard_map/border/pallas_call | solution.py:454
  44.2 11.8 %psum.28 = f32[16,128]{1,0:T(8,128)S(1)} all-reduce(f32[16,128]{1,0:T(8,128)S(1)} %get-tuple-element.77), channel_id=1, replica_groups=mesh['y'=8,'z_hi'=4,'core'=2,'z_lo'=2,'x'=4] {'core'}, use_global_device_ids=true, to_apply=%region_0.0 | all-reduce | flops 2048 | bytes 16384 | tf_op jit(solution)/shard_map/psum | solution.py:541
  56.0 8.7 %psum.29 = f32[16,128]{1,0:T(8,128)S(1)} all-reduce(f32[16,128]{1,0:T(8,128)S(1)} %psum.28), channel_id=1, replica_groups=mesh['y'=8,'z_hi'=4,'core'=2,'z_lo'=2,'x'=4] {'x'}, use_global_device_ids=true, to_apply=%region_1.0 | all-reduce | flops 2048 | bytes 16384 | tf_op jit(solution)/shard_map/psum | solution.py:541
  64.7 19.4 %psum.30 = f32[16,128]{1,0:T(8,128)S(1)} all-reduce(f32[16,128]{1,0:T(8,128)S(1)} %psum.29), channel_id=1, replica_groups=mesh['y'=8,'z_hi'=4,'core'=2,'z_lo'=2,'x'=4] {'z_hi','z_lo'}, use_global_device_ids=true, to_apply=%region_2.0 | all-reduce | flops 2048 | bytes 16384 | tf_op jit(solution)/shard_map/psum | solution.py:541
  84.1 18.7 %psum.31.sums = f32[16,128]{1,0:T(8,128)S(1)} all-reduce(f32[16,128]{1,0:T(8,128)S(1)} %psum.30), channel_id=1, replica_groups=mesh['y'=8,'z_hi'=4,'core'=2,'z_lo'=2,'x'=4] {'y'}, use_global_device_ids=true, to_apply=%region_3.0 | all-reduce | flops 2048 | bytes 16384 | tf_op jit(solution)/shard_map/psum | solution.py:541
  102.8 0.8 unpack.1
  (2 shorter events, 0.0 us)
Async XLA Ops:
  0.6 13.4 %copy-start.6 = (f32[16]{0:T(128)S(1)}, f32[16]{0:T(128)}, u32[]{:S(2)}) copy-start(f32[16]{0:T(128)} %param.14) | copy-start | bytes 196
  0.6 13.4 %copy-start.7 = (f32[16]{0:T(128)S(1)}, f32[16]{0:T(128)}, u32[]{:S(2)}) copy-start(f32[16]{0:T(128)} %param.11) | copy-start | bytes 196
  0.7 13.4 %copy-start.2 = (f32[16,16]{1,0:T(8,128)S(1)}, f32[16,16]{1,0:T(8,128)}, u32[]{:S(2)}) copy-start(f32[16,16]{1,0:T(8,128)} %param.10) | copy-start | bytes 3076
  0.7 13.5 %copy-start.3 = (f32[16,16]{1,0:T(8,128)S(1)}, f32[16,16]{1,0:T(8,128)}, u32[]{:S(2)}) copy-start(f32[16,16]{1,0:T(8,128)} %param.13) | copy-start | bytes 3076
  0.7 13.6 %copy-start.4 = (f32[16,3,9]{0,1,2:T(4,128)S(1)}, f32[16,3,9]{0,1,2:T(4,128)}, u32[]{:S(2)}) copy-start(f32[16,3,9]{0,1,2:T(4,128)} %param.9) | copy-start | bytes 5188
  0.7 13.8 %copy-start.5 = (f32[16,3,9]{0,1,2:T(4,128)S(1)}, f32[16,3,9]{0,1,2:T(4,128)}, u32[]{:S(2)}) copy-start(f32[16,3,9]{0,1,2:T(4,128)} %param.12) | copy-start | bytes 5188
  0.7 16.4 %collective-permute-start = (f32[16,64,128]{2,1,0:T(8,128)}, f32[16,64,128]{2,1,0:T(8,128)S(1)}, u32[]{:S(2)}, u32[]{:S(2)}) collective-permute-start(f32[16,64,128]{2,1,0:T(8,128)} %s_own.1), channel_id=1, source_target_pairs={{0,8},{8,16},{16,24},{24,32},{32,40},{40,48},{48,56},{56,64},{64,7... | collective-permute-start | bytes 1572872 | tf_op jit(solution)/shard_map/ppermute | solution.py:503
  2.6 14.5 %collective-permute-start.1 = (f32[16,64,128]{2,1,0:T(8,128)}, f32[16,64,128]{2,1,0:T(8,128)S(1)}, u32[]{:S(2)}, u32[]{:S(2)}) collective-permute-start(f32[16,64,128]{2,1,0:T(8,128)} %s_own.1), channel_id=1, source_target_pairs={{8,0},{16,8},{24,16},{32,24},{40,32},{48,40},{56,48},{64,56},{72,6... | collective-permute-start | bytes 1572872 | tf_op jit(solution)/shard_map/ppermute | solution.py:503
  5.3 9.3 %copy-start = (f32[16,64,128]{2,1,0:T(8,128)S(1)}, f32[16,64,128]{2,1,0:T(8,128)}, u32[]{:S(2)}) copy-start(f32[16,64,128]{2,1,0:T(8,128)} %u_own.3) | copy-start | bytes 1572868
  5.3 9.3 %copy-start.1 = (f32[16,64,128]{2,1,0:T(8,128)S(1)}, f32[16,64,128]{2,1,0:T(8,128)}, u32[]{:S(2)}) copy-start(f32[16,64,128]{2,1,0:T(8,128)} %s_own.1) | copy-start | bytes 1572868
  5.5 16.7 %collective-permute-start.2 = (f32[16,32,128]{2,1,0:T(8,128)S(1)}, f32[16,32,128]{2,1,0:T(8,128)S(1)}, u32[]{:S(2)}, u32[]{:S(2)}) collective-permute-start(f32[16,32,128]{2,1,0:T(8,128)S(1)} %pad_maximum_fusion), channel_id=1, source_target_pairs={{0,8},{8,16},{16,24},{24,32},{32,40},{40,48},{48,56},{56,64},{64,7... | collective-permute-start | bytes 786440 | tf_op jit(solution)/shard_map/ppermute | solution.py:503
  12.7 9.5 %collective-permute-start.3 = (f32[16,32,128]{2,1,0:T(8,128)S(1)}, f32[16,32,128]{2,1,0:T(8,128)S(1)}, u32[]{:S(2)}, u32[]{:S(2)}) collective-permute-start(f32[16,32,128]{2,1,0:T(8,128)S(1)} %pad_maximum_fusion.1), channel_id=1, source_target_pairs={{8,0},{16,8},{24,16},{32,24},{40,32},{48,40},{56,48},{64,56},{72,6... | collective-permute-start | bytes 786440 | tf_op jit(solution)/shard_map/ppermute | solution.py:503
  22.5 13.7 %collective-permute-start.4 = (f32[16,24,128]{2,1,0:T(8,128)S(1)}, f32[16,24,128]{2,1,0:T(8,128)S(1)}, u32[]{:S(2)}, u32[]{:S(2)}) collective-permute-start(f32[16,24,128]{2,1,0:T(8,128)S(1)} %get-tuple-element.57), channel_id=1, source_target_pairs={{0,1},{1,2},{2,3},{3,4},{4,5},{5,6},{6,7},{8,9},{9,10},{10,11},{11... | collective-permute-start | bytes 589832 | tf_op jit(solution)/shard_map/ppermute | solution.py:503
  25.9 10.3 %collective-permute-start.5 = (f32[16,24,128]{2,1,0:T(8,128)S(1)}, f32[16,24,128]{2,1,0:T(8,128)S(1)}, u32[]{:S(2)}, u32[]{:S(2)}) collective-permute-start(f32[16,24,128]{2,1,0:T(8,128)S(1)} %get-tuple-element.58), channel_id=1, source_target_pairs={{1,0},{2,1},{3,2},{4,3},{5,4},{6,5},{7,6},{9,8},{10,9},{11,10},{12... | collective-permute-start | bytes 589832 | tf_op jit(solution)/shard_map/ppermute | solution.py:503
